TPU v7x, 256 devices: a whole 4x4x8 slice. The times are simulated.
256 devices in a mesh: ep: 64 (over y, z, core), dp: 4 (over x).
Axes of the slice: x: 4, y: 4, z: 8, core: 2. Of those that a mesh axis runs over, the one named last changes fastest.
Arguments:
- tokens: bfloat16 [8192, 2048], P(('ep', 'dp')), may hold values from -6 to 6
- cotangent: bfloat16 [8192, 2048], P(('ep', 'dp')), may hold values from -6 to 6
- expert_ids: int32 [8192, 8], P(('ep', 'dp')), may hold values from 0 to 63, as said below
- route_weights: bfloat16 [8192, 8], P(('ep', 'dp')), may hold values from 0.049804688 to 0.5
- w_gate: bfloat16 [64, 2048, 768], P('ep'), may hold values from -0.125 to 0.125
- w_up: bfloat16 [64, 2048, 768], P('ep'), may hold values from -0.125 to 0.125
- w_down: bfloat16 [64, 768, 2048], P('ep'), may hold values from -0.21875 to 0.21875
Outputs:
- grad_tokens: bfloat16 [8192, 2048], P(('ep', 'dp'))
- grad_route: bfloat16 [8192, 8], P(('ep', 'dp'))
- grad_gate: bfloat16 [64, 2048, 768], P('ep', 'dp')
- grad_up: bfloat16 [64, 2048, 768], P('ep', 'dp')
- grad_down: bfloat16 [64, 768, 2048], P('ep', None, 'dp')
Inputs may be any that keep to these rules, and one draw needn't show every extreme that they name: `expert_ids`: each token names 8 different experts. The tokens of one device name no expert more than 8 times; 4 experts, drawn from the seed, are named exactly 8 times by every device's tokens.
All inputs are finite; a program needn't handle non-finite values.
Results may differ from a plain program's by a relative error of at most 0.0095.
Values may be sent and summed in bfloat16 or wider, within the bound.
No kernel may reach another device: no remote copies, remote signals or barrier semaphores. Data moves between devices by JAX's collectives and lax.ppermute only.
A program may use at most 128 MiB of HBM per device.

v0:
```python
import functools

import jax
import jax.numpy as jnp
from jax import lax
from jax.experimental import pallas as pl
from jax.experimental.pallas import tpu as pltpu
from jax.sharding import PartitionSpec as P

bf16 = jnp.bfloat16
f32 = jnp.float32
i32 = jnp.int32

NY, NZ, NC = 4, 8, 2
CAP = 8
TOK = 32
TOPK = 8
D = 2048
FF = 768
META = 128
DA = D + META
HALF = NY * NZ * CAP
ROWS = 2 * HALF
FB = 256
NFB = FF // FB
DY = (0, -1, 1, 2)
DZ = (0, -1, 1, -2, 2, -3, 3, 4)
NDP = 4
PIECE = D // NDP // 2
VLIM = 60 * 1024 * 1024

contract_last = (((1,), (1,)), ((), ()))
contract_first = (((0,), (0,)), ((), ()))
nothing = (((1,), (0,)), ((), ()))


def dot(a, b, dims=nothing):
    return lax.dot_general(a, b, dims, preferred_element_type=f32)


def flat(y, z, c):
    return ((y % NY) * NZ + (z % NZ)) * NC + c


def shift(arr, dy=0, dz=0):
    pairs = [
        (flat(y, z, c), flat(y + dy, z + dz, c))
        for y in range(NY)
        for z in range(NZ)
        for c in range(NC)
    ]
    return lax.ppermute(arr, "ep", pairs)


def swap_core(arr):
    return lax.ppermute(arr, "ep", [(i, i ^ 1) for i in range(NY * NZ * NC)])


def shift_dp(arr, by):
    return lax.ppermute(arr, "dp", [(i, (i + by) % NDP) for i in range(NDP)])


def join_kernel(count, *refs):
    out_ref = refs[-1]
    at = 0
    for ref in refs[:count]:
        out_ref[at : at + ref.shape[0], :] = ref[...]
        at += ref.shape[0]


def join(parts, after=()):
    rows = sum(part.shape[0] for part in parts)
    return pl.pallas_call(
        functools.partial(join_kernel, len(parts)),
        out_shape=jax.ShapeDtypeStruct((rows, parts[0].shape[1]), parts[0].dtype),
        in_specs=[VM] * len(parts) + [pl.BlockSpec(memory_space=pl.ANY)] * len(after),
        out_specs=VM,
        name="join",
    )(*parts, *after)


def cost(flops):
    return pl.CostEstimate(flops=flops, transcendentals=0, bytes_accessed=0)


VM = pl.BlockSpec(memory_space=pltpu.VMEM)
SM = pl.BlockSpec(memory_space=pltpu.SMEM)


def iota(shape, dim):
    return lax.broadcasted_iota(i32, shape, dim)


def pick_x_kernel(me_ref, *refs):
    blocks = refs[:5]
    own_ref, sib_ref, code_ref, meta_scr, sel_scr = refs[5:]
    me = me_ref[0]
    n = NZ * TOK
    at = 0
    for ref in blocks:
        meta_scr[at : at + ref.shape[0]] = ref[:, D:]
        at += ref.shape[0]
    lane = iota((n, META), 1)
    tok = iota((n, META), 0)
    low = iota((n, n), 0)
    col = iota((n, n), 1)
    before = jnp.where((col < low) & (col // TOK == low // TOK), 1.0, 0.0).astype(bf16)
    which = iota((2 * META, META), 0) // META == iota((2 * META, META), 1) // 64
    spread = jnp.where(which, 1.0, 0.0).astype(bf16)
    row_pos = (lane % CAP).astype(f32)
    here = tok // TOK == (lane % 64) // CAP
    mine = me.astype(f32)
    other = (me ^ 1).astype(f32)

    def step(b, _):
        part = pl.ds(pl.multiple_of(b * n, n), n)
        meta = meta_scr[part].astype(f32)
        ids = lane < TOPK
        hits = jnp.concatenate(
            [
                jnp.where(ids & (meta == mine), 1.0, 0.0).astype(bf16),
                jnp.where(ids & (meta == other), 1.0, 0.0).astype(bf16),
            ],
            axis=1,
        )
        named = dot(hits, spread)
        earlier = dot(before, named.astype(bf16))
        code = jnp.where(named > 0, earlier, -1.0)
        code_ref[b] = code.astype(bf16)
        sel_scr[part] = jnp.where((code == row_pos) & here, 1.0, 0.0).astype(bf16)
        return 0

    lax.fori_loop(0, NY, step, 0)
    for b in range(NY):
        mine_refs = blocks[b : b + 1] if b < 3 else blocks[3:]
        rows = 0.0
        at = b * n
        for ref in mine_refs:
            size = ref.shape[0]
            rows = rows + dot(sel_scr[at : at + size], ref[...], contract_first)
            at += size
        rows = rows.astype(bf16)
        own_ref[b * 64 : (b + 1) * 64, :] = rows[:64]
        sib_ref[b * 64 : (b + 1) * 64, :] = rows[64:]


def pick_x(me, blocks):
    return pl.pallas_call(
        pick_x_kernel,
        out_shape=(
            jax.ShapeDtypeStruct((HALF, DA), bf16),
            jax.ShapeDtypeStruct((HALF, DA), bf16),
            jax.ShapeDtypeStruct((NY, NZ * TOK, META), bf16),
        ),
        in_specs=[SM] + [VM] * 5,
        out_specs=(VM, VM, VM),
        scratch_shapes=[
            pltpu.VMEM((NY * NZ * TOK, META), bf16), pltpu.VMEM((NY * NZ * TOK, META), bf16),
        ],
        compiler_params=pltpu.CompilerParams(vmem_limit_bytes=VLIM),
        name="pick_x",
    )(me, *blocks)


def pick_cot_kernel(code_ref, *refs):
    blocks = refs[:9]
    own_ref, sib_ref, own_acc, sib_acc = refs[10:]
    n = NY * TOK
    lane = iota((n, META), 1)
    tok = iota((n, META), 0)
    row_pos = (lane % CAP).astype(f32)
    row_src = (lane % 64) // CAP
    place = 0
    for s in range(NZ):
        if DZ[s] == 4:
            blk = jnp.concatenate([blocks[place][...], blocks[place + 1][...]], axis=0)
            place += 2
        else:
            blk = blocks[place][...]
            place += 1
        code = jnp.concatenate(
            [code_ref[b, s * TOK : (s + 1) * TOK, :] for b in range(NY)], axis=0
        ).astype(f32)
        sel = jnp.where((code == row_pos) & (tok // TOK == row_src), 1.0, 0.0).astype(bf16)
        rows = dot(sel, blk, contract_first)
        for b in range(NY):
            at = b * 64 + s * CAP
            own_acc[at : at + CAP, :] = rows[b * CAP : (b + 1) * CAP]
            sib_acc[at : at + CAP, :] = rows[64 + b * CAP : 64 + (b + 1) * CAP]
    own_ref[...] = own_acc[...].astype(bf16)
    sib_ref[...] = sib_acc[...].astype(bf16)


def pick_cot(code, blocks, after):
    return pl.pallas_call(
        pick_cot_kernel,
        out_shape=(
            jax.ShapeDtypeStruct((HALF, D), bf16),
            jax.ShapeDtypeStruct((HALF, D), bf16),
        ),
        in_specs=[VM] * 10 + [pl.BlockSpec(memory_space=pl.ANY)],
        out_specs=(VM, VM),
        scratch_shapes=[pltpu.VMEM((HALF, D), f32), pltpu.VMEM((HALF, D), f32)],
        compiler_params=pltpu.CompilerParams(vmem_limit_bytes=VLIM),
        cost_estimate=cost(20_000_000_000),
        name="pick_cot",
    )(code, *blocks, after)


def front_kernel(
    me_ref, own_ref, sib_ref, wg_ref, wu_ref,
    hid_ref, hid_t_ref, a_ref, b_ref, weight_ref, x_scr,
):
    @pl.when(pl.program_id(0) == 0)
    def _():
        x_scr[:HALF] = own_ref[:, :D]
        x_scr[HALF:] = sib_ref[:, :D]
        meta = jnp.concatenate([own_ref[:, D:], sib_ref[:, D:]], axis=0).astype(f32)
        expert = me_ref[0].astype(f32)
        total = jnp.zeros((ROWS, 1), f32)
        for k in range(TOPK):
            total = total + jnp.where(
                meta[:, k : k + 1] == expert, meta[:, TOPK + k : TOPK + k + 1], 0.0
            )
        weight_ref[...] = jnp.broadcast_to(total, (ROWS, META))

    x = x_scr[...]
    gate = dot(x, wg_ref[...])
    up = dot(x, wu_ref[...])
    sig = jax.nn.sigmoid(gate)
    act = gate * sig
    hid = (act * up).astype(bf16)
    hid_ref[...] = hid
    hid_t_ref[...] = hid.T
    a_ref[...] = up * (sig * (1.0 + gate * (1.0 - sig)))
    b_ref[...] = act


def front(me, own, sib, wg, wu):
    whole = lambda shape: pl.BlockSpec(shape, lambda j: (0,) * len(shape))
    wide = pl.BlockSpec((ROWS, FB), lambda j: (0, j))
    return pl.pallas_call(
        front_kernel,
        grid=(NFB,),
        out_shape=(
            jax.ShapeDtypeStruct((ROWS, FF), bf16),
            jax.ShapeDtypeStruct((FF, ROWS), bf16),
            jax.ShapeDtypeStruct((ROWS, FF), f32),
            jax.ShapeDtypeStruct((ROWS, FF), f32),
            jax.ShapeDtypeStruct((ROWS, META), f32),
        ),
        in_specs=[
            SM, whole((HALF, DA)), whole((HALF, DA)),
            pl.BlockSpec((D, FB), lambda j: (0, j)),
            pl.BlockSpec((D, FB), lambda j: (0, j)),
        ],
        out_specs=(
            wide, pl.BlockSpec((FB, ROWS), lambda j: (j, 0)), wide, wide,
            whole((ROWS, META)),
        ),
        scratch_shapes=[pltpu.VMEM((ROWS, D), bf16)],
        compiler_params=pltpu.CompilerParams(vmem_limit_bytes=VLIM),
        cost_estimate=cost(1_000_000_000),
        name="front",
    )(me, own, sib, wg, wu)


def piece_into(out_ref, x_own, x_sib, gg_ref, gu_ref, hid_t_ref, scot_cols):
    for n, ref in enumerate((gg_ref, gu_ref)):
        value = dot(x_own, ref[:HALF], contract_first) + dot(x_sib, ref[HALF:], contract_first)
        out_ref[:, n * FF : (n + 1) * FF] = value.astype(bf16)
    for q in range(NFB):
        value = dot(hid_t_ref[q * FB : (q + 1) * FB], scot_cols)
        out_ref[:, 2 * FF + q * FB : 2 * FF + (q + 1) * FB] = value.astype(bf16)


def place(pos_ref, piece):
    return (2 * pos_ref[1] + piece) % (2 * NDP)


def mid_kernel(
    pos_ref, own_ref, sib_ref, hid_ref, hid_t_ref, a_ref, b_ref, weight_ref,
    xoa_ref, xsa_ref, xob_ref, xsb_ref, wd_ref,
    pa_ref, pb_ref, gg_ref, gu_ref, route_ref, scot_ref, cot_scr, x_scr, out_scr,
):
    j = pl.program_id(0)

    @pl.when(j == 0)
    def _():
        cot_scr[:HALF] = own_ref[...]
        cot_scr[HALF:] = sib_ref[...]
        weight = weight_ref[:, :1]
        scot_ref[...] = (weight * cot_scr[...].astype(f32)).astype(bf16)
        route_ref[...] = jnp.zeros_like(route_ref)
        for n, ref in enumerate((xoa_ref, xsa_ref, xob_ref, xsb_ref)):
            x_scr[n] = ref[...]

    back = dot(cot_scr[...], wd_ref[...], contract_last)
    part = jnp.sum(hid_ref[...].astype(f32) * back, axis=1, keepdims=True)
    route_ref[...] += jnp.broadcast_to(part, (ROWS, META))
    scaled = weight_ref[:, :1] * back
    cols = pl.ds(pl.multiple_of(j * FB, FB), FB)
    gg_ref[:, cols] = (scaled * a_ref[...]).astype(bf16)
    gu_ref[:, cols] = (scaled * b_ref[...]).astype(bf16)

    @pl.when(j == NFB - 1)
    def _():
        def step(n, _):
            some = pl.ds(pl.multiple_of(place(pos_ref, 4 + n) * PIECE, PIECE), PIECE)
            piece_into(
                out_scr.at[n], x_scr[2 * n], x_scr[2 * n + 1], gg_ref, gu_ref, hid_t_ref,
                scot_ref[:, some],
            )
            return 0

        lax.fori_loop(0, 2, step, 0)
        pa_ref[...] = out_scr[0]
        pb_ref[...] = out_scr[1]


def whole(shape):
    return pl.BlockSpec(shape, lambda *_: (0,) * len(shape))


def mid(pos, own, sib, hid, hid_t, a, b, weight, x_own, x_sib, wd):
    wide = pl.BlockSpec((ROWS, FB), lambda j, pos_ref: (0, j))
    xa = pl.BlockSpec((HALF, PIECE), lambda j, pos_ref: (0, place(pos_ref, 4)))
    xb = pl.BlockSpec((HALF, PIECE), lambda j, pos_ref: (0, place(pos_ref, 5)))
    return pl.pallas_call(
        mid_kernel,
        out_shape=(
            jax.ShapeDtypeStruct((PIECE, 3 * FF), bf16),
            jax.ShapeDtypeStruct((PIECE, 3 * FF), bf16),
            jax.ShapeDtypeStruct((ROWS, FF), bf16),
            jax.ShapeDtypeStruct((ROWS, FF), bf16),
            jax.ShapeDtypeStruct((ROWS, META), f32),
            jax.ShapeDtypeStruct((ROWS, D), bf16),
        ),
        grid_spec=pltpu.PrefetchScalarGridSpec(
            num_scalar_prefetch=1,
            grid=(NFB,),
            in_specs=[
                whole((HALF, D)), whole((HALF, D)), wide, whole((FF, ROWS)), wide, wide,
                whole((ROWS, META)), xa, xa, xb, xb,
                pl.BlockSpec((FB, D), lambda j, pos_ref: (j, 0)),
            ],
            out_specs=(
                whole((PIECE, 3 * FF)), whole((PIECE, 3 * FF)), whole((ROWS, FF)),
                whole((ROWS, FF)), whole((ROWS, META)), whole((ROWS, D)),
            ),
            scratch_shapes=[
                pltpu.VMEM((ROWS, D), bf16),
                pltpu.VMEM((4, HALF, PIECE), bf16),
                pltpu.VMEM((2, PIECE, 3 * FF), bf16),
            ],
        ),
        compiler_params=pltpu.CompilerParams(vmem_limit_bytes=VLIM),
        name="mid",
    )(pos, own, sib, hid, hid_t, a, b, weight, x_own, x_sib, x_own, x_sib, wd)


def rest_piece(n):
    first = jnp.where(n == 0, 3, 6)
    second = jnp.where(n == 2, 2, 7)
    return jnp.where(n < 2, first, jnp.where(n < 4, second, n - 4))


def rest_kernel(
    pos_ref, x_own_ref, x_sib_ref, scot_ref, gg_ref, gu_ref, hid_t_ref,
    pa_ref, pb_ref, more_ref, out_scr,
):
    n = pl.program_id(0)
    piece_into(
        out_scr, x_own_ref[...], x_sib_ref[...], gg_ref, gu_ref, hid_t_ref, scot_ref[...]
    )

    @pl.when(n == 0)
    def _():
        pa_ref[...] = out_scr[...]

    @pl.when(n == 1)
    def _():
        pb_ref[...] = out_scr[...]

    @pl.when(n > 1)
    def _():
        more_ref[...] = out_scr[...]


def rest(pos, x_own, x_sib, scot, gg, gu, hid_t):
    size = (PIECE, 3 * FF)
    x_spec = pl.BlockSpec((HALF, PIECE), lambda n, pos_ref: (0, place(pos_ref, rest_piece(n))))
    return pl.pallas_call(
        rest_kernel,
        out_shape=(
            jax.ShapeDtypeStruct(size, bf16),
            jax.ShapeDtypeStruct(size, bf16),
            jax.ShapeDtypeStruct((4 * PIECE, 3 * FF), bf16),
        ),
        grid_spec=pltpu.PrefetchScalarGridSpec(
            num_scalar_prefetch=1,
            grid=(6,),
            in_specs=[
                x_spec, x_spec,
                pl.BlockSpec((ROWS, PIECE), lambda n, pos_ref: (0, place(pos_ref, rest_piece(n)))),
                whole((ROWS, FF)), whole((ROWS, FF)), whole((FF, ROWS)),
            ],
            out_specs=(
                whole(size), whole(size),
                pl.BlockSpec(size, lambda n, pos_ref: (jnp.maximum(n - 2, 0), 0)),
            ),
            scratch_shapes=[pltpu.VMEM(size, bf16)],
        ),
        compiler_params=pltpu.CompilerParams(vmem_limit_bytes=VLIM),
        name="rest",
    )(pos, x_own, x_sib, scot, gg, gu, hid_t)


def add_kernel(more_ref, ra_ref, rb_ref, _, oa_ref, ob_ref):
    for n, (r_ref, o_ref) in enumerate(((ra_ref, oa_ref), (rb_ref, ob_ref))):
        value = more_ref[n * PIECE : (n + 1) * PIECE].astype(f32) + r_ref[...].astype(f32)
        o_ref[...] = value.astype(bf16)


def add(more, ra, rb, after):
    size = (PIECE, 3 * FF)
    thin = pl.BlockSpec((PIECE, FF), lambda j: (0, j))
    return pl.pallas_call(
        add_kernel,
        grid=(3,),
        out_shape=(jax.ShapeDtypeStruct(size, bf16), jax.ShapeDtypeStruct(size, bf16)),
        in_specs=[
            pl.BlockSpec((2 * PIECE, FF), lambda j: (0, j)), thin, thin,
            pl.BlockSpec(memory_space=pl.ANY),
        ],
        out_specs=(thin, thin),
        name="add",
    )(more, ra, rb, after)


def final_kernel(more_ref, r2a, r2b, r3a, r3b, gate_ref, up_ref, down_ref):
    j = pl.program_id(0)
    for n, refs in enumerate(((r2a, r3a), (r2b, r3b))):
        side = slice(n * PIECE, (n + 1) * PIECE)
        value = more_ref[side].astype(f32)
        for ref in refs:
            value = value + ref[...].astype(f32)
        value = value.astype(bf16)

        @pl.when(j == 0)
        def _():
            gate_ref[0, side, :] = value

        @pl.when(j == 1)
        def _():
            up_ref[0, side, :] = value

        @pl.when(j == 2)
        def _():
            for q in range(NFB):
                down_ref[0, q * FB : (q + 1) * FB, side] = value[:, q * FB : (q + 1) * FB]


def final(more, *arrived):
    per = D // NDP
    thin = pl.BlockSpec((PIECE, FF), lambda j: (0, j))
    return pl.pallas_call(
        final_kernel,
        grid=(3,),
        out_shape=(
            jax.ShapeDtypeStruct((1, per, FF), bf16),
            jax.ShapeDtypeStruct((1, per, FF), bf16),
            jax.ShapeDtypeStruct((1, FF, per), bf16),
        ),
        in_specs=[pl.BlockSpec((2 * PIECE, FF), lambda j: (1, j))] + [thin] * 4,
        out_specs=(whole((1, per, FF)), whole((1, per, FF)), whole((1, FF, per))),
        compiler_params=pltpu.CompilerParams(vmem_limit_bytes=VLIM),
        cost_estimate=cost(30_000_000_000),
        name="final",
    )(more, *arrived)


def slots_kernel(me_ref, gg_ref, gu_ref, route_ref, wg_ref, wu_ref, _, out_ref, scr):
    me = me_ref[0]
    core = me % NC
    z = (me // NC) % NZ
    y = me // (NC * NZ)
    quarter = ROWS // 4

    def part(i, _):
        rows = pl.ds(pl.multiple_of(i * quarter, quarter), quarter)
        scr[rows] = dot(gg_ref[rows], wg_ref[...], contract_last) + dot(
            gu_ref[rows], wu_ref[...], contract_last
        )
        return 0

    lax.fori_loop(0, 4, part, 0)

    def put(i, _):
        h, b, s = i // (NY * NZ), (i // NZ) % NY, i % NZ
        dy = jnp.where(b == 1, NY - 1, jnp.where(b == 2, 1, b - b // 3))
        dz = jnp.where(s % 2 == 1, NZ - (s + 1) // 2, s // 2)
        to = (((y + dy) % NY) * NZ + (z + dz) % NZ) * NC + (core + h) % NC
        rows = pl.ds(pl.multiple_of(i * CAP, CAP), CAP)
        out_ref[to, :, :D] = scr[rows, :].astype(bf16)
        out_ref[to, :, D:] = route_ref[rows, :].astype(bf16)
        return 0

    lax.fori_loop(0, 2 * NY * NZ, put, 0)


def slots(me, gg, gu, route, wg, wu, after):
    return pl.pallas_call(
        slots_kernel,
        out_shape=jax.ShapeDtypeStruct((NY * NZ * NC, CAP, DA), bf16),
        in_specs=[SM] + [VM] * 5 + [pl.BlockSpec(memory_space=pl.ANY)],
        out_specs=VM,
        scratch_shapes=[pltpu.VMEM((ROWS, D), f32)],
        compiler_params=pltpu.CompilerParams(vmem_limit_bytes=VLIM),
        name="slots",
    )(me, gg, gu, route, wg, wu, after)


def body(tokens, cotangent, expert_ids, route_weights, w_gate, w_up, w_down):
    pos = jnp.stack([lax.axis_index("ep"), lax.axis_index("dp")]).astype(i32)
    meta = jnp.concatenate(
        [expert_ids.astype(bf16), route_weights, jnp.zeros((TOK, META - 2 * TOPK), bf16)], axis=1
    )
    xa = jnp.concatenate([tokens, meta], axis=1)

    c1 = shift(cotangent, dy=1)
    c2 = shift(cotangent, dy=-1)
    c3 = shift(c1, dy=1)

    u = [xa]
    d = [xa]
    for _ in range(3):
        u.append(shift(u[-1], dz=1))
        d.append(shift(d[-1], dz=-1))
    u.append(shift(u[-1], dz=1))

    def ring_y(part):
        p1 = shift(part, dy=1)
        m1 = shift(part, dy=-1)
        n = part.shape[0] // 2
        return part, p1, m1, shift(p1[:n], dy=1), shift(m1[n:], dy=-1)

    blocks = ring_y(join([xa, u[1], d[1], u[2], d[2], u[3], d[3], u[4]], after=[c2, c3]))
    cot0 = join([cotangent, c1, c2, c3], after=[u[3], d[3]])
    cu = [cot0]
    cd = [cot0]
    for _ in range(3):
        cu.append(shift(cu[-1], dz=1))
        cd.append(shift(cd[-1], dz=-1))
    n = NY * TOK // 2
    cq = [shift(cu[-1][:n], dz=1), shift(cd[-1][n:], dz=-1)]

    own_x, sib_x, code = pick_x(pos, blocks)
    sib_x = swap_core(sib_x)
    wg, wu, wd = w_gate[0], w_up[0], w_down[0]
    hid, hid_t, a, b, weight = front(pos, own_x, sib_x, wg, wu)

    parts = [cot0, cu[1], cd[1], cu[2], cd[2], cu[3], cd[3], *cq]
    own_c, sib_c = pick_cot(code, parts, after=hid)
    sib_c = swap_core(sib_c)

    p2a, p2b, gg, gu, route, scot = mid(
        pos, own_c, sib_c, hid, hid_t, a, b, weight, own_x, sib_x, wd
    )
    r1a, r1b = shift_dp(p2a, 1), shift_dp(p2b, -1)
    p1b, p3a, more = rest(pos, own_x, sib_x, scot, gg, gu, hid_t)
    r2b, r2a = shift_dp(p1b, 1), shift_dp(p3a, -1)
    out = slots(pos, gg, gu, route, wg, wu, after=p1b)
    got = lax.all_to_all(out, "ep", split_axis=0, concat_axis=0, tiled=True)
    p1a, p3b = add(more, r1a, r1b, after=out)
    r3a, r3b = shift_dp(p1a, 1), shift_dp(p3b, -1)
    grad_gate, grad_up, grad_down = final(more, r2a, r2b, r3a, r3b)

    experts = NY * NZ * NC
    one = (expert_ids[:, :, None] == jnp.arange(experts, dtype=i32)).astype(i32)
    named = jnp.sum(one, axis=1)
    token = jnp.arange(TOK, dtype=i32)
    lower = (token[None, :] < token[:, None]).astype(bf16)
    earlier = dot(lower, named.astype(bf16)).astype(i32)
    row = jnp.arange(experts * CAP, dtype=i32)
    code_of = jnp.repeat(jnp.where(named > 0, earlier, -1), CAP, axis=1)
    sel = code_of == (row % CAP)[None, :]
    got = got.reshape(experts * CAP, DA)
    grad_tokens = dot(sel.astype(bf16), got[:, :D]).astype(bf16)
    mine = sel[:, None, :] & (expert_ids[:, :, None] == (row // CAP)[None, None, :])
    grad_route = jnp.sum(jnp.where(mine, got[:, D].astype(f32), 0.0), axis=2).astype(bf16)

    return grad_tokens, grad_route, grad_gate, grad_up, grad_down


def solution(mesh):
    row = P(("ep", "dp"), None)
    expert = P("ep", None, None)
    return jax.shard_map(
        body,
        mesh=mesh,
        in_specs=(row, row, row, row, expert, expert, expert),
        out_specs=(row, row, P("ep", "dp", None), P("ep", "dp", None), P("ep", None, "dp")),
        check_vma=False,
    )
```

profile of v0, /device:TPU:1, one launch (start us, length us, event | category | flops | bytes accessed | tf_op | source)
XLA Modules:
  0.0 234.7 jit_solution(3785742492272842370)
XLA Ops:
  5.7 4.0 %collective-permute-start.1 = (bf16[32,2176]{1,0:T(8,128)(2,1)S(1)}, bf16[32,2176]{1,0:T(8,128)(2,1)S(1)}, u32[]{:S(2)}, u32[]{:S(2)}) collective-permute-start(bf16[32,2176]{1,0:T(8,128)(2,1)S(1)} %concatenate.3.refs_0_), channel_id=1, source_target_pairs={{0,56},{4,60},{8,0},{12,4},{16,8},{20,12},{24,16},{28,20},{32,24},... | collective-permute-start | bytes 417800 | tf_op jit(solution)/shard_map/ppermute | solution.py:52
  9.8 3.3 %collective-permute-done.refs_1_ = bf16[32,2176]{1,0:T(8,128)(2,1)S(1)} collective-permute-done((bf16[32,2176]{1,0:T(8,128)(2,1)S(1)}, bf16[32,2176]{1,0:T(8,128)(2,1)S(1)}, u32[]{:S(2)}, u32[]{:S(2)}) %collective-permute-start) | collective-permute-done | bytes 139296 | tf_op jit(solution)/shard_map/ppermute | solution.py:52
  19.5 2.7 %collective-permute-start.5 = (bf16[32,2176]{1,0:T(8,128)(2,1)S(1)}, bf16[32,2176]{1,0:T(8,128)(2,1)S(1)}, u32[]{:S(2)}, u32[]{:S(2)}) collective-permute-start(bf16[32,2176]{1,0:T(8,128)(2,1)S(1)} %collective-permute-done.3.refs_4_), channel_id=1, source_target_pairs={{0,56},{4,60},{8,0},{12,4},{16,8},{20,12},{24,16},{28,20},{32,24},... | collective-permute-start | bytes 417800 | tf_op jit(solution)/shard_map/ppermute | solution.py:52
  23.3 2.7 %collective-permute-start.7 = (bf16[32,2048]{1,0:T(8,128)(2,1)}, bf16[32,2048]{1,0:T(8,128)(2,1)S(1)}, u32[]{:S(2)}, u32[]{:S(2)}) collective-permute-start(bf16[32,2048]{1,0:T(8,128)(2,1)} %refs_0_.1), channel_id=1, source_target_pairs={{0,192},{4,196},{8,200},{12,204},{16,208},{20,212},{24,216},{28,22... | collective-permute-start | bytes 393224 | tf_op jit(solution)/shard_map/ppermute | solution.py:52
  28.3 3.1 %collective-permute-done.9.refs_9_.refs_3_ = bf16[32,2048]{1,0:T(8,128)(2,1)S(1)} collective-permute-done((bf16[32,2048]{1,0:T(8,128)(2,1)S(1)}, bf16[32,2048]{1,0:T(8,128)(2,1)S(1)}, u32[]{:S(2)}, u32[]{:S(2)}) %collective-permute-start.9) | collective-permute-done | bytes 131104 | tf_op jit(solution)/shard_map/ppermute | solution.py:52
  35.2 2.7 %collective-permute-start.11 = (bf16[256,2176]{1,0:T(8,128)(2,1)}, bf16[256,2176]{1,0:T(8,128)(2,1)S(1)}, u32[]{:S(2)}, u32[]{:S(2)}) collective-permute-start(bf16[256,2176]{1,0:T(8,128)(2,1)} %join.2.refs_0_), channel_id=1, source_target_pairs={{0,192},{4,196},{8,200},{12,204},{16,208},{20,212},{24,216},{28,22... | collective-permute-start | bytes 3342344 | tf_op jit(solution)/shard_map/ppermute | solution.py:52
  39.8 2.7 %collective-permute-start.15 = (bf16[128,2048]{1,0:T(8,128)(2,1)}, bf16[128,2048]{1,0:T(8,128)(2,1)}, u32[]{:S(2)}, u32[]{:S(2)}) collective-permute-start(bf16[128,2048]{1,0:T(8,128)(2,1)} %join.3.refs_0_), channel_id=1, source_target_pairs={{0,56},{4,60},{8,0},{12,4},{16,8},{20,12},{24,16},{28,20},{32,24},... | collective-permute-start | bytes 1572872 | tf_op jit(solution)/shard_map/ppermute | solution.py:52
  42.4 15.5 %collective-permute-done.10.refs_1_ = bf16[256,2176]{1,0:T(8,128)(2,1)S(1)} collective-permute-done((bf16[256,2176]{1,0:T(8,128)(2,1)}, bf16[256,2176]{1,0:T(8,128)(2,1)S(1)}, u32[]{:S(2)}, u32[]{:S(2)}) %collective-permute-start.10) | collective-permute-done | bytes 1114144 | tf_op jit(solution)/shard_map/ppermute | solution.py:52
  65.8 3.1 %collective-permute-done.12.refs_3_ = bf16[128,2176]{1,0:T(8,128)(2,1)S(1)} collective-permute-done((bf16[128,2176]{1,0:T(8,128)(2,1)}, bf16[128,2176]{1,0:T(8,128)(2,1)S(1)}, u32[]{:S(2)}, u32[]{:S(2)}) %collective-permute-start.12) | collective-permute-done | bytes 557088 | tf_op jit(solution)/shard_map/ppermute | solution.py:52
  70.4 6.3 %pick_x.1 = (bf16[256,2176]{1,0:T(8,128)(2,1)}, bf16[256,2176]{1,0:T(8,128)(2,1)}, bf16[4,256,128]{2,1,0:T(8,128)(2,1)}) custom-call(s32[2]{0:T(128)} %pad_add_fusion.me_ref.pos_ref, bf16[256,2176]{1,0:T(8,128)(2,1)} %join.2.refs_0_, bf16[256,2176]{1,0:T(8,128)(2,1)} %copy-done.1, bf16[256,2176]{1,0:T(8,128)(2,1)} %copy-done.2, bf16[128,2176]{1,0:T(8,128)(2,1)} %copy-done.5, ...), custom_call_target="tpu_custom_call" | custom-call | tf_op jit(solution)/shard_map/pick_x/pallas_call | solution.py:148
  76.7 6.7 %collective-permute-start.22 = (bf16[256,2176]{1,0:T(8,128)(2,1)}, bf16[256,2176]{1,0:T(8,128)(2,1)S(1)}, u32[]{:S(2)}, u32[]{:S(2)}) collective-permute-start(bf16[256,2176]{1,0:T(8,128)(2,1)} %get-tuple-element.31), channel_id=1, source_target_pairs={{0,4},{4,0},{8,12},{12,8},{16,20},{20,16},{24,28},{28,24},{32,36},... | collective-permute-start | bytes 3342344 | tf_op jit(solution)/shard_map/ppermute | solution.py:56
  83.4 3.0 %collective-permute-start.19 = (bf16[128,2048]{1,0:T(8,128)(2,1)}, bf16[128,2048]{1,0:T(8,128)(2,1)S(1)}, u32[]{:S(2)}, u32[]{:S(2)}) collective-permute-start(bf16[128,2048]{1,0:T(8,128)(2,1)} %collective-permute-done.17.refs_4_), channel_id=1, source_target_pairs={{0,56},{4,60},{8,0},{12,4},{16,8},{20,12},{24,16},{28,20},{32,24},... | collective-permute-start | bytes 1572872 | tf_op jit(solution)/shard_map/ppermute | solution.py:52
  86.4 12.3 %collective-permute-done.18.refs_5_ = bf16[128,2048]{1,0:T(8,128)(2,1)S(1)} collective-permute-done((bf16[128,2048]{1,0:T(8,128)(2,1)}, bf16[128,2048]{1,0:T(8,128)(2,1)S(1)}, u32[]{:S(2)}, u32[]{:S(2)}) %collective-permute-start.18) | collective-permute-done | bytes 524320 | tf_op jit(solution)/shard_map/ppermute | solution.py:52
  98.9 2.7 %collective-permute-start.21 = (bf16[64,2048]{1,0:T(8,128)(2,1)S(1)}, bf16[64,2048]{1,0:T(8,128)(2,1)S(1)}, u32[]{:S(2)}, u32[]{:S(2)}) collective-permute-start(bf16[64,2048]{1,0:T(8,128)(2,1)S(1)} %slice.27), channel_id=1, source_target_pairs={{0,56},{4,60},{8,0},{12,4},{16,8},{20,12},{24,16},{28,20},{32,24},... | collective-permute-start | bytes 786440 | tf_op jit(solution)/shard_map/ppermute | solution.py:52
  102.6 8.8 %front.1 = (bf16[512,768]{1,0:T(8,128)(2,1)}, bf16[768,512]{1,0:T(8,128)(2,1)}, f32[512,768]{1,0:T(8,128)}, f32[512,768]{1,0:T(8,128)}, f32[512,128]{1,0:T(8,128)}) custom-call(s32[2]{0:T(128)} %pad_add_fusion.me_ref.pos_ref, bf16[256,2176]{1,0:T(8,128)(2,1)} %get-tuple-element.30.own_ref.xoa_ref.xob_ref.x_own_ref, bf16[256,2176]{1,0:T(8,128)(2,1)} %copy-done, ...), custom_call_target="tpu_custom_call" | custom-call | flops 1000000000 | tf_op jit(solution)/shard_map/front/pallas_call | solution.py:242
  112.3 4.8 %pick_cot.1 = (bf16[256,2048]{1,0:T(8,128)(2,1)}, bf16[256,2048]{1,0:T(8,128)(2,1)}) custom-call(bf16[4,256,128]{2,1,0:T(8,128)(2,1)} %get-tuple-element.29.code_ref, bf16[128,2048]{1,0:T(8,128)(2,1)} %join.3.refs_0_, bf16[128,2048]{1,0:T(8,128)(2,1)} %collective-permute-done.14.refs_1_, bf16[128,2048]{1,0:T(8,128)(2,1)} %collective-permute-done.15.refs_2_, ...), custom_call_target="tpu_custom_call" | custom-call | flops 20000000000 | tf_op jit(solution)/shard_map/pick_cot/pallas_call | solution.py:195
  121.8 11.7 %mid.1 = (bf16[256,2304]{1,0:T(8,128)(2,1)}, bf16[256,2304]{1,0:T(8,128)(2,1)}, bf16[512,768]{1,0:T(8,128)(2,1)}, bf16[512,768]{1,0:T(8,128)(2,1)}, f32[512,128]{1,0:T(8,128)}, /*index=5*/bf16[512,2048]{1,0:T(8,128)(2,1)}) custom-call(s32[2]{0:T(128)} %pad_add_fusion.me_ref.pos_ref, bf16[256,2048]{1,0:T(8,128)(2,1)} %get-tuple-element.33.own_ref, ...), custom_call_target="tpu_custom_call" | custom-call | tf_op jit(solution)/shard_map/mid/pallas_call | solution.py:329
  136.2 10.7 %rest.1 = (bf16[256,2304]{1,0:T(8,128)(2,1)}, bf16[256,2304]{1,0:T(8,128)(2,1)}, bf16[1024,2304]{1,0:T(8,128)(2,1)}) custom-call(s32[2]{0:T(128)} %pad_add_fusion.me_ref.pos_ref, bf16[256,2176]{1,0:T(8,128)(2,1)} %get-tuple-element.30.own_ref.xoa_ref.xob_ref.x_own_ref, bf16[256,2176]{1,0:T(8,128)(2,1)} %copy-done, ...), custom_call_target="tpu_custom_call" | custom-call | tf_op jit(solution)/shard_map/rest/pallas_call | solution.py:393
  146.9 15.9 %slots.1._ = bf16[64,8,2176]{2,1,0:T(8,128)(2,1)} custom-call(s32[2]{0:T(128)} %pad_add_fusion.me_ref.pos_ref, bf16[512,768]{1,0:T(8,128)(2,1)} %get-tuple-element.39.gg_ref, bf16[512,768]{1,0:T(8,128)(2,1)} %get-tuple-element.40.gu_ref, f32[512,128]{1,0:T(8,128)} %get-tuple-element.41.route_ref, bf16[2048,768]{1,0:T(8,128)(2,1)} %bitcast.11, ...), custom_call_target="tpu_custom_call" | custom-call | tf_op jit(solution)/shard_map/slots/pallas_call | solution.py:513
  162.8 10.0 %all-to-all-start = ((bf16[64,8,2176]{2,1,0:T(8,128)(2,1)}), bf16[64,8,2176]{2,1,0:T(8,128)(2,1)S(1)}, u32[]{:S(2)}, u32[]{:S(2)}) async-start(bf16[64,8,2176]{2,1,0:T(8,128)(2,1)} %slots.1._), calls=%async_computation | async-start | bytes 4456448 | tf_op jit(solution)/shard_map/all_to_all | solution.py:574
  175.6 4.6 %add.20 = (bf16[256,2304]{1,0:T(8,128)(2,1)}, bf16[256,2304]{1,0:T(8,128)(2,1)}) custom-call(bf16[1024,2304]{1,0:T(8,128)(2,1)} %get-tuple-element.44.more_ref, bf16[256,2304]{1,0:T(8,128)(2,1)} %collective-permute-done.26.ra_ref, bf16[256,2304]{1,0:T(8,128)(2,1)} %collective-permute-done.27.rb_ref, bf16[64,8,2176]{2,1,0:T(8,128)(2,1)} %slots.1._), custom_call_target="tpu_custom_call" | custom-call | tf_op jit(solution)/shard_map/add/pallas_call | solution.py:428
  183.5 16.9 %collective-permute-done.24.r2a = bf16[256,2304]{1,0:T(8,128)(2,1)} collective-permute-done((bf16[256,2304]{1,0:T(8,128)(2,1)}, bf16[256,2304]{1,0:T(8,128)(2,1)}, u32[]{:S(2)}, u32[]{:S(2)}) %collective-permute-start.24) | collective-permute-done | bytes 1179680 | tf_op jit(solution)/shard_map/ppermute | solution.py:60
  201.3 25.3 %collective-permute-done.28.r3a = bf16[256,2304]{1,0:T(8,128)(2,1)} collective-permute-done((bf16[256,2304]{1,0:T(8,128)(2,1)}, bf16[256,2304]{1,0:T(8,128)(2,1)}, u32[]{:S(2)}, u32[]{:S(2)}) %collective-permute-start.28) | collective-permute-done | bytes 1179680 | tf_op jit(solution)/shard_map/ppermute | solution.py:60
  226.6 5.8 %final.1 = (bf16[1,512,768]{2,1,0:T(8,128)(2,1)}, bf16[1,512,768]{2,1,0:T(8,128)(2,1)}, bf16[1,768,512]{2,1,0:T(8,128)(2,1)}) custom-call(bf16[1024,2304]{1,0:T(8,128)(2,1)} %get-tuple-element.44.more_ref, bf16[256,2304]{1,0:T(8,128)(2,1)} %collective-permute-done.24.r2a, bf16[256,2304]{1,0:T(8,128)(2,1)} %collective-permute-done.25.r2b, ...), custom_call_target="tpu_custom_call" | custom-call | flops 30000001024 | tf_op jit(solution)/shard_map/final/pallas_call | solution.py:467
  (117 shorter events, 48.5 us)
Async XLA Ops:
  3.2 9.9 %collective-permute-start = (bf16[32,2176]{1,0:T(8,128)(2,1)S(1)}, bf16[32,2176]{1,0:T(8,128)(2,1)S(1)}, u32[]{:S(2)}, u32[]{:S(2)}) collective-permute-start(bf16[32,2176]{1,0:T(8,128)(2,1)S(1)} %concatenate.3.refs_0_), channel_id=1, source_target_pairs={{0,8},{4,12},{8,16},{12,20},{16,24},{20,28},{24,32},{28,36},{32,40... | collective-permute-start | bytes 417800 | tf_op jit(solution)/shard_map/ppermute | solution.py:52
  18.2 7.9 %collective-permute-start.8 = (bf16[32,2048]{1,0:T(8,128)(2,1)}, bf16[32,2048]{1,0:T(8,128)(2,1)S(1)}, u32[]{:S(2)}, u32[]{:S(2)}) collective-permute-start(bf16[32,2048]{1,0:T(8,128)(2,1)} %refs_0_.1), channel_id=1, source_target_pairs={{0,64},{4,68},{8,72},{12,76},{16,80},{20,84},{24,88},{28,92},{32,9... | collective-permute-start | bytes 393224 | tf_op jit(solution)/shard_map/ppermute | solution.py:52
  19.5 11.9 %collective-permute-start.5 = (bf16[32,2176]{1,0:T(8,128)(2,1)S(1)}, bf16[32,2176]{1,0:T(8,128)(2,1)S(1)}, u32[]{:S(2)}, u32[]{:S(2)}) collective-permute-start(bf16[32,2176]{1,0:T(8,128)(2,1)S(1)} %collective-permute-done.3.refs_4_), channel_id=1, source_target_pairs={{0,56},{4,60},{8,0},{12,4},{16,8},{20,12},{24,16},{28,20},{32,24},... | collective-permute-start | bytes 417800 | tf_op jit(solution)/shard_map/ppermute | solution.py:52
  23.3 8.1 %collective-permute-start.6 = (bf16[32,2176]{1,0:T(8,128)(2,1)S(1)}, bf16[32,2176]{1,0:T(8,128)(2,1)S(1)}, u32[]{:S(2)}, u32[]{:S(2)}) collective-permute-start(bf16[32,2176]{1,0:T(8,128)(2,1)S(1)} %collective-permute-done.4.refs_5_.refs_4_), channel_id=1, source_target_pairs={{0,8},{4,12},{8,16},{12,20},{16,24},{20,28},{24,32},{28,36},{32,40... | collective-permute-start | bytes 417800 | tf_op jit(solution)/shard_map/ppermute | solution.py:52
  35.2 22.8 %collective-permute-start.10 = (bf16[256,2176]{1,0:T(8,128)(2,1)}, bf16[256,2176]{1,0:T(8,128)(2,1)S(1)}, u32[]{:S(2)}, u32[]{:S(2)}) collective-permute-start(bf16[256,2176]{1,0:T(8,128)(2,1)} %join.2.refs_0_), channel_id=1, source_target_pairs={{0,64},{4,68},{8,72},{12,76},{16,80},{20,84},{24,88},{28,92},{32,9... | collective-permute-start | bytes 3342344 | tf_op jit(solution)/shard_map/ppermute | solution.py:52
  35.2 23.7 %collective-permute-start.11 = (bf16[256,2176]{1,0:T(8,128)(2,1)}, bf16[256,2176]{1,0:T(8,128)(2,1)S(1)}, u32[]{:S(2)}, u32[]{:S(2)}) collective-permute-start(bf16[256,2176]{1,0:T(8,128)(2,1)} %join.2.refs_0_), channel_id=1, source_target_pairs={{0,192},{4,196},{8,200},{12,204},{16,208},{20,212},{24,216},{28,22... | collective-permute-start | bytes 3342344 | tf_op jit(solution)/shard_map/ppermute | solution.py:52
  39.8 22.7 %collective-permute-start.14 = (bf16[128,2048]{1,0:T(8,128)(2,1)}, bf16[128,2048]{1,0:T(8,128)(2,1)}, u32[]{:S(2)}, u32[]{:S(2)}) collective-permute-start(bf16[128,2048]{1,0:T(8,128)(2,1)} %join.3.refs_0_), channel_id=1, source_target_pairs={{0,8},{4,12},{8,16},{12,20},{16,24},{20,28},{24,32},{28,36},{32,40... | collective-permute-start | bytes 1572872 | tf_op jit(solution)/shard_map/ppermute | solution.py:52
  39.8 22.7 %collective-permute-start.15 = (bf16[128,2048]{1,0:T(8,128)(2,1)}, bf16[128,2048]{1,0:T(8,128)(2,1)}, u32[]{:S(2)}, u32[]{:S(2)}) collective-permute-start(bf16[128,2048]{1,0:T(8,128)(2,1)} %join.3.refs_0_), channel_id=1, source_target_pairs={{0,56},{4,60},{8,0},{12,4},{16,8},{20,12},{24,16},{28,20},{32,24},... | collective-permute-start | bytes 1572872 | tf_op jit(solution)/shard_map/ppermute | solution.py:52
  58.9 10.0 %collective-permute-start.12 = (bf16[128,2176]{1,0:T(8,128)(2,1)}, bf16[128,2176]{1,0:T(8,128)(2,1)S(1)}, u32[]{:S(2)}, u32[]{:S(2)}) collective-permute-start(bf16[128,2176]{1,0:T(8,128)(2,1)} %slice.24), channel_id=1, source_target_pairs={{0,64},{4,68},{8,72},{12,76},{16,80},{20,84},{24,88},{28,92},{32,9... | collective-permute-start | bytes 1671176 | tf_op jit(solution)/shard_map/ppermute | solution.py:52
  59.8 9.4 %collective-permute-start.13 = (bf16[128,2176]{1,0:T(8,128)(2,1)}, bf16[128,2176]{1,0:T(8,128)(2,1)S(1)}, u32[]{:S(2)}, u32[]{:S(2)}) collective-permute-start(bf16[128,2176]{1,0:T(8,128)(2,1)} %slice.25), channel_id=1, source_target_pairs={{0,192},{4,196},{8,200},{12,204},{16,208},{20,212},{24,216},{28,22... | collective-permute-start | bytes 1671176 | tf_op jit(solution)/shard_map/ppermute | solution.py:52
  62.5 20.9 %collective-permute-start.16 = (bf16[128,2048]{1,0:T(8,128)(2,1)}, bf16[128,2048]{1,0:T(8,128)(2,1)}, u32[]{:S(2)}, u32[]{:S(2)}) collective-permute-start(bf16[128,2048]{1,0:T(8,128)(2,1)} %collective-permute-done.14.refs_1_), channel_id=1, source_target_pairs={{0,8},{4,12},{8,16},{12,20},{16,24},{20,28},{24,32},{28,36},{32,40... | collective-permute-start | bytes 1572872 | tf_op jit(solution)/shard_map/ppermute | solution.py:52
  62.5 20.9 %collective-permute-start.17 = (bf16[128,2048]{1,0:T(8,128)(2,1)}, bf16[128,2048]{1,0:T(8,128)(2,1)}, u32[]{:S(2)}, u32[]{:S(2)}) collective-permute-start(bf16[128,2048]{1,0:T(8,128)(2,1)} %collective-permute-done.15.refs_2_), channel_id=1, source_target_pairs={{0,56},{4,60},{8,0},{12,4},{16,8},{20,12},{24,16},{28,20},{32,24},... | collective-permute-start | bytes 1572872 | tf_op jit(solution)/shard_map/ppermute | solution.py:52
  76.7 24.9 %collective-permute-start.22 = (bf16[256,2176]{1,0:T(8,128)(2,1)}, bf16[256,2176]{1,0:T(8,128)(2,1)S(1)}, u32[]{:S(2)}, u32[]{:S(2)}) collective-permute-start(bf16[256,2176]{1,0:T(8,128)(2,1)} %get-tuple-element.31), channel_id=1, source_target_pairs={{0,4},{4,0},{8,12},{12,8},{16,20},{20,16},{24,28},{28,24},{32,36},... | collective-permute-start | bytes 3342344 | tf_op jit(solution)/shard_map/ppermute | solution.py:56
  83.4 15.4 %collective-permute-start.18 = (bf16[128,2048]{1,0:T(8,128)(2,1)}, bf16[128,2048]{1,0:T(8,128)(2,1)S(1)}, u32[]{:S(2)}, u32[]{:S(2)}) collective-permute-start(bf16[128,2048]{1,0:T(8,128)(2,1)} %collective-permute-done.16.refs_3_), channel_id=1, source_target_pairs={{0,8},{4,12},{8,16},{12,20},{16,24},{20,28},{24,32},{28,36},{32,40... | collective-permute-start | bytes 1572872 | tf_op jit(solution)/shard_map/ppermute | solution.py:52
  83.4 15.5 %collective-permute-start.19 = (bf16[128,2048]{1,0:T(8,128)(2,1)}, bf16[128,2048]{1,0:T(8,128)(2,1)S(1)}, u32[]{:S(2)}, u32[]{:S(2)}) collective-permute-start(bf16[128,2048]{1,0:T(8,128)(2,1)} %collective-permute-done.17.refs_4_), channel_id=1, source_target_pairs={{0,56},{4,60},{8,0},{12,4},{16,8},{20,12},{24,16},{28,20},{32,24},... | collective-permute-start | bytes 1572872 | tf_op jit(solution)/shard_map/ppermute | solution.py:52
  98.8 12.7 %collective-permute-start.20 = (bf16[64,2048]{1,0:T(8,128)(2,1)S(1)}, bf16[64,2048]{1,0:T(8,128)(2,1)S(1)}, u32[]{:S(2)}, u32[]{:S(2)}) collective-permute-start(bf16[64,2048]{1,0:T(8,128)(2,1)S(1)} %slice.26), channel_id=1, source_target_pairs={{0,8},{4,12},{8,16},{12,20},{16,24},{20,28},{24,32},{28,36},{32,40... | collective-permute-start | bytes 786440 | tf_op jit(solution)/shard_map/ppermute | solution.py:52
  98.9 12.6 %collective-permute-start.21 = (bf16[64,2048]{1,0:T(8,128)(2,1)S(1)}, bf16[64,2048]{1,0:T(8,128)(2,1)S(1)}, u32[]{:S(2)}, u32[]{:S(2)}) collective-permute-start(bf16[64,2048]{1,0:T(8,128)(2,1)S(1)} %slice.27), channel_id=1, source_target_pairs={{0,56},{4,60},{8,0},{12,4},{16,8},{20,12},{24,16},{28,20},{32,24},... | collective-permute-start | bytes 786440 | tf_op jit(solution)/shard_map/ppermute | solution.py:52
  133.5 42.2 %collective-permute-start.26 = (bf16[256,2304]{1,0:T(8,128)(2,1)}, bf16[256,2304]{1,0:T(8,128)(2,1)}, u32[]{:S(2)}, u32[]{:S(2)}) collective-permute-start(bf16[256,2304]{1,0:T(8,128)(2,1)} %get-tuple-element.46), channel_id=1, source_target_pairs={{0,1},{1,2},{2,3},{3,0},{4,5},{5,6},{6,7},{7,4},{8,9},{9,10},{10,1... | collective-permute-start | bytes 3538952 | tf_op jit(solution)/shard_map/ppermute | solution.py:60
  134.8 40.9 %collective-permute-start.27 = (bf16[256,2304]{1,0:T(8,128)(2,1)}, bf16[256,2304]{1,0:T(8,128)(2,1)}, u32[]{:S(2)}, u32[]{:S(2)}) collective-permute-start(bf16[256,2304]{1,0:T(8,128)(2,1)} %get-tuple-element.47), channel_id=1, source_target_pairs={{0,3},{1,0},{2,1},{3,2},{4,7},{5,4},{6,5},{7,6},{8,11},{9,8},{10,9... | collective-permute-start | bytes 3538952 | tf_op jit(solution)/shard_map/ppermute | solution.py:60
  162.8 69.5 %all-to-all-start = ((bf16[64,8,2176]{2,1,0:T(8,128)(2,1)}), bf16[64,8,2176]{2,1,0:T(8,128)(2,1)S(1)}, u32[]{:S(2)}, u32[]{:S(2)}) async-start(bf16[64,8,2176]{2,1,0:T(8,128)(2,1)} %slots.1._), calls=%async_computation | async-start | bytes 4456448 | tf_op jit(solution)/shard_map/all_to_all | solution.py:574
  172.8 28.5 %collective-permute-start.25 = (bf16[256,2304]{1,0:T(8,128)(2,1)S(1)}, bf16[256,2304]{1,0:T(8,128)(2,1)}, u32[]{:S(2)}, u32[]{:S(2)}) collective-permute-start(bf16[256,2304]{1,0:T(8,128)(2,1)S(1)} %copy-done.3), channel_id=1, source_target_pairs={{0,1},{1,2},{2,3},{3,0},{4,5},{5,6},{6,7},{7,4},{8,9},{9,10},{10,1... | collective-permute-start | bytes 3538952 | tf_op jit(solution)/shard_map/ppermute | solution.py:60
  172.9 27.5 %collective-permute-start.24 = (bf16[256,2304]{1,0:T(8,128)(2,1)}, bf16[256,2304]{1,0:T(8,128)(2,1)}, u32[]{:S(2)}, u32[]{:S(2)}) collective-permute-start(bf16[256,2304]{1,0:T(8,128)(2,1)} %get-tuple-element.45), channel_id=1, source_target_pairs={{0,3},{1,0},{2,1},{3,2},{4,7},{5,4},{6,5},{7,6},{8,11},{9,8},{10,9... | collective-permute-start | bytes 3538952 | tf_op jit(solution)/shard_map/ppermute | solution.py:60
  180.2 46.4 %collective-permute-start.28 = (bf16[256,2304]{1,0:T(8,128)(2,1)}, bf16[256,2304]{1,0:T(8,128)(2,1)}, u32[]{:S(2)}, u32[]{:S(2)}) collective-permute-start(bf16[256,2304]{1,0:T(8,128)(2,1)} %get-tuple-element.48), channel_id=1, source_target_pairs={{0,1},{1,2},{2,3},{3,0},{4,5},{5,6},{6,7},{7,4},{8,9},{9,10},{10,1... | collective-permute-start | bytes 3538952 | tf_op jit(solution)/shard_map/ppermute | solution.py:60
  180.2 46.4 %collective-permute-start.29 = (bf16[256,2304]{1,0:T(8,128)(2,1)}, bf16[256,2304]{1,0:T(8,128)(2,1)}, u32[]{:S(2)}, u32[]{:S(2)}) collective-permute-start(bf16[256,2304]{1,0:T(8,128)(2,1)} %get-tuple-element.49), channel_id=1, source_target_pairs={{0,3},{1,0},{2,1},{3,2},{4,7},{5,4},{6,5},{7,6},{8,11},{9,8},{10,9... | collective-permute-start | bytes 3538952 | tf_op jit(solution)/shard_map/ppermute | solution.py:60
  (30 other events, 222.3 us)
where the time goes:
time: 236 us; the launch traced here: 235 us
  waiting for transfers between devices  89.2 us (38%)
  Pallas kernels  72.8 us (31%)
  starting transfers between devices  58.5 us (25%)
  local copies, waits for them, and re-layouts  10 us (4%)
    ppermute x22, waiting for transfers between devices, shift(): return lax.ppermute(arr, 'ep', pairs)  43.6 us
    ppermute x6, waiting for transfers between devices, shift_dp(): return lax.ppermute(arr, 'dp', [(i, (i + by) % NDP) for i in range(NDP)])  43.1 us
    ppermute x22, starting transfers between devices, shift(): return lax.ppermute(arr, 'ep', pairs)  32.5 us
    pallas_call x1, Pallas kernels, slots(): pl.pallas_call(slots_kernel, out_shape=jax.ShapeDtypeStruct((NY * NZ * NC...  15.9 us
    pallas_call x1, Pallas kernels, mid(): pl.pallas_call(mid_kernel, out_shape=(jax.ShapeDtypeStruct((PIECE, 3 * FF...  11.7 us
    pallas_call x1, Pallas kernels, rest(): pl.pallas_call(rest_kernel, out_shape=(jax.ShapeDtypeStruct(size, bf16),...  10.7 us
    all_to_all x1, starting transfers between devices, body(): got = lax.all_to_all(out, 'ep', split_axis=0, concat_axis=0, tiled=True)  9.98 us
    pallas_call x1, Pallas kernels, front(): pl.pallas_call(front_kernel, grid=(NFB,), out_shape=(jax.ShapeDtypeStruct...  8.8 us
  transfers between devices with their start and end apart: 31, of which 13 were waited for; matrix products, arithmetic and copies ran while one was open for 1% of the time, Pallas kernels for 23%

commit v1 on v0

--- a/solution.py
+++ b/solution.py
@@ -66,6 +66,23 @@
     for ref in refs[:count]:
         out_ref[at : at + ref.shape[0], :] = ref[...]
         at += ref.shape[0]
+
+
+def halves_kernel(a_ref, b_ref, *refs):
+    n = a_ref.shape[0] // 2
+    refs[-2][...] = a_ref[:n]
+    refs[-1][...] = b_ref[n:]
+
+
+def halves(a, b, after):
+    half = jax.ShapeDtypeStruct((a.shape[0] // 2, a.shape[1]), a.dtype)
+    return pl.pallas_call(
+        halves_kernel,
+        out_shape=(half, half),
+        in_specs=[VM, VM] + [pl.BlockSpec(memory_space=pl.ANY)] * len(after),
+        out_specs=(VM, VM),
+        name="halves",
+    )(a, b, *after)
 
 
 def join(parts, after=()):
@@ -202,7 +219,7 @@
         out_specs=(VM, VM),
         scratch_shapes=[pltpu.VMEM((HALF, D), f32), pltpu.VMEM((HALF, D), f32)],
         compiler_params=pltpu.CompilerParams(vmem_limit_bytes=VLIM),
-        cost_estimate=cost(20_000_000_000),
+        cost_estimate=cost(PICK_COST),
         name="pick_cot",
     )(code, *blocks, after)
 
@@ -260,28 +277,42 @@
         ),
         scratch_shapes=[pltpu.VMEM((ROWS, D), bf16)],
         compiler_params=pltpu.CompilerParams(vmem_limit_bytes=VLIM),
-        cost_estimate=cost(1_000_000_000),
+        cost_estimate=cost(FRONT_COST),
         name="front",
     )(me, own, sib, wg, wu)
 
 
-def piece_into(out_ref, x_own, x_sib, gg_ref, gu_ref, hid_t_ref, scot_cols):
-    for n, ref in enumerate((gg_ref, gu_ref)):
-        value = dot(x_own, ref[:HALF], contract_first) + dot(x_sib, ref[HALF:], contract_first)
-        out_ref[:, n * FF : (n + 1) * FF] = value.astype(bf16)
+def whole(shape):
+    return pl.BlockSpec(shape, lambda *_: (0,) * len(shape))
+
+
+def place(pos_ref, piece):
+    return (2 * pos_ref[1] + piece) % (2 * NDP)
+
+
+def scale(weight_ref, own, sib):
+    weight = weight_ref[:, :1]
+    cot = jnp.concatenate([own, sib], axis=0)
+    return (weight * cot.astype(f32)).astype(bf16)
+
+
+def piece_into(out_ref, x_own, x_sib, g_ref, hid_t_ref, scot_cols):
+    def side(n, _):
+        value = dot(x_own, g_ref[n, :HALF], contract_first)
+        value = value + dot(x_sib, g_ref[n, HALF:], contract_first)
+        out_ref[:, pl.ds(pl.multiple_of(n * FF, FF), FF)] = value.astype(out_ref.dtype)
+        return 0
+
+    lax.fori_loop(0, 2, side, 0)
     for q in range(NFB):
         value = dot(hid_t_ref[q * FB : (q + 1) * FB], scot_cols)
-        out_ref[:, 2 * FF + q * FB : 2 * FF + (q + 1) * FB] = value.astype(bf16)
-
-
-def place(pos_ref, piece):
-    return (2 * pos_ref[1] + piece) % (2 * NDP)
+        out_ref[:, 2 * FF + q * FB : 2 * FF + (q + 1) * FB] = value.astype(out_ref.dtype)
 
 
 def mid_kernel(
     pos_ref, own_ref, sib_ref, hid_ref, hid_t_ref, a_ref, b_ref, weight_ref,
     xoa_ref, xsa_ref, xob_ref, xsb_ref, wd_ref,
-    pa_ref, pb_ref, gg_ref, gu_ref, route_ref, scot_ref, cot_scr, x_scr, out_scr,
+    pa_ref, pb_ref, g_ref, route_ref, cot_scr, x_scr, out_scr,
 ):
     j = pl.program_id(0)
 
@@ -289,8 +320,6 @@
     def _():
         cot_scr[:HALF] = own_ref[...]
         cot_scr[HALF:] = sib_ref[...]
-        weight = weight_ref[:, :1]
-        scot_ref[...] = (weight * cot_scr[...].astype(f32)).astype(bf16)
         route_ref[...] = jnp.zeros_like(route_ref)
         for n, ref in enumerate((xoa_ref, xsa_ref, xob_ref, xsb_ref)):
             x_scr[n] = ref[...]
@@ -300,26 +329,22 @@
     route_ref[...] += jnp.broadcast_to(part, (ROWS, META))
     scaled = weight_ref[:, :1] * back
     cols = pl.ds(pl.multiple_of(j * FB, FB), FB)
-    gg_ref[:, cols] = (scaled * a_ref[...]).astype(bf16)
-    gu_ref[:, cols] = (scaled * b_ref[...]).astype(bf16)
+    g_ref[0, :, cols] = (scaled * a_ref[...]).astype(bf16)
+    g_ref[1, :, cols] = (scaled * b_ref[...]).astype(bf16)
 
     @pl.when(j == NFB - 1)
     def _():
         def step(n, _):
             some = pl.ds(pl.multiple_of(place(pos_ref, 4 + n) * PIECE, PIECE), PIECE)
             piece_into(
-                out_scr.at[n], x_scr[2 * n], x_scr[2 * n + 1], gg_ref, gu_ref, hid_t_ref,
-                scot_ref[:, some],
+                out_scr.at[n], x_scr[2 * n], x_scr[2 * n + 1], g_ref, hid_t_ref,
+                scale(weight_ref, own_ref[:, some], sib_ref[:, some]),
             )
             return 0
 
         lax.fori_loop(0, 2, step, 0)
         pa_ref[...] = out_scr[0]
         pb_ref[...] = out_scr[1]
-
-
-def whole(shape):
-    return pl.BlockSpec(shape, lambda *_: (0,) * len(shape))
 
 
 def mid(pos, own, sib, hid, hid_t, a, b, weight, x_own, x_sib, wd):
@@ -331,10 +356,8 @@
         out_shape=(
             jax.ShapeDtypeStruct((PIECE, 3 * FF), bf16),
             jax.ShapeDtypeStruct((PIECE, 3 * FF), bf16),
-            jax.ShapeDtypeStruct((ROWS, FF), bf16),
-            jax.ShapeDtypeStruct((ROWS, FF), bf16),
+            jax.ShapeDtypeStruct((2, ROWS, FF), bf16),
             jax.ShapeDtypeStruct((ROWS, META), f32),
-            jax.ShapeDtypeStruct((ROWS, D), bf16),
         ),
         grid_spec=pltpu.PrefetchScalarGridSpec(
             num_scalar_prefetch=1,
@@ -345,8 +368,8 @@
                 pl.BlockSpec((FB, D), lambda j, pos_ref: (j, 0)),
             ],
             out_specs=(
-                whole((PIECE, 3 * FF)), whole((PIECE, 3 * FF)), whole((ROWS, FF)),
-                whole((ROWS, FF)), whole((ROWS, META)), whole((ROWS, D)),
+                whole((PIECE, 3 * FF)), whole((PIECE, 3 * FF)), whole((2, ROWS, FF)),
+                whole((ROWS, META)),
             ),
             scratch_shapes=[
                 pltpu.VMEM((ROWS, D), bf16),
@@ -359,52 +382,48 @@
     )(pos, own, sib, hid, hid_t, a, b, weight, x_own, x_sib, x_own, x_sib, wd)
 
 
-def rest_piece(n):
-    first = jnp.where(n == 0, 3, 6)
-    second = jnp.where(n == 2, 2, 7)
-    return jnp.where(n < 2, first, jnp.where(n < 4, second, n - 4))
-
-
-def rest_kernel(
-    pos_ref, x_own_ref, x_sib_ref, scot_ref, gg_ref, gu_ref, hid_t_ref,
-    pa_ref, pb_ref, more_ref, out_scr,
+def pick_pieces(*which):
+    def index(n, pos_ref):
+        piece = which[0]
+        for i in range(1, len(which)):
+            piece = jnp.where(n == i, which[i], piece)
+        return (0, place(pos_ref, piece))
+
+    half = pl.BlockSpec((HALF, PIECE), index)
+    return [half] * 4 + [whole((ROWS, META)), whole((2, ROWS, FF)), whole((FF, ROWS))]
+
+
+def plain_kernel(
+    pos_ref, xo, xs, co, cs, weight_ref, g_ref, hid_t_ref, a_ref, b_ref, own_ref, scr
 ):
-    n = pl.program_id(0)
-    piece_into(
-        out_scr, x_own_ref[...], x_sib_ref[...], gg_ref, gu_ref, hid_t_ref, scot_ref[...]
-    )
-
-    @pl.when(n == 0)
+    piece_into(scr, xo[...], xs[...], g_ref, hid_t_ref, scale(weight_ref, co[...], cs[...]))
+
+    @pl.when(pl.program_id(0) == 0)
     def _():
-        pa_ref[...] = out_scr[...]
-
-    @pl.when(n == 1)
+        a_ref[...] = scr[...]
+
+    @pl.when(pl.program_id(0) == 1)
     def _():
-        pb_ref[...] = out_scr[...]
-
-    @pl.when(n > 1)
+        b_ref[...] = scr[...]
+
+    @pl.when(pl.program_id(0) > 1)
     def _():
-        more_ref[...] = out_scr[...]
-
-
-def rest(pos, x_own, x_sib, scot, gg, gu, hid_t):
+        own_ref[...] = scr[...]
+
+
+def plain(pos, *args):
     size = (PIECE, 3 * FF)
-    x_spec = pl.BlockSpec((HALF, PIECE), lambda n, pos_ref: (0, place(pos_ref, rest_piece(n))))
-    return pl.pallas_call(
-        rest_kernel,
+    return pl.pallas_call(
+        plain_kernel,
         out_shape=(
             jax.ShapeDtypeStruct(size, bf16),
             jax.ShapeDtypeStruct(size, bf16),
-            jax.ShapeDtypeStruct((4 * PIECE, 3 * FF), bf16),
+            jax.ShapeDtypeStruct((2 * PIECE, 3 * FF), bf16),
         ),
         grid_spec=pltpu.PrefetchScalarGridSpec(
             num_scalar_prefetch=1,
-            grid=(6,),
-            in_specs=[
-                x_spec, x_spec,
-                pl.BlockSpec((ROWS, PIECE), lambda n, pos_ref: (0, place(pos_ref, rest_piece(n)))),
-                whole((ROWS, FF)), whole((ROWS, FF)), whole((FF, ROWS)),
-            ],
+            grid=(4,),
+            in_specs=pick_pieces(3, 6, 0, 1),
             out_specs=(
                 whole(size), whole(size),
                 pl.BlockSpec(size, lambda n, pos_ref: (jnp.maximum(n - 2, 0), 0)),
@@ -412,113 +431,153 @@
             scratch_shapes=[pltpu.VMEM(size, bf16)],
         ),
         compiler_params=pltpu.CompilerParams(vmem_limit_bytes=VLIM),
-        name="rest",
-    )(pos, x_own, x_sib, scot, gg, gu, hid_t)
-
-
-def add_kernel(more_ref, ra_ref, rb_ref, _, oa_ref, ob_ref):
-    for n, (r_ref, o_ref) in enumerate(((ra_ref, oa_ref), (rb_ref, ob_ref))):
-        value = more_ref[n * PIECE : (n + 1) * PIECE].astype(f32) + r_ref[...].astype(f32)
-        o_ref[...] = value.astype(bf16)
-
-
-def add(more, ra, rb, after):
+        name="plain",
+    )(pos, *args)
+
+
+def added_kernel(
+    pos_ref, xo, xs, co, cs, weight_ref, g_ref, hid_t_ref, ra_ref, rb_ref,
+    a_ref, ad_ref, b_ref, bd_ref, scr,
+):
+    piece_into(
+        scr, xo[...], xs[...], g_ref, hid_t_ref, scale(weight_ref, co[...], cs[...])
+    )
+    for n, (r_ref, o_ref, d_ref) in enumerate(((ra_ref, a_ref, ad_ref), (rb_ref, b_ref, bd_ref))):
+
+        @pl.when(pl.program_id(0) == n)
+        def _():
+            o_ref[...] = (scr[:, : 2 * FF] + r_ref[:, : 2 * FF].astype(f32)).astype(bf16)
+            d_ref[...] = (scr[:, 2 * FF :] + r_ref[:, 2 * FF :].astype(f32)).astype(bf16)
+
+
+def added(pos, *args):
     size = (PIECE, 3 * FF)
-    thin = pl.BlockSpec((PIECE, FF), lambda j: (0, j))
-    return pl.pallas_call(
-        add_kernel,
-        grid=(3,),
-        out_shape=(jax.ShapeDtypeStruct(size, bf16), jax.ShapeDtypeStruct(size, bf16)),
-        in_specs=[
-            pl.BlockSpec((2 * PIECE, FF), lambda j: (0, j)), thin, thin,
-            pl.BlockSpec(memory_space=pl.ANY),
-        ],
-        out_specs=(thin, thin),
-        name="add",
-    )(more, ra, rb, after)
-
-
-def final_kernel(more_ref, r2a, r2b, r3a, r3b, gate_ref, up_ref, down_ref):
-    j = pl.program_id(0)
-    for n, refs in enumerate(((r2a, r3a), (r2b, r3b))):
-        side = slice(n * PIECE, (n + 1) * PIECE)
-        value = more_ref[side].astype(f32)
-        for ref in refs:
-            value = value + ref[...].astype(f32)
-        value = value.astype(bf16)
-
-        @pl.when(j == 0)
+    sizes = ((PIECE, 2 * FF), (PIECE, FF)) * 2
+    return pl.pallas_call(
+        added_kernel,
+        out_shape=tuple(jax.ShapeDtypeStruct(shape, bf16) for shape in sizes),
+        grid_spec=pltpu.PrefetchScalarGridSpec(
+            num_scalar_prefetch=1,
+            grid=(2,),
+            in_specs=pick_pieces(2, 7) + [whole(size)] * 2,
+            out_specs=tuple(whole(shape) for shape in sizes),
+            scratch_shapes=[pltpu.VMEM(size, f32)],
+        ),
+        compiler_params=pltpu.CompilerParams(vmem_limit_bytes=VLIM),
+        name="added",
+    )(pos, *args)
+
+
+def chunk_kernel(own_ref, r2a, r2b, r3a, r3b, gate_ref, up_ref, down_ref):
+    for n, (r2, r3) in enumerate(((r2a, r3a), (r2b, r3b))):
+
+        @pl.when(pl.program_id(0) == n)
         def _():
-            gate_ref[0, side, :] = value
-
-        @pl.when(j == 1)
-        def _():
-            up_ref[0, side, :] = value
-
-        @pl.when(j == 2)
-        def _():
-            for q in range(NFB):
-                down_ref[0, q * FB : (q + 1) * FB, side] = value[:, q * FB : (q + 1) * FB]
-
-
-def final(more, *arrived):
+            def rows(i, _):
+                some = pl.ds(pl.multiple_of(i * 64, 64), 64)
+                to = pl.ds(pl.multiple_of(n * PIECE + i * 64, 64), 64)
+                for k, ref in enumerate((gate_ref, up_ref)):
+                    cols = slice(k * FF, (k + 1) * FF)
+                    value = own_ref[some, cols].astype(f32) + r2[some, cols].astype(f32)
+                    ref[0, to, :] = (value + r3[some, cols].astype(f32)).astype(bf16)
+                cols = slice(2 * FF, 3 * FF)
+                down_ref[to, :] = own_ref[some, cols].astype(f32) + r2[some, cols].astype(f32)
+                return 0
+
+            lax.fori_loop(0, PIECE // 64, rows, 0)
+
+
+def chunk(own, *arrived):
+    size = (PIECE, 3 * FF)
     per = D // NDP
-    thin = pl.BlockSpec((PIECE, FF), lambda j: (0, j))
-    return pl.pallas_call(
-        final_kernel,
-        grid=(3,),
+    return pl.pallas_call(
+        chunk_kernel,
+        grid=(2,),
         out_shape=(
             jax.ShapeDtypeStruct((1, per, FF), bf16),
             jax.ShapeDtypeStruct((1, per, FF), bf16),
-            jax.ShapeDtypeStruct((1, FF, per), bf16),
-        ),
-        in_specs=[pl.BlockSpec((2 * PIECE, FF), lambda j: (1, j))] + [thin] * 4,
-        out_specs=(whole((1, per, FF)), whole((1, per, FF)), whole((1, FF, per))),
-        compiler_params=pltpu.CompilerParams(vmem_limit_bytes=VLIM),
-        cost_estimate=cost(30_000_000_000),
-        name="final",
-    )(more, *arrived)
-
-
-def slots_kernel(me_ref, gg_ref, gu_ref, route_ref, wg_ref, wu_ref, _, out_ref, scr):
-    me = me_ref[0]
+            jax.ShapeDtypeStruct((per, FF), f32),
+        ),
+        in_specs=[pl.BlockSpec(size, lambda n: (n, 0))]
+        + [whole(size)] * 2 + [whole((PIECE, 2 * FF))] * 2,
+        out_specs=(whole((1, per, FF)), whole((1, per, FF)), whole((per, FF))),
+        compiler_params=pltpu.CompilerParams(vmem_limit_bytes=VLIM),
+        name="chunk",
+    )(own, *arrived)
+
+
+def tail_kernel(sum_ref, ra_ref, rb_ref, out_ref):
+    for n, ref in enumerate((ra_ref, rb_ref)):
+        side = slice(n * PIECE, (n + 1) * PIECE)
+        for q in range(NFB):
+            cols = slice(q * FB, (q + 1) * FB)
+            out_ref[0, cols, side] = (sum_ref[side, cols] + ref[:, cols].astype(f32)).astype(bf16)
+
+
+def tail(partial, ra, rb):
+    return pl.pallas_call(
+        tail_kernel,
+        out_shape=jax.ShapeDtypeStruct((1, FF, D // NDP), bf16),
+        in_specs=[VM] * 3,
+        out_specs=VM,
+        compiler_params=pltpu.CompilerParams(vmem_limit_bytes=VLIM),
+        cost_estimate=cost(TAIL_COST),
+        name="tail",
+    )(partial, ra, rb)
+
+
+def slots_kernel(pos_ref, g_ref, route_ref, wg_ref, wu_ref, out_ref):
+    me = pos_ref[0]
+    j = pl.program_id(0)
     core = me % NC
     z = (me // NC) % NZ
     y = me // (NC * NZ)
-    quarter = ROWS // 4
-
-    def part(i, _):
-        rows = pl.ds(pl.multiple_of(i * quarter, quarter), quarter)
-        scr[rows] = dot(gg_ref[rows], wg_ref[...], contract_last) + dot(
-            gu_ref[rows], wu_ref[...], contract_last
-        )
-        return 0
-
-    lax.fori_loop(0, 4, part, 0)
-
-    def put(i, _):
-        h, b, s = i // (NY * NZ), (i // NZ) % NY, i % NZ
-        dy = jnp.where(b == 1, NY - 1, jnp.where(b == 2, 1, b - b // 3))
-        dz = jnp.where(s % 2 == 1, NZ - (s + 1) // 2, s // 2)
-        to = (((y + dy) % NY) * NZ + (z + dz) % NZ) * NC + (core + h) % NC
-        rows = pl.ds(pl.multiple_of(i * CAP, CAP), CAP)
-        out_ref[to, :, :D] = scr[rows, :].astype(bf16)
-        out_ref[to, :, D:] = route_ref[rows, :].astype(bf16)
-        return 0
-
-    lax.fori_loop(0, 2 * NY * NZ, put, 0)
-
-
-def slots(me, gg, gu, route, wg, wu, after):
+    part = dot(g_ref[0], wg_ref[...], contract_last)
+    part = part + dot(g_ref[1], wu_ref[...], contract_last)
+    cols = pl.ds(pl.multiple_of(j * WIDE, WIDE), WIDE)
+    for h in range(2):
+        for b in range(NY):
+            for s in range(NZ):
+                src = ((y + DY[b] + NY) % NY) * NZ + (z + DZ[s] + NZ) % NZ
+                to = src * NC + (core + h) % NC
+                at = h * HALF + b * 64 + s * CAP
+                out_ref[to, :, cols] = part[at : at + CAP].astype(bf16)
+
+    @pl.when(j == 0)
+    def _():
+        def put(i, _):
+            h, b, s = i // (NY * NZ), (i // NZ) % NY, i % NZ
+            dy = jnp.where(b == 1, NY - 1, jnp.where(b == 2, 1, b - b // 3))
+            dz = jnp.where(s % 2 == 1, NZ - (s + 1) // 2, s // 2)
+            to = (((y + dy) % NY) * NZ + (z + dz) % NZ) * NC + (core + h) % NC
+            rows = pl.ds(pl.multiple_of(i * CAP, CAP), CAP)
+            out_ref[to, :, D:] = route_ref[rows, :].astype(bf16)
+            return 0
+
+        lax.fori_loop(0, 2 * NY * NZ, put, 0)
+
+
+WIDE = 512
+TAIL_COST = 30_000_000_000
+PICK_COST = 0
+FRONT_COST = 5_000_000_000
+
+
+def slots(pos, g, route, wg, wu):
+    size = (NY * NZ * NC, CAP, DA)
     return pl.pallas_call(
         slots_kernel,
-        out_shape=jax.ShapeDtypeStruct((NY * NZ * NC, CAP, DA), bf16),
-        in_specs=[SM] + [VM] * 5 + [pl.BlockSpec(memory_space=pl.ANY)],
-        out_specs=VM,
-        scratch_shapes=[pltpu.VMEM((ROWS, D), f32)],
+        grid=(D // WIDE,),
+        out_shape=jax.ShapeDtypeStruct(size, bf16),
+        in_specs=[
+            SM, whole((2, ROWS, FF)), whole((ROWS, META)),
+            pl.BlockSpec((WIDE, FF), lambda j: (j, 0)),
+            pl.BlockSpec((WIDE, FF), lambda j: (j, 0)),
+        ],
+        out_specs=whole(size),
         compiler_params=pltpu.CompilerParams(vmem_limit_bytes=VLIM),
         name="slots",
-    )(me, gg, gu, route, wg, wu, after)
+    )(pos, g, route, wg, wu)
 
 
 def body(tokens, cotangent, expert_ids, route_weights, w_gate, w_up, w_down):
@@ -539,21 +598,22 @@
         d.append(shift(d[-1], dz=-1))
     u.append(shift(u[-1], dz=1))
 
-    def ring_y(part):
-        p1 = shift(part, dy=1)
-        m1 = shift(part, dy=-1)
-        n = part.shape[0] // 2
-        return part, p1, m1, shift(p1[:n], dy=1), shift(m1[n:], dy=-1)
-
-    blocks = ring_y(join([xa, u[1], d[1], u[2], d[2], u[3], d[3], u[4]], after=[c2, c3]))
-    cot0 = join([cotangent, c1, c2, c3], after=[u[3], d[3]])
+    x0 = join([xa, u[1], d[1], u[2], d[2], u[3], d[3], u[4]], after=[c2, c3])
+    p1 = shift(x0, dy=1)
+    m1 = shift(x0, dy=-1)
+
+    cot0 = join([cotangent, c1, c2, c3], after=[x0])
     cu = [cot0]
     cd = [cot0]
     for _ in range(3):
         cu.append(shift(cu[-1], dz=1))
         cd.append(shift(cd[-1], dz=-1))
-    n = NY * TOK // 2
-    cq = [shift(cu[-1][:n], dz=1), shift(cd[-1][n:], dz=-1)]
+
+    qa, qb = halves(p1, m1, after=[])
+    blocks = x0, p1, m1, shift(qa, dy=1), shift(qb, dy=-1)
+
+    qa, qb = halves(cu[-1], cd[-1], after=[])
+    cq = [shift(qa, dz=1), shift(qb, dz=-1)]
 
     own_x, sib_x, code = pick_x(pos, blocks)
     sib_x = swap_core(sib_x)
@@ -561,20 +621,23 @@
     hid, hid_t, a, b, weight = front(pos, own_x, sib_x, wg, wu)
 
     parts = [cot0, cu[1], cd[1], cu[2], cd[2], cu[3], cd[3], *cq]
-    own_c, sib_c = pick_cot(code, parts, after=hid)
+    own_c, sib_c = pick_cot(code, parts, after=code)
     sib_c = swap_core(sib_c)
 
-    p2a, p2b, gg, gu, route, scot = mid(
+    p2a, p2b, g, route = mid(
         pos, own_c, sib_c, hid, hid_t, a, b, weight, own_x, sib_x, wd
     )
     r1a, r1b = shift_dp(p2a, 1), shift_dp(p2b, -1)
-    p1b, p3a, more = rest(pos, own_x, sib_x, scot, gg, gu, hid_t)
+    out = slots(pos, g, route, wg, wu)
+    got = lax.all_to_all(out, "ep", split_axis=0, concat_axis=0, tiled=True)
+    args = (own_x, sib_x, own_c, sib_c, weight, g, hid_t)
+    p1b, p3a, own = plain(pos, *args)
     r2b, r2a = shift_dp(p1b, 1), shift_dp(p3a, -1)
-    out = slots(pos, gg, gu, route, wg, wu, after=p1b)
-    got = lax.all_to_all(out, "ep", split_axis=0, concat_axis=0, tiled=True)
-    p1a, p3b = add(more, r1a, r1b, after=out)
+    p1a, p1a_down, p3b, p3b_down = added(pos, *args, r1a, r1b)
     r3a, r3b = shift_dp(p1a, 1), shift_dp(p3b, -1)
-    grad_gate, grad_up, grad_down = final(more, r2a, r2b, r3a, r3b)
+    r3a_down, r3b_down = shift_dp(p1a_down, 1), shift_dp(p3b_down, -1)
+    grad_gate, grad_up, partial = chunk(own, r2a, r2b, r3a, r3b)
+    grad_down = tail(partial, r3a_down, r3b_down)
 
     experts = NY * NZ * NC
     one = (expert_ids[:, :, None] == jnp.arange(experts, dtype=i32)).astype(i32)

time: 236 us -> 223 us (0.945)
  waiting for transfers between devices: 89.2 us -> 68.6 us
  local copies, waits for them, and re-layouts: 10 us -> 14.9 us
  Pallas kernels: 72.8 us -> 76.8 us
    ppermute x6 -> x8, waiting for transfers between devices: 43.1 us -> 32.9 us  [shift_dp(): return lax.ppermute(arr, 'dp', [(i, (i + by) % NDP) for i in range(NDP)])]
    ppermute x22, waiting for transfers between devices: 43.6 us -> 35.6 us  [shift(): return lax.ppermute(arr, 'ep', pairs)]
    unnamed x50 -> x58, local copies, waits for them, and re-layouts: 6.84 us -> 13.6 us
    pallas_call x4 -> x7, Pallas kernels: 36.9 us -> 41 us  [the longest x1 10.6 us: slots(): pl.pallas_call(slots_kernel, grid=(D // WIDE,), out_shape=jax.ShapeDtypeS...]
    ppermute x2, waiting for transfers between devices: 2.5 us -> 0.01 us  [swap_core(): return lax.ppermute(arr, 'ep', [(i, i ^ 1) for i in range(NY * NZ * NC)])]
    ppermute x6 -> x8, starting transfers between devices: 8.19 us -> 9.82 us  [shift_dp(): return lax.ppermute(arr, 'dp', [(i, (i + by) % NDP) for i in range(NDP)])]
  transfers between devices with their start and end apart: 31 -> 33, of which waited for: 13 -> 13; matrix products, arithmetic and copies ran while one was open for 1% -> 1% of each run, Pallas kernels for 23% -> 28%
where the time goes in v1:
time: 223 us; the launch traced here: 222 us
  Pallas kernels  76.8 us (34%)
  waiting for transfers between devices  68.6 us (31%)
  starting transfers between devices  57.8 us (26%)
  local copies, waits for them, and re-layouts  14.9 us (7%)
    ppermute x22, waiting for transfers between devices, shift(): return lax.ppermute(arr, 'ep', pairs)  35.6 us
    ppermute x8, waiting for transfers between devices, shift_dp(): return lax.ppermute(arr, 'dp', [(i, (i + by) % NDP) for i in range(NDP)])  32.9 us
    ppermute x22, starting transfers between devices, shift(): return lax.ppermute(arr, 'ep', pairs)  32 us
    unnamed x58, local copies, waits for them, and re-layouts  13.6 us
    pallas_call x1, Pallas kernels, mid(): pl.pallas_call(mid_kernel, out_shape=(jax.ShapeDtypeStruct((PIECE, 3 * FF...  11.6 us
    pallas_call x1, Pallas kernels, slots(): pl.pallas_call(slots_kernel, grid=(D // WIDE,), out_shape=jax.ShapeDtypeS...  10.6 us
    pallas_call x1, Pallas kernels, plain(): pl.pallas_call(plain_kernel, out_shape=(jax.ShapeDtypeStruct(size, bf16),...  10.4 us
    ppermute x8, starting transfers between devices, shift_dp(): return lax.ppermute(arr, 'dp', [(i, (i + by) % NDP) for i in range(NDP)])  9.82 us
  transfers between devices with their start and end apart: 33, of which 13 were waited for; matrix products, arithmetic and copies ran while one was open for 1% of the time, Pallas kernels for 28%

profile of v1, /device:TPU:1, one launch (start us, length us, event | category | flops | bytes accessed | tf_op | source)
XLA Modules:
  0.0 222.1 jit_solution(12252398457070183715)
XLA Ops:
  5.7 4.0 %collective-permute-start.1 = (bf16[32,2176]{1,0:T(8,128)(2,1)S(1)}, bf16[32,2176]{1,0:T(8,128)(2,1)S(1)}, u32[]{:S(2)}, u32[]{:S(2)}) collective-permute-start(bf16[32,2176]{1,0:T(8,128)(2,1)S(1)} %concatenate.3.refs_0_), channel_id=1, source_target_pairs={{0,56},{4,60},{8,0},{12,4},{16,8},{20,12},{24,16},{28,20},{32,24},... | collective-permute-start | bytes 417800 | tf_op jit(solution)/shard_map/ppermute | solution.py:52
  9.8 3.3 %collective-permute-done.refs_1_ = bf16[32,2176]{1,0:T(8,128)(2,1)S(1)} collective-permute-done((bf16[32,2176]{1,0:T(8,128)(2,1)S(1)}, bf16[32,2176]{1,0:T(8,128)(2,1)S(1)}, u32[]{:S(2)}, u32[]{:S(2)}) %collective-permute-start) | collective-permute-done | bytes 139296 | tf_op jit(solution)/shard_map/ppermute | solution.py:52
  19.5 2.7 %collective-permute-start.5 = (bf16[32,2176]{1,0:T(8,128)(2,1)S(1)}, bf16[32,2176]{1,0:T(8,128)(2,1)S(1)}, u32[]{:S(2)}, u32[]{:S(2)}) collective-permute-start(bf16[32,2176]{1,0:T(8,128)(2,1)S(1)} %collective-permute-done.3.refs_4_), channel_id=1, source_target_pairs={{0,56},{4,60},{8,0},{12,4},{16,8},{20,12},{24,16},{28,20},{32,24},... | collective-permute-start | bytes 417800 | tf_op jit(solution)/shard_map/ppermute | solution.py:52
  23.3 2.7 %collective-permute-start.7 = (bf16[32,2048]{1,0:T(8,128)(2,1)}, bf16[32,2048]{1,0:T(8,128)(2,1)S(1)}, u32[]{:S(2)}, u32[]{:S(2)}) collective-permute-start(bf16[32,2048]{1,0:T(8,128)(2,1)} %refs_0_.1), channel_id=1, source_target_pairs={{0,192},{4,196},{8,200},{12,204},{16,208},{20,212},{24,216},{28,22... | collective-permute-start | bytes 393224 | tf_op jit(solution)/shard_map/ppermute | solution.py:52
  28.3 3.1 %collective-permute-done.9.refs_9_.refs_3_ = bf16[32,2048]{1,0:T(8,128)(2,1)S(1)} collective-permute-done((bf16[32,2048]{1,0:T(8,128)(2,1)S(1)}, bf16[32,2048]{1,0:T(8,128)(2,1)S(1)}, u32[]{:S(2)}, u32[]{:S(2)}) %collective-permute-start.9) | collective-permute-done | bytes 131104 | tf_op jit(solution)/shard_map/ppermute | solution.py:52
  35.1 2.7 %collective-permute-start.11 = (bf16[256,2176]{1,0:T(8,128)(2,1)}, bf16[256,2176]{1,0:T(8,128)(2,1)S(1)}, u32[]{:S(2)}, u32[]{:S(2)}) collective-permute-start(bf16[256,2176]{1,0:T(8,128)(2,1)} %join.2.refs_0_.refs_4_), channel_id=1, source_target_pairs={{0,192},{4,196},{8,200},{12,204},{16,208},{20,212},{24,216},{28,22... | collective-permute-start | bytes 3342344 | tf_op jit(solution)/shard_map/ppermute | solution.py:52
  42.4 7.1 %collective-permute-done.14.refs_1_ = bf16[128,2048]{1,0:T(8,128)(2,1)S(1)} collective-permute-done((bf16[128,2048]{1,0:T(8,128)(2,1)}, bf16[128,2048]{1,0:T(8,128)(2,1)S(1)}, u32[]{:S(2)}, u32[]{:S(2)}) %collective-permute-start.14) | collective-permute-done | bytes 524320 | tf_op jit(solution)/shard_map/ppermute | solution.py:52
  52.2 5.8 %collective-permute-done.10.a_ref.refs_1_ = bf16[256,2176]{1,0:T(8,128)(2,1)S(1)} collective-permute-done((bf16[256,2176]{1,0:T(8,128)(2,1)}, bf16[256,2176]{1,0:T(8,128)(2,1)S(1)}, u32[]{:S(2)}, u32[]{:S(2)}) %collective-permute-start.10) | collective-permute-done | bytes 1114144 | tf_op jit(solution)/shard_map/ppermute | solution.py:52
  68.5 3.9 %collective-permute-done.12.refs_3_ = bf16[128,2176]{1,0:T(8,128)(2,1)S(1)} collective-permute-done((bf16[128,2176]{1,0:T(8,128)(2,1)}, bf16[128,2176]{1,0:T(8,128)(2,1)S(1)}, u32[]{:S(2)}, u32[]{:S(2)}) %collective-permute-start.12) | collective-permute-done | bytes 557088 | tf_op jit(solution)/shard_map/ppermute | solution.py:52
  74.0 6.3 %pick_x.1 = (bf16[256,2176]{1,0:T(8,128)(2,1)}, bf16[256,2176]{1,0:T(8,128)(2,1)}, bf16[4,256,128]{2,1,0:T(8,128)(2,1)}) custom-call(s32[2]{0:T(128)} %pad_add_fusion.me_ref.pos_ref, bf16[256,2176]{1,0:T(8,128)(2,1)} %join.2.refs_0_.refs_4_, bf16[256,2176]{1,0:T(8,128)(2,1)} %copy-done.2, bf16[256,2176]{1,0:T(8,128)(2,1)} %copy-done.3, ...), custom_call_target="tpu_custom_call" | custom-call | tf_op jit(solution)/shard_map/pick_x/pallas_call | solution.py:165
  80.3 6.7 %collective-permute-start.23 = (bf16[256,2176]{1,0:T(8,128)(2,1)}, bf16[256,2176]{1,0:T(8,128)(2,1)S(1)}, u32[]{:S(2)}, u32[]{:S(2)}) collective-permute-start(bf16[256,2176]{1,0:T(8,128)(2,1)} %get-tuple-element.41), channel_id=1, source_target_pairs={{0,4},{4,0},{8,12},{12,8},{16,20},{20,16},{24,28},{28,24},{32,36},... | collective-permute-start | bytes 3342344 | tf_op jit(solution)/shard_map/ppermute | solution.py:56
  90.6 2.7 %collective-permute-start.21 = (bf16[64,2048]{1,0:T(8,128)(2,1)}, bf16[64,2048]{1,0:T(8,128)(2,1)S(1)}, u32[]{:S(2)}, u32[]{:S(2)}) collective-permute-start(bf16[64,2048]{1,0:T(8,128)(2,1)} %get-tuple-element.37), channel_id=1, source_target_pairs={{0,56},{4,60},{8,0},{12,4},{16,8},{20,12},{24,16},{28,20},{32,24},... | collective-permute-start | bytes 786440 | tf_op jit(solution)/shard_map/ppermute | solution.py:52
  93.3 6.7 %collective-permute-done.20.refs_7_ = bf16[64,2048]{1,0:T(8,128)(2,1)S(1)} collective-permute-done((bf16[64,2048]{1,0:T(8,128)(2,1)}, bf16[64,2048]{1,0:T(8,128)(2,1)S(1)}, u32[]{:S(2)}, u32[]{:S(2)}) %collective-permute-start.20) | collective-permute-done | bytes 262176 | tf_op jit(solution)/shard_map/ppermute | solution.py:52
  100.8 4.9 %pick_cot.1 = (bf16[256,2048]{1,0:T(8,128)(2,1)}, bf16[256,2048]{1,0:T(8,128)(2,1)}) custom-call(bf16[4,256,128]{2,1,0:T(8,128)(2,1)} %get-tuple-element.35.code_ref.refs_9_, bf16[128,2048]{1,0:T(8,128)(2,1)} %join.3.refs_0_, bf16[128,2048]{1,0:T(8,128)(2,1)} %copy-done.11, bf16[128,2048]{1,0:T(8,128)(2,1)} %copy-done.12, ...), custom_call_target="tpu_custom_call" | custom-call | tf_op jit(solution)/shard_map/pick_cot/pallas_call | solution.py:212
  107.4 8.8 %front.1 = (bf16[512,768]{1,0:T(8,128)(2,1)}, bf16[768,512]{1,0:T(8,128)(2,1)}, f32[512,768]{1,0:T(8,128)}, f32[512,768]{1,0:T(8,128)}, f32[512,128]{1,0:T(8,128)}) custom-call(s32[2]{0:T(128)} %pad_add_fusion.me_ref.pos_ref, bf16[256,2176]{1,0:T(8,128)(2,1)} %get-tuple-element.40.own_ref.xoa_ref.xob_ref.xo, bf16[256,2176]{1,0:T(8,128)(2,1)} %copy-done, ...), custom_call_target="tpu_custom_call" | custom-call | flops 5000000000 | tf_op jit(solution)/shard_map/front/pallas_call | solution.py:259
  117.2 11.6 %mid.1 = (bf16[256,2304]{1,0:T(8,128)(2,1)}, bf16[256,2304]{1,0:T(8,128)(2,1)}, bf16[2,512,768]{2,1,0:T(8,128)(2,1)}, f32[512,128]{1,0:T(8,128)}) custom-call(s32[2]{0:T(128)} %pad_add_fusion.me_ref.pos_ref, bf16[256,2048]{1,0:T(8,128)(2,1)} %get-tuple-element.38.own_ref.co, bf16[256,2048]{1,0:T(8,128)(2,1)} %copy-done.1, ...), custom_call_target="tpu_custom_call" | custom-call | tf_op jit(solution)/shard_map/mid/pallas_call | solution.py:354
  131.8 10.4 %plain.1 = (bf16[256,2304]{1,0:T(8,128)(2,1)}, bf16[256,2304]{1,0:T(8,128)(2,1)}, bf16[512,2304]{1,0:T(8,128)(2,1)}) custom-call(s32[2]{0:T(128)} %pad_add_fusion.me_ref.pos_ref, bf16[256,2176]{1,0:T(8,128)(2,1)} %get-tuple-element.40.own_ref.xoa_ref.xob_ref.xo, bf16[256,2176]{1,0:T(8,128)(2,1)} %copy-done, bf16[256,2048]{1,0:T(8,128)(2,1)} %get-tuple-element.38.own_ref.co, ...), custom_call_target="tpu_custom_call" | custom-call | tf_op jit(solution)/shard_map/plain/pallas_call | solution.py:416
  143.5 10.6 %slots.1 = bf16[64,8,2176]{2,1,0:T(8,128)(2,1)} custom-call(s32[2]{0:T(128)} %pad_add_fusion.me_ref.pos_ref, bf16[2,512,768]{2,1,0:T(8,128)(2,1)} %get-tuple-element.47.g_ref, f32[512,128]{1,0:T(8,128)} %get-tuple-element.48.route_ref, bf16[2048,768]{1,0:T(8,128)(2,1)} %bitcast.14, bf16[2048,768]{1,0:T(8,128)(2,1)} %bitcast.16), custom_call_target="tpu_custom_call" | custom-call | tf_op jit(solution)/shard_map/slots/pallas_call | solution.py:568
  154.1 8.5 %all-to-all-start = ((bf16[64,8,2176]{2,1,0:T(8,128)(2,1)}), bf16[64,8,2176]{2,1,0:T(8,128)(2,1)S(1)}, u32[]{:S(2)}, u32[]{:S(2)}) async-start(bf16[64,8,2176]{2,1,0:T(8,128)(2,1)} %slots.1), calls=%async_computation | async-start | bytes 4456448 | tf_op jit(solution)/shard_map/all_to_all | solution.py:632
  163.9 7.9 %added.1 = (bf16[256,1536]{1,0:T(8,128)(2,1)}, bf16[256,768]{1,0:T(8,128)(2,1)}, bf16[256,1536]{1,0:T(8,128)(2,1)}, bf16[256,768]{1,0:T(8,128)(2,1)}) custom-call(s32[2]{0:T(128)} %pad_add_fusion.me_ref.pos_ref, bf16[256,2176]{1,0:T(8,128)(2,1)} %get-tuple-element.40.own_ref.xoa_ref.xob_ref.xo, bf16[256,2176]{1,0:T(8,128)(2,1)} %copy-done, ...), custom_call_target="tpu_custom_call" | custom-call | tf_op jit(solution)/shard_map/added/pallas_call | solution.py:456
  174.8 8.4 %collective-permute-done.24.r2a = bf16[256,2304]{1,0:T(8,128)(2,1)} collective-permute-done((bf16[256,2304]{1,0:T(8,128)(2,1)}, bf16[256,2304]{1,0:T(8,128)(2,1)}, u32[]{:S(2)}, u32[]{:S(2)}) %collective-permute-start.24) | collective-permute-done | bytes 1179680 | tf_op jit(solution)/shard_map/ppermute | solution.py:60
  186.2 5.1 %collective-permute-done.25.r2b = bf16[256,2304]{1,0:T(8,128)(2,1)} collective-permute-done((bf16[256,2304]{1,0:T(8,128)(2,1)}, bf16[256,2304]{1,0:T(8,128)(2,1)}, u32[]{:S(2)}, u32[]{:S(2)}) %collective-permute-start.25) | collective-permute-done | bytes 1179680 | tf_op jit(solution)/shard_map/ppermute | solution.py:60
  191.3 16.7 %collective-permute-done.28.r3a = bf16[256,1536]{1,0:T(8,128)(2,1)S(1)} collective-permute-done((bf16[256,1536]{1,0:T(8,128)(2,1)}, bf16[256,1536]{1,0:T(8,128)(2,1)S(1)}, u32[]{:S(2)}, u32[]{:S(2)}) %collective-permute-start.28) | collective-permute-done | bytes 786464 | tf_op jit(solution)/shard_map/ppermute | solution.py:60
  208.9 4.9 %chunk.1 = (bf16[1,512,768]{2,1,0:T(8,128)(2,1)}, bf16[1,512,768]{2,1,0:T(8,128)(2,1)}, f32[512,768]{1,0:T(8,128)}) custom-call(bf16[512,2304]{1,0:T(8,128)(2,1)} %get-tuple-element.49.own_ref, bf16[256,2304]{1,0:T(8,128)(2,1)} %collective-permute-done.24.r2a, bf16[256,2304]{1,0:T(8,128)(2,1)} %collective-permute-done.25.r2b, bf16[256,1536]{1,0:T(8,128)(2,1)} %copy-done.7, ...), custom_call_target="tpu_custom_call" | custom-call | tf_op jit(solution)/shard_map/chunk/pallas_call | solution.py:493
  (128 shorter events, 65.9 us)
Async XLA Ops:
  3.2 9.9 %collective-permute-start = (bf16[32,2176]{1,0:T(8,128)(2,1)S(1)}, bf16[32,2176]{1,0:T(8,128)(2,1)S(1)}, u32[]{:S(2)}, u32[]{:S(2)}) collective-permute-start(bf16[32,2176]{1,0:T(8,128)(2,1)S(1)} %concatenate.3.refs_0_), channel_id=1, source_target_pairs={{0,8},{4,12},{8,16},{12,20},{16,24},{20,28},{24,32},{28,36},{32,40... | collective-permute-start | bytes 417800 | tf_op jit(solution)/shard_map/ppermute | solution.py:52
  19.5 11.9 %collective-permute-start.5 = (bf16[32,2176]{1,0:T(8,128)(2,1)S(1)}, bf16[32,2176]{1,0:T(8,128)(2,1)S(1)}, u32[]{:S(2)}, u32[]{:S(2)}) collective-permute-start(bf16[32,2176]{1,0:T(8,128)(2,1)S(1)} %collective-permute-done.3.refs_4_), channel_id=1, source_target_pairs={{0,56},{4,60},{8,0},{12,4},{16,8},{20,12},{24,16},{28,20},{32,24},... | collective-permute-start | bytes 417800 | tf_op jit(solution)/shard_map/ppermute | solution.py:52
  35.1 22.8 %collective-permute-start.10 = (bf16[256,2176]{1,0:T(8,128)(2,1)}, bf16[256,2176]{1,0:T(8,128)(2,1)S(1)}, u32[]{:S(2)}, u32[]{:S(2)}) collective-permute-start(bf16[256,2176]{1,0:T(8,128)(2,1)} %join.2.refs_0_.refs_4_), channel_id=1, source_target_pairs={{0,64},{4,68},{8,72},{12,76},{16,80},{20,84},{24,88},{28,92},{32,9... | collective-permute-start | bytes 3342344 | tf_op jit(solution)/shard_map/ppermute | solution.py:52
  35.1 22.8 %collective-permute-start.11 = (bf16[256,2176]{1,0:T(8,128)(2,1)}, bf16[256,2176]{1,0:T(8,128)(2,1)S(1)}, u32[]{:S(2)}, u32[]{:S(2)}) collective-permute-start(bf16[256,2176]{1,0:T(8,128)(2,1)} %join.2.refs_0_.refs_4_), channel_id=1, source_target_pairs={{0,192},{4,196},{8,200},{12,204},{16,208},{20,212},{24,216},{28,22... | collective-permute-start | bytes 3342344 | tf_op jit(solution)/shard_map/ppermute | solution.py:52
  39.7 9.7 %collective-permute-start.14 = (bf16[128,2048]{1,0:T(8,128)(2,1)}, bf16[128,2048]{1,0:T(8,128)(2,1)S(1)}, u32[]{:S(2)}, u32[]{:S(2)}) collective-permute-start(bf16[128,2048]{1,0:T(8,128)(2,1)} %join.3.refs_0_), channel_id=1, source_target_pairs={{0,8},{4,12},{8,16},{12,20},{16,24},{20,28},{24,32},{28,36},{32,40... | collective-permute-start | bytes 1572872 | tf_op jit(solution)/shard_map/ppermute | solution.py:52
  39.7 9.8 %collective-permute-start.15 = (bf16[128,2048]{1,0:T(8,128)(2,1)}, bf16[128,2048]{1,0:T(8,128)(2,1)S(1)}, u32[]{:S(2)}, u32[]{:S(2)}) collective-permute-start(bf16[128,2048]{1,0:T(8,128)(2,1)} %join.3.refs_0_), channel_id=1, source_target_pairs={{0,56},{4,60},{8,0},{12,4},{16,8},{20,12},{24,16},{28,20},{32,24},... | collective-permute-start | bytes 1572872 | tf_op jit(solution)/shard_map/ppermute | solution.py:52
  49.5 15.8 %collective-permute-start.16 = (bf16[128,2048]{1,0:T(8,128)(2,1)S(1)}, bf16[128,2048]{1,0:T(8,128)(2,1)}, u32[]{:S(2)}, u32[]{:S(2)}) collective-permute-start(bf16[128,2048]{1,0:T(8,128)(2,1)S(1)} %collective-permute-done.14.refs_1_), channel_id=1, source_target_pairs={{0,8},{4,12},{8,16},{12,20},{16,24},{20,28},{24,32},{28,36},{32,40... | collective-permute-start | bytes 1572872 | tf_op jit(solution)/shard_map/ppermute | solution.py:52
  49.5 15.8 %collective-permute-start.17 = (bf16[128,2048]{1,0:T(8,128)(2,1)S(1)}, bf16[128,2048]{1,0:T(8,128)(2,1)}, u32[]{:S(2)}, u32[]{:S(2)}) collective-permute-start(bf16[128,2048]{1,0:T(8,128)(2,1)S(1)} %collective-permute-done.15.refs_2_), channel_id=1, source_target_pairs={{0,56},{4,60},{8,0},{12,4},{16,8},{20,12},{24,16},{28,20},{32,24},... | collective-permute-start | bytes 1572872 | tf_op jit(solution)/shard_map/ppermute | solution.py:52
  62.6 9.8 %collective-permute-start.12 = (bf16[128,2176]{1,0:T(8,128)(2,1)}, bf16[128,2176]{1,0:T(8,128)(2,1)S(1)}, u32[]{:S(2)}, u32[]{:S(2)}) collective-permute-start(bf16[128,2176]{1,0:T(8,128)(2,1)} %get-tuple-element.33), channel_id=1, source_target_pairs={{0,64},{4,68},{8,72},{12,76},{16,80},{20,84},{24,88},{28,92},{32,9... | collective-permute-start | bytes 1671176 | tf_op jit(solution)/shard_map/ppermute | solution.py:52
  62.6 9.8 %collective-permute-start.13 = (bf16[128,2176]{1,0:T(8,128)(2,1)}, bf16[128,2176]{1,0:T(8,128)(2,1)S(1)}, u32[]{:S(2)}, u32[]{:S(2)}) collective-permute-start(bf16[128,2176]{1,0:T(8,128)(2,1)} %get-tuple-element.34), channel_id=1, source_target_pairs={{0,192},{4,196},{8,200},{12,204},{16,208},{20,212},{24,216},{28,22... | collective-permute-start | bytes 1671176 | tf_op jit(solution)/shard_map/ppermute | solution.py:52
  65.3 21.7 %collective-permute-start.18 = (bf16[128,2048]{1,0:T(8,128)(2,1)}, bf16[128,2048]{1,0:T(8,128)(2,1)S(1)}, u32[]{:S(2)}, u32[]{:S(2)}) collective-permute-start(bf16[128,2048]{1,0:T(8,128)(2,1)} %collective-permute-done.16.refs_3_), channel_id=1, source_target_pairs={{0,8},{4,12},{8,16},{12,20},{16,24},{20,28},{24,32},{28,36},{32,40... | collective-permute-start | bytes 1572872 | tf_op jit(solution)/shard_map/ppermute | solution.py:52
  65.3 21.7 %collective-permute-start.19 = (bf16[128,2048]{1,0:T(8,128)(2,1)}, bf16[128,2048]{1,0:T(8,128)(2,1)S(1)}, u32[]{:S(2)}, u32[]{:S(2)}) collective-permute-start(bf16[128,2048]{1,0:T(8,128)(2,1)} %collective-permute-done.17.refs_4_), channel_id=1, source_target_pairs={{0,56},{4,60},{8,0},{12,4},{16,8},{20,12},{24,16},{28,20},{32,24},... | collective-permute-start | bytes 1572872 | tf_op jit(solution)/shard_map/ppermute | solution.py:52
  80.3 26.2 %collective-permute-start.23 = (bf16[256,2176]{1,0:T(8,128)(2,1)}, bf16[256,2176]{1,0:T(8,128)(2,1)S(1)}, u32[]{:S(2)}, u32[]{:S(2)}) collective-permute-start(bf16[256,2176]{1,0:T(8,128)(2,1)} %get-tuple-element.41), channel_id=1, source_target_pairs={{0,4},{4,0},{8,12},{12,8},{16,20},{20,16},{24,28},{28,24},{32,36},... | collective-permute-start | bytes 3342344 | tf_op jit(solution)/shard_map/ppermute | solution.py:56
  90.6 9.4 %collective-permute-start.21 = (bf16[64,2048]{1,0:T(8,128)(2,1)}, bf16[64,2048]{1,0:T(8,128)(2,1)S(1)}, u32[]{:S(2)}, u32[]{:S(2)}) collective-permute-start(bf16[64,2048]{1,0:T(8,128)(2,1)} %get-tuple-element.37), channel_id=1, source_target_pairs={{0,56},{4,60},{8,0},{12,4},{16,8},{20,12},{24,16},{28,20},{32,24},... | collective-permute-start | bytes 786440 | tf_op jit(solution)/shard_map/ppermute | solution.py:52
  105.6 10.6 %collective-permute-start.22 = (bf16[256,2048]{1,0:T(8,128)(2,1)}, bf16[256,2048]{1,0:T(8,128)(2,1)S(1)}, u32[]{:S(2)}, u32[]{:S(2)}) collective-permute-start(bf16[256,2048]{1,0:T(8,128)(2,1)} %get-tuple-element.39), channel_id=1, source_target_pairs={{0,4},{4,0},{8,12},{12,8},{16,20},{20,16},{24,28},{28,24},{32,36},... | collective-permute-start | bytes 3145736 | tf_op jit(solution)/shard_map/ppermute | solution.py:56
  128.8 34.0 %collective-permute-start.26 = (bf16[256,2304]{1,0:T(8,128)(2,1)}, bf16[256,2304]{1,0:T(8,128)(2,1)S(1)}, u32[]{:S(2)}, u32[]{:S(2)}) collective-permute-start(bf16[256,2304]{1,0:T(8,128)(2,1)} %get-tuple-element.52), channel_id=1, source_target_pairs={{0,1},{1,2},{2,3},{3,0},{4,5},{5,6},{6,7},{7,4},{8,9},{9,10},{10,1... | collective-permute-start | bytes 3538952 | tf_op jit(solution)/shard_map/ppermute | solution.py:60
  130.3 32.6 %collective-permute-start.27 = (bf16[256,2304]{1,0:T(8,128)(2,1)}, bf16[256,2304]{1,0:T(8,128)(2,1)}, u32[]{:S(2)}, u32[]{:S(2)}) collective-permute-start(bf16[256,2304]{1,0:T(8,128)(2,1)} %get-tuple-element.53), channel_id=1, source_target_pairs={{0,3},{1,0},{2,1},{3,2},{4,7},{5,4},{6,5},{7,6},{8,11},{9,8},{10,9... | collective-permute-start | bytes 3538952 | tf_op jit(solution)/shard_map/ppermute | solution.py:60
  142.2 41.0 %collective-permute-start.24 = (bf16[256,2304]{1,0:T(8,128)(2,1)}, bf16[256,2304]{1,0:T(8,128)(2,1)}, u32[]{:S(2)}, u32[]{:S(2)}) collective-permute-start(bf16[256,2304]{1,0:T(8,128)(2,1)} %get-tuple-element.50), channel_id=1, source_target_pairs={{0,3},{1,0},{2,1},{3,2},{4,7},{5,4},{6,5},{7,6},{8,11},{9,8},{10,9... | collective-permute-start | bytes 3538952 | tf_op jit(solution)/shard_map/ppermute | solution.py:60
  154.1 65.8 %all-to-all-start = ((bf16[64,8,2176]{2,1,0:T(8,128)(2,1)}), bf16[64,8,2176]{2,1,0:T(8,128)(2,1)S(1)}, u32[]{:S(2)}, u32[]{:S(2)}) async-start(bf16[64,8,2176]{2,1,0:T(8,128)(2,1)} %slots.1), calls=%async_computation | async-start | bytes 4456448 | tf_op jit(solution)/shard_map/all_to_all | solution.py:632
  162.6 28.7 %collective-permute-start.25 = (bf16[256,2304]{1,0:T(8,128)(2,1)}, bf16[256,2304]{1,0:T(8,128)(2,1)}, u32[]{:S(2)}, u32[]{:S(2)}) collective-permute-start(bf16[256,2304]{1,0:T(8,128)(2,1)} %get-tuple-element.51), channel_id=1, source_target_pairs={{0,1},{1,2},{2,3},{3,0},{4,5},{5,6},{6,7},{7,4},{8,9},{9,10},{10,1... | collective-permute-start | bytes 3538952 | tf_op jit(solution)/shard_map/ppermute | solution.py:60
  171.8 36.2 %collective-permute-start.28 = (bf16[256,1536]{1,0:T(8,128)(2,1)}, bf16[256,1536]{1,0:T(8,128)(2,1)S(1)}, u32[]{:S(2)}, u32[]{:S(2)}) collective-permute-start(bf16[256,1536]{1,0:T(8,128)(2,1)} %get-tuple-element.54), channel_id=1, source_target_pairs={{0,1},{1,2},{2,3},{3,0},{4,5},{5,6},{6,7},{7,4},{8,9},{9,10},{10,1... | collective-permute-start | bytes 2359304 | tf_op jit(solution)/shard_map/ppermute | solution.py:60
  171.8 36.2 %collective-permute-start.29 = (bf16[256,1536]{1,0:T(8,128)(2,1)}, bf16[256,1536]{1,0:T(8,128)(2,1)}, u32[]{:S(2)}, u32[]{:S(2)}) collective-permute-start(bf16[256,1536]{1,0:T(8,128)(2,1)} %get-tuple-element.55), channel_id=1, source_target_pairs={{0,3},{1,0},{2,1},{3,2},{4,7},{5,4},{6,5},{7,6},{8,11},{9,8},{10,9... | collective-permute-start | bytes 2359304 | tf_op jit(solution)/shard_map/ppermute | solution.py:60
  174.7 41.7 %collective-permute-start.30 = (bf16[256,768]{1,0:T(8,128)(2,1)}, bf16[256,768]{1,0:T(8,128)(2,1)S(1)}, u32[]{:S(2)}, u32[]{:S(2)}) collective-permute-start(bf16[256,768]{1,0:T(8,128)(2,1)} %get-tuple-element.59), channel_id=1, source_target_pairs={{0,1},{1,2},{2,3},{3,0},{4,5},{5,6},{6,7},{7,4},{8,9},{9,10},{10,1... | collective-permute-start | bytes 1179656 | tf_op jit(solution)/shard_map/ppermute | solution.py:60
  183.2 33.3 %collective-permute-start.31 = (bf16[256,768]{1,0:T(8,128)(2,1)}, bf16[256,768]{1,0:T(8,128)(2,1)}, u32[]{:S(2)}, u32[]{:S(2)}) collective-permute-start(bf16[256,768]{1,0:T(8,128)(2,1)} %get-tuple-element.60), channel_id=1, source_target_pairs={{0,3},{1,0},{2,1},{3,2},{4,7},{5,4},{6,5},{7,6},{8,11},{9,8},{10,9... | collective-permute-start | bytes 1179656 | tf_op jit(solution)/shard_map/ppermute | solution.py:60
  (36 other events, 295.8 us)

commit v2 on v1

--- a/solution.py
+++ b/solution.py
@@ -66,23 +66,6 @@
     for ref in refs[:count]:
         out_ref[at : at + ref.shape[0], :] = ref[...]
         at += ref.shape[0]
-
-
-def halves_kernel(a_ref, b_ref, *refs):
-    n = a_ref.shape[0] // 2
-    refs[-2][...] = a_ref[:n]
-    refs[-1][...] = b_ref[n:]
-
-
-def halves(a, b, after):
-    half = jax.ShapeDtypeStruct((a.shape[0] // 2, a.shape[1]), a.dtype)
-    return pl.pallas_call(
-        halves_kernel,
-        out_shape=(half, half),
-        in_specs=[VM, VM] + [pl.BlockSpec(memory_space=pl.ANY)] * len(after),
-        out_specs=(VM, VM),
-        name="halves",
-    )(a, b, *after)
 
 
 def join(parts, after=()):
@@ -226,12 +209,13 @@
 
 def front_kernel(
     me_ref, own_ref, sib_ref, wg_ref, wu_ref,
-    hid_ref, hid_t_ref, a_ref, b_ref, weight_ref, x_scr,
+    hid_ref, hid_t_ref, a_ref, b_ref, weight_ref, x_t_ref, x_scr,
 ):
     @pl.when(pl.program_id(0) == 0)
     def _():
         x_scr[:HALF] = own_ref[:, :D]
         x_scr[HALF:] = sib_ref[:, :D]
+        x_t_ref[...] = x_scr[...].T
         meta = jnp.concatenate([own_ref[:, D:], sib_ref[:, D:]], axis=0).astype(f32)
         expert = me_ref[0].astype(f32)
         total = jnp.zeros((ROWS, 1), f32)
@@ -265,6 +249,7 @@
             jax.ShapeDtypeStruct((ROWS, FF), f32),
             jax.ShapeDtypeStruct((ROWS, FF), f32),
             jax.ShapeDtypeStruct((ROWS, META), f32),
+            jax.ShapeDtypeStruct((D, ROWS), bf16),
         ),
         in_specs=[
             SM, whole((HALF, DA)), whole((HALF, DA)),
@@ -273,7 +258,7 @@
         ],
         out_specs=(
             wide, pl.BlockSpec((FB, ROWS), lambda j: (j, 0)), wide, wide,
-            whole((ROWS, META)),
+            whole((ROWS, META)), whole((D, ROWS)),
         ),
         scratch_shapes=[pltpu.VMEM((ROWS, D), bf16)],
         compiler_params=pltpu.CompilerParams(vmem_limit_bytes=VLIM),
@@ -290,29 +275,17 @@
     return (2 * pos_ref[1] + piece) % (2 * NDP)
 
 
-def scale(weight_ref, own, sib):
-    weight = weight_ref[:, :1]
-    cot = jnp.concatenate([own, sib], axis=0)
-    return (weight * cot.astype(f32)).astype(bf16)
-
-
-def piece_into(out_ref, x_own, x_sib, g_ref, hid_t_ref, scot_cols):
-    def side(n, _):
-        value = dot(x_own, g_ref[n, :HALF], contract_first)
-        value = value + dot(x_sib, g_ref[n, HALF:], contract_first)
-        out_ref[:, pl.ds(pl.multiple_of(n * FF, FF), FF)] = value.astype(out_ref.dtype)
-        return 0
-
-    lax.fori_loop(0, 2, side, 0)
+def piece_into(out_ref, x_rows, g_ref, hid_t_ref, scot_cols):
+    for n in range(2):
+        out_ref[:, n * FF : (n + 1) * FF] = dot(x_rows, g_ref[n]).astype(bf16)
     for q in range(NFB):
         value = dot(hid_t_ref[q * FB : (q + 1) * FB], scot_cols)
-        out_ref[:, 2 * FF + q * FB : 2 * FF + (q + 1) * FB] = value.astype(out_ref.dtype)
+        out_ref[:, 2 * FF + q * FB : 2 * FF + (q + 1) * FB] = value.astype(bf16)
 
 
 def mid_kernel(
-    pos_ref, own_ref, sib_ref, hid_ref, hid_t_ref, a_ref, b_ref, weight_ref,
-    xoa_ref, xsa_ref, xob_ref, xsb_ref, wd_ref,
-    pa_ref, pb_ref, g_ref, route_ref, cot_scr, x_scr, out_scr,
+    pos_ref, own_ref, sib_ref, hid_ref, hid_t_ref, a_ref, b_ref, weight_ref, x_t_ref, wd_ref,
+    pa_ref, pb_ref, g_ref, route_ref, scot_ref, cot_scr, out_scr,
 ):
     j = pl.program_id(0)
 
@@ -320,9 +293,8 @@
     def _():
         cot_scr[:HALF] = own_ref[...]
         cot_scr[HALF:] = sib_ref[...]
+        scot_ref[...] = (weight_ref[:, :1] * cot_scr[...].astype(f32)).astype(bf16)
         route_ref[...] = jnp.zeros_like(route_ref)
-        for n, ref in enumerate((xoa_ref, xsa_ref, xob_ref, xsb_ref)):
-            x_scr[n] = ref[...]
 
     back = dot(cot_scr[...], wd_ref[...], contract_last)
     part = jnp.sum(hid_ref[...].astype(f32) * back, axis=1, keepdims=True)
@@ -335,137 +307,76 @@
     @pl.when(j == NFB - 1)
     def _():
         def step(n, _):
-            some = pl.ds(pl.multiple_of(place(pos_ref, 4 + n) * PIECE, PIECE), PIECE)
+            piece = jnp.where(n == 0, 4, jnp.where(n == 1, 3, jnp.where(n == 2, 5, 6)))
+            some = pl.ds(pl.multiple_of(place(pos_ref, piece) * PIECE, PIECE), PIECE)
             piece_into(
-                out_scr.at[n], x_scr[2 * n], x_scr[2 * n + 1], g_ref, hid_t_ref,
-                scale(weight_ref, own_ref[:, some], sib_ref[:, some]),
+                out_scr.at[n], x_t_ref[some, :], g_ref, hid_t_ref, scot_ref[:, some]
             )
             return 0
 
-        lax.fori_loop(0, 2, step, 0)
-        pa_ref[...] = out_scr[0]
-        pb_ref[...] = out_scr[1]
-
-
-def mid(pos, own, sib, hid, hid_t, a, b, weight, x_own, x_sib, wd):
+        lax.fori_loop(0, 4, step, 0)
+        for n in range(2):
+            pa_ref[n * PIECE : (n + 1) * PIECE] = out_scr[n]
+            pb_ref[n * PIECE : (n + 1) * PIECE] = out_scr[2 + n]
+
+
+def mid(pos, own, sib, hid, hid_t, a, b, weight, x_t, wd):
     wide = pl.BlockSpec((ROWS, FB), lambda j, pos_ref: (0, j))
-    xa = pl.BlockSpec((HALF, PIECE), lambda j, pos_ref: (0, place(pos_ref, 4)))
-    xb = pl.BlockSpec((HALF, PIECE), lambda j, pos_ref: (0, place(pos_ref, 5)))
+    size = (2 * PIECE, 3 * FF)
     return pl.pallas_call(
         mid_kernel,
         out_shape=(
-            jax.ShapeDtypeStruct((PIECE, 3 * FF), bf16),
-            jax.ShapeDtypeStruct((PIECE, 3 * FF), bf16),
+            jax.ShapeDtypeStruct(size, bf16),
+            jax.ShapeDtypeStruct(size, bf16),
             jax.ShapeDtypeStruct((2, ROWS, FF), bf16),
             jax.ShapeDtypeStruct((ROWS, META), f32),
+            jax.ShapeDtypeStruct((ROWS, D), bf16),
         ),
         grid_spec=pltpu.PrefetchScalarGridSpec(
             num_scalar_prefetch=1,
             grid=(NFB,),
             in_specs=[
                 whole((HALF, D)), whole((HALF, D)), wide, whole((FF, ROWS)), wide, wide,
-                whole((ROWS, META)), xa, xa, xb, xb,
+                whole((ROWS, META)), whole((D, ROWS)),
                 pl.BlockSpec((FB, D), lambda j, pos_ref: (j, 0)),
             ],
             out_specs=(
-                whole((PIECE, 3 * FF)), whole((PIECE, 3 * FF)), whole((2, ROWS, FF)),
-                whole((ROWS, META)),
+                whole(size), whole(size), whole((2, ROWS, FF)), whole((ROWS, META)),
+                whole((ROWS, D)),
             ),
             scratch_shapes=[
-                pltpu.VMEM((ROWS, D), bf16),
-                pltpu.VMEM((4, HALF, PIECE), bf16),
-                pltpu.VMEM((2, PIECE, 3 * FF), bf16),
+                pltpu.VMEM((ROWS, D), bf16), pltpu.VMEM((4, PIECE, 3 * FF), bf16),
             ],
         ),
         compiler_params=pltpu.CompilerParams(vmem_limit_bytes=VLIM),
         name="mid",
-    )(pos, own, sib, hid, hid_t, a, b, weight, x_own, x_sib, x_own, x_sib, wd)
-
-
-def pick_pieces(*which):
+    )(pos, own, sib, hid, hid_t, a, b, weight, x_t, wd)
+
+
+def plain_kernel(pos_ref, x_ref, c_ref, g_ref, hid_t_ref, out_ref):
+    piece_into(out_ref, x_ref[...], g_ref, hid_t_ref, c_ref[...])
+
+
+def plain(pos, x_t, scot, g, hid_t):
     def index(n, pos_ref):
-        piece = which[0]
-        for i in range(1, len(which)):
-            piece = jnp.where(n == i, which[i], piece)
-        return (0, place(pos_ref, piece))
-
-    half = pl.BlockSpec((HALF, PIECE), index)
-    return [half] * 4 + [whole((ROWS, META)), whole((2, ROWS, FF)), whole((FF, ROWS))]
-
-
-def plain_kernel(
-    pos_ref, xo, xs, co, cs, weight_ref, g_ref, hid_t_ref, a_ref, b_ref, own_ref, scr
-):
-    piece_into(scr, xo[...], xs[...], g_ref, hid_t_ref, scale(weight_ref, co[...], cs[...]))
-
-    @pl.when(pl.program_id(0) == 0)
-    def _():
-        a_ref[...] = scr[...]
-
-    @pl.when(pl.program_id(0) == 1)
-    def _():
-        b_ref[...] = scr[...]
-
-    @pl.when(pl.program_id(0) > 1)
-    def _():
-        own_ref[...] = scr[...]
-
-
-def plain(pos, *args):
-    size = (PIECE, 3 * FF)
+        return place(pos_ref, jnp.where(n == 0, 2, jnp.where(n == 1, 7, n - 2)))
+
     return pl.pallas_call(
         plain_kernel,
-        out_shape=(
-            jax.ShapeDtypeStruct(size, bf16),
-            jax.ShapeDtypeStruct(size, bf16),
-            jax.ShapeDtypeStruct((2 * PIECE, 3 * FF), bf16),
-        ),
+        out_shape=jax.ShapeDtypeStruct((4 * PIECE, 3 * FF), bf16),
         grid_spec=pltpu.PrefetchScalarGridSpec(
             num_scalar_prefetch=1,
             grid=(4,),
-            in_specs=pick_pieces(3, 6, 0, 1),
-            out_specs=(
-                whole(size), whole(size),
-                pl.BlockSpec(size, lambda n, pos_ref: (jnp.maximum(n - 2, 0), 0)),
-            ),
-            scratch_shapes=[pltpu.VMEM(size, bf16)],
+            in_specs=[
+                pl.BlockSpec((PIECE, ROWS), lambda n, pos_ref: (index(n, pos_ref), 0)),
+                pl.BlockSpec((ROWS, PIECE), lambda n, pos_ref: (0, index(n, pos_ref))),
+                whole((2, ROWS, FF)), whole((FF, ROWS)),
+            ],
+            out_specs=pl.BlockSpec((PIECE, 3 * FF), lambda n, pos_ref: (n, 0)),
         ),
         compiler_params=pltpu.CompilerParams(vmem_limit_bytes=VLIM),
         name="plain",
-    )(pos, *args)
-
-
-def added_kernel(
-    pos_ref, xo, xs, co, cs, weight_ref, g_ref, hid_t_ref, ra_ref, rb_ref,
-    a_ref, ad_ref, b_ref, bd_ref, scr,
-):
-    piece_into(
-        scr, xo[...], xs[...], g_ref, hid_t_ref, scale(weight_ref, co[...], cs[...])
-    )
-    for n, (r_ref, o_ref, d_ref) in enumerate(((ra_ref, a_ref, ad_ref), (rb_ref, b_ref, bd_ref))):
-
-        @pl.when(pl.program_id(0) == n)
-        def _():
-            o_ref[...] = (scr[:, : 2 * FF] + r_ref[:, : 2 * FF].astype(f32)).astype(bf16)
-            d_ref[...] = (scr[:, 2 * FF :] + r_ref[:, 2 * FF :].astype(f32)).astype(bf16)
-
-
-def added(pos, *args):
-    size = (PIECE, 3 * FF)
-    sizes = ((PIECE, 2 * FF), (PIECE, FF)) * 2
-    return pl.pallas_call(
-        added_kernel,
-        out_shape=tuple(jax.ShapeDtypeStruct(shape, bf16) for shape in sizes),
-        grid_spec=pltpu.PrefetchScalarGridSpec(
-            num_scalar_prefetch=1,
-            grid=(2,),
-            in_specs=pick_pieces(2, 7) + [whole(size)] * 2,
-            out_specs=tuple(whole(shape) for shape in sizes),
-            scratch_shapes=[pltpu.VMEM(size, f32)],
-        ),
-        compiler_params=pltpu.CompilerParams(vmem_limit_bytes=VLIM),
-        name="added",
-    )(pos, *args)
+    )(pos, x_t, scot, g, hid_t)
 
 
 def chunk_kernel(own_ref, r2a, r2b, r3a, r3b, gate_ref, up_ref, down_ref):
@@ -487,7 +398,7 @@
             lax.fori_loop(0, PIECE // 64, rows, 0)
 
 
-def chunk(own, *arrived):
+def chunk(more, *arrived):
     size = (PIECE, 3 * FF)
     per = D // NDP
     return pl.pallas_call(
@@ -498,12 +409,12 @@
             jax.ShapeDtypeStruct((1, per, FF), bf16),
             jax.ShapeDtypeStruct((per, FF), f32),
         ),
-        in_specs=[pl.BlockSpec(size, lambda n: (n, 0))]
-        + [whole(size)] * 2 + [whole((PIECE, 2 * FF))] * 2,
+        in_specs=[pl.BlockSpec(size, lambda n: (n + 2, 0))]
+        + [pl.BlockSpec(size, lambda n: (1, 0))] * 2 + [whole((PIECE, 2 * FF))] * 2,
         out_specs=(whole((1, per, FF)), whole((1, per, FF)), whole((per, FF))),
         compiler_params=pltpu.CompilerParams(vmem_limit_bytes=VLIM),
         name="chunk",
-    )(own, *arrived)
+    )(more, *arrived)
 
 
 def tail_kernel(sum_ref, ra_ref, rb_ref, out_ref):
@@ -609,34 +520,37 @@
         cu.append(shift(cu[-1], dz=1))
         cd.append(shift(cd[-1], dz=-1))
 
-    qa, qb = halves(p1, m1, after=[])
+    n = NZ * TOK // 2
+    qa, qb = p1[:n], m1[n:]
     blocks = x0, p1, m1, shift(qa, dy=1), shift(qb, dy=-1)
 
-    qa, qb = halves(cu[-1], cd[-1], after=[])
+    n = NY * TOK // 2
+    qa, qb = cu[-1][:n], cd[-1][n:]
     cq = [shift(qa, dz=1), shift(qb, dz=-1)]
 
     own_x, sib_x, code = pick_x(pos, blocks)
     sib_x = swap_core(sib_x)
     wg, wu, wd = w_gate[0], w_up[0], w_down[0]
-    hid, hid_t, a, b, weight = front(pos, own_x, sib_x, wg, wu)
+    hid, hid_t, a, b, weight, x_t = front(pos, own_x, sib_x, wg, wu)
 
     parts = [cot0, cu[1], cd[1], cu[2], cd[2], cu[3], cd[3], *cq]
     own_c, sib_c = pick_cot(code, parts, after=code)
     sib_c = swap_core(sib_c)
 
-    p2a, p2b, g, route = mid(
-        pos, own_c, sib_c, hid, hid_t, a, b, weight, own_x, sib_x, wd
-    )
-    r1a, r1b = shift_dp(p2a, 1), shift_dp(p2b, -1)
+    pa, pb, g, route, scot = mid(pos, own_c, sib_c, hid, hid_t, a, b, weight, x_t, wd)
+    ra, rb = shift_dp(pa, 1), shift_dp(pb, -1)
     out = slots(pos, g, route, wg, wu)
     got = lax.all_to_all(out, "ep", split_axis=0, concat_axis=0, tiled=True)
-    args = (own_x, sib_x, own_c, sib_c, weight, g, hid_t)
-    p1b, p3a, own = plain(pos, *args)
-    r2b, r2a = shift_dp(p1b, 1), shift_dp(p3a, -1)
-    p1a, p1a_down, p3b, p3b_down = added(pos, *args, r1a, r1b)
-    r3a, r3b = shift_dp(p1a, 1), shift_dp(p3b, -1)
-    r3a_down, r3b_down = shift_dp(p1a_down, 1), shift_dp(p3b_down, -1)
-    grad_gate, grad_up, partial = chunk(own, r2a, r2b, r3a, r3b)
+    more = plain(pos, x_t, scot, g, hid_t)
+
+    def added(n, arrived, cols):
+        mine = more[n * PIECE : (n + 1) * PIECE, cols].astype(f32)
+        return (mine + arrived[:PIECE, cols].astype(f32)).astype(bf16)
+
+    first, last = slice(0, 2 * FF), slice(2 * FF, 3 * FF)
+    r3a, r3b = shift_dp(added(0, ra, first), 1), shift_dp(added(1, rb, first), -1)
+    r3a_down, r3b_down = shift_dp(added(0, ra, last), 1), shift_dp(added(1, rb, last), -1)
+    grad_gate, grad_up, partial = chunk(more, rb, ra, r3a, r3b)
     grad_down = tail(partial, r3a_down, r3b_down)
 
     experts = NY * NZ * NC

time: 223 us -> 219 us (0.982)
  Pallas kernels: 76.8 us -> 64.8 us
  waiting for transfers between devices: 68.6 us -> 76 us
  local copies, waits for them, and re-layouts: 14.9 us -> 8.81 us
  other arithmetic: 1.82 us -> 7.25 us
    pallas_call x5 -> x2, Pallas kernels: 34.5 us -> 22.1 us  [the longest x1 14.7 us: mid(): pl.pallas_call(mid_kernel, out_shape=(jax.ShapeDtypeStruct(size, bf16), j...]
    ppermute x8 -> x6, waiting for transfers between devices: 32.9 us -> 41 us  [shift_dp(): return lax.ppermute(arr, 'dp', [(i, (i + by) % NDP) for i in range(NDP)])]
    unnamed x58 -> x48, local copies, waits for them, and re-layouts: 13.6 us -> 5.67 us
    convert_element_type x0 -> x2, other arithmetic: none -> 5.39 us  [added(): return (mine + arrived[:PIECE, cols].astype(f32)).astype(bf16)]
    ppermute x8 -> x6, starting transfers between devices: 9.82 us -> 7.83 us  [shift_dp(): return lax.ppermute(arr, 'dp', [(i, (i + by) % NDP) for i in range(NDP)])]
  transfers between devices with their start and end apart: 33 -> 31, of which waited for: 13 -> 14; matrix products, arithmetic and copies ran while one was open for 1% -> 4% of each run, Pallas kernels for 28% -> 22%
where the time goes in v2:
time: 219 us; the launch traced here: 217 us
  waiting for transfers between devices  76 us (35%)
  Pallas kernels  64.8 us (30%)
  starting transfers between devices  57.6 us (26%)
  local copies, waits for them, and re-layouts  8.81 us (4%)
  other arithmetic  7.25 us (3%)
    ppermute x6, waiting for transfers between devices, shift_dp(): return lax.ppermute(arr, 'dp', [(i, (i + by) % NDP) for i in range(NDP)])  41 us
    ppermute x22, waiting for transfers between devices, shift(): return lax.ppermute(arr, 'ep', pairs)  35 us
    ppermute x22, starting transfers between devices, shift(): return lax.ppermute(arr, 'ep', pairs)  32.5 us
    pallas_call x1, Pallas kernels, mid(): pl.pallas_call(mid_kernel, out_shape=(jax.ShapeDtypeStruct(size, bf16), j...  14.7 us
    pallas_call x1, Pallas kernels, slots(): pl.pallas_call(slots_kernel, grid=(D // WIDE,), out_shape=jax.ShapeDtypeS...  10.5 us
    all_to_all x1, starting transfers between devices, body(): got = lax.all_to_all(out, 'ep', split_axis=0, concat_axis=0, tiled=True)  9.85 us
    pallas_call x1, Pallas kernels, front(): pl.pallas_call(front_kernel, grid=(NFB,), out_shape=(jax.ShapeDtypeStruct...  9.31 us
    ppermute x6, starting transfers between devices, shift_dp(): return lax.ppermute(arr, 'dp', [(i, (i + by) % NDP) for i in range(NDP)])  7.83 us
  transfers between devices with their start and end apart: 31, of which 14 were waited for; matrix products, arithmetic and copies ran while one was open for 4% of the time, Pallas kernels for 22%

profile of v2, /device:TPU:1, one launch (start us, length us, event | category | flops | bytes accessed | tf_op | source)
XLA Modules:
  0.0 216.7 jit_solution(9221773136664649403)
XLA Ops:
  5.7 4.0 %collective-permute-start.1 = (bf16[32,2176]{1,0:T(8,128)(2,1)S(1)}, bf16[32,2176]{1,0:T(8,128)(2,1)S(1)}, u32[]{:S(2)}, u32[]{:S(2)}) collective-permute-start(bf16[32,2176]{1,0:T(8,128)(2,1)S(1)} %concatenate.3.refs_0_), channel_id=1, source_target_pairs={{0,56},{4,60},{8,0},{12,4},{16,8},{20,12},{24,16},{28,20},{32,24},... | collective-permute-start | bytes 417800 | tf_op jit(solution)/shard_map/ppermute | solution.py:52
  9.8 3.3 %collective-permute-done.refs_1_ = bf16[32,2176]{1,0:T(8,128)(2,1)S(1)} collective-permute-done((bf16[32,2176]{1,0:T(8,128)(2,1)S(1)}, bf16[32,2176]{1,0:T(8,128)(2,1)S(1)}, u32[]{:S(2)}, u32[]{:S(2)}) %collective-permute-start) | collective-permute-done | bytes 139296 | tf_op jit(solution)/shard_map/ppermute | solution.py:52
  23.3 2.7 %collective-permute-start.7 = (bf16[32,2048]{1,0:T(8,128)(2,1)}, bf16[32,2048]{1,0:T(8,128)(2,1)S(1)}, u32[]{:S(2)}, u32[]{:S(2)}) collective-permute-start(bf16[32,2048]{1,0:T(8,128)(2,1)} %refs_0_.1), channel_id=1, source_target_pairs={{0,192},{4,196},{8,200},{12,204},{16,208},{20,212},{24,216},{28,22... | collective-permute-start | bytes 393224 | tf_op jit(solution)/shard_map/ppermute | solution.py:52
  28.3 3.1 %collective-permute-done.9.refs_9_.refs_3_ = bf16[32,2048]{1,0:T(8,128)(2,1)S(1)} collective-permute-done((bf16[32,2048]{1,0:T(8,128)(2,1)S(1)}, bf16[32,2048]{1,0:T(8,128)(2,1)S(1)}, u32[]{:S(2)}, u32[]{:S(2)}) %collective-permute-start.9) | collective-permute-done | bytes 131104 | tf_op jit(solution)/shard_map/ppermute | solution.py:52
  42.4 7.1 %collective-permute-done.14.refs_1_ = bf16[128,2048]{1,0:T(8,128)(2,1)S(1)} collective-permute-done((bf16[128,2048]{1,0:T(8,128)(2,1)}, bf16[128,2048]{1,0:T(8,128)(2,1)S(1)}, u32[]{:S(2)}, u32[]{:S(2)}) %collective-permute-start.14) | collective-permute-done | bytes 524320 | tf_op jit(solution)/shard_map/ppermute | solution.py:52
  52.2 5.8 %collective-permute-done.10.refs_1_ = bf16[256,2176]{1,0:T(8,128)(2,1)S(1)} collective-permute-done((bf16[256,2176]{1,0:T(8,128)(2,1)}, bf16[256,2176]{1,0:T(8,128)(2,1)S(1)}, u32[]{:S(2)}, u32[]{:S(2)}) %collective-permute-start.10) | collective-permute-done | bytes 1114144 | tf_op jit(solution)/shard_map/ppermute | solution.py:52
  62.5 2.7 %collective-permute-start.19 = (bf16[128,2048]{1,0:T(8,128)(2,1)}, bf16[128,2048]{1,0:T(8,128)(2,1)S(1)}, u32[]{:S(2)}, u32[]{:S(2)}) collective-permute-start(bf16[128,2048]{1,0:T(8,128)(2,1)} %collective-permute-done.17.refs_4_), channel_id=1, source_target_pairs={{0,56},{4,60},{8,0},{12,4},{16,8},{20,12},{24,16},{28,20},{32,24},... | collective-permute-start | bytes 1572872 | tf_op jit(solution)/shard_map/ppermute | solution.py:52
  65.9 3.3 %collective-permute-done.12.refs_3_ = bf16[128,2176]{1,0:T(8,128)(2,1)} collective-permute-done((bf16[128,2176]{1,0:T(8,128)(2,1)}, bf16[128,2176]{1,0:T(8,128)(2,1)}, u32[]{:S(2)}, u32[]{:S(2)}) %collective-permute-start.12) | collective-permute-done | bytes 557088 | tf_op jit(solution)/shard_map/ppermute | solution.py:52
  69.3 6.2 %pick_x.1 = (bf16[256,2176]{1,0:T(8,128)(2,1)}, bf16[256,2176]{1,0:T(8,128)(2,1)}, bf16[4,256,128]{2,1,0:T(8,128)(2,1)}) custom-call(s32[2]{0:T(128)} %pad_add_fusion.me_ref.pos_ref, bf16[256,2176]{1,0:T(8,128)(2,1)} %join.2.refs_0_.refs_4_, bf16[256,2176]{1,0:T(8,128)(2,1)} %copy-done, bf16[256,2176]{1,0:T(8,128)(2,1)} %copy-done.1, ...), custom_call_target="tpu_custom_call" | custom-call | tf_op jit(solution)/shard_map/pick_x/pallas_call | solution.py:148
  75.5 6.8 %collective-permute-start.23 = (bf16[256,2176]{1,0:T(8,128)(2,1)}, bf16[256,2176]{1,0:T(8,128)(2,1)S(1)}, u32[]{:S(2)}, u32[]{:S(2)}) collective-permute-start(bf16[256,2176]{1,0:T(8,128)(2,1)} %get-tuple-element.28), channel_id=1, source_target_pairs={{0,4},{4,0},{8,12},{12,8},{16,20},{20,16},{24,28},{28,24},{32,36},... | collective-permute-start | bytes 3342344 | tf_op jit(solution)/shard_map/ppermute | solution.py:56
  82.5 3.0 %collective-permute-start.21 = (bf16[64,2048]{1,0:T(8,128)(2,1)S(1)}, bf16[64,2048]{1,0:T(8,128)(2,1)S(1)}, u32[]{:S(2)}, u32[]{:S(2)}) collective-permute-start(bf16[64,2048]{1,0:T(8,128)(2,1)S(1)} %slice.59), channel_id=1, source_target_pairs={{0,56},{4,60},{8,0},{12,4},{16,8},{20,12},{24,16},{28,20},{32,24},... | collective-permute-start | bytes 786440 | tf_op jit(solution)/shard_map/ppermute | solution.py:52
  85.5 6.5 %collective-permute-done.20.refs_7_ = bf16[64,2048]{1,0:T(8,128)(2,1)S(1)} collective-permute-done((bf16[64,2048]{1,0:T(8,128)(2,1)S(1)}, bf16[64,2048]{1,0:T(8,128)(2,1)S(1)}, u32[]{:S(2)}, u32[]{:S(2)}) %collective-permute-start.20) | collective-permute-done | bytes 262176 | tf_op jit(solution)/shard_map/ppermute | solution.py:52
  92.8 4.8 %pick_cot.1 = (bf16[256,2048]{1,0:T(8,128)(2,1)}, bf16[256,2048]{1,0:T(8,128)(2,1)}) custom-call(bf16[4,256,128]{2,1,0:T(8,128)(2,1)} %get-tuple-element.24.code_ref.refs_9_, bf16[128,2048]{1,0:T(8,128)(2,1)} %join.3.refs_0_, bf16[128,2048]{1,0:T(8,128)(2,1)} %copy-done.6, bf16[128,2048]{1,0:T(8,128)(2,1)} %copy-done.7, ...), custom_call_target="tpu_custom_call" | custom-call | tf_op jit(solution)/shard_map/pick_cot/pallas_call | solution.py:195
  99.2 9.3 %front.1 = (bf16[512,768]{1,0:T(8,128)(2,1)}, bf16[768,512]{1,0:T(8,128)(2,1)}, f32[512,768]{1,0:T(8,128)}, f32[512,768]{1,0:T(8,128)}, f32[512,128]{1,0:T(8,128)}, /*index=5*/bf16[2048,512]{1,0:T(8,128)(2,1)}) custom-call(s32[2]{0:T(128)} %pad_add_fusion.me_ref.pos_ref, bf16[256,2176]{1,0:T(8,128)(2,1)} %get-tuple-element.27.own_ref, ...), custom_call_target="tpu_custom_call" | custom-call | flops 5000000000 | tf_op jit(solution)/shard_map/front/pallas_call | solution.py:243
  109.5 14.7 %mid.1 = (bf16[512,2304]{1,0:T(8,128)(2,1)}, bf16[512,2304]{1,0:T(8,128)(2,1)}, bf16[2,512,768]{2,1,0:T(8,128)(2,1)}, f32[512,128]{1,0:T(8,128)}, bf16[512,2048]{1,0:T(8,128)(2,1)}) custom-call(s32[2]{0:T(128)} %pad_add_fusion.me_ref.pos_ref, bf16[256,2048]{1,0:T(8,128)(2,1)} %get-tuple-element.25.own_ref, bf16[256,2048]{1,0:T(8,128)(2,1)} %copy-done.4, ...), custom_call_target="tpu_custom_call" | custom-call | tf_op jit(solution)/shard_map/mid/pallas_call | solution.py:326
  126.8 10.5 %slots.1 = bf16[64,8,2176]{2,1,0:T(8,128)(2,1)} custom-call(s32[2]{0:T(128)} %pad_add_fusion.me_ref.pos_ref, bf16[2,512,768]{2,1,0:T(8,128)(2,1)} %get-tuple-element.35.g_ref, f32[512,128]{1,0:T(8,128)} %get-tuple-element.36.route_ref, bf16[2048,768]{1,0:T(8,128)(2,1)} %bitcast.14, bf16[2048,768]{1,0:T(8,128)(2,1)} %bitcast.16), custom_call_target="tpu_custom_call" | custom-call | tf_op jit(solution)/shard_map/slots/pallas_call | solution.py:479
  137.3 9.8 %all-to-all-start = ((bf16[64,8,2176]{2,1,0:T(8,128)(2,1)}), bf16[64,8,2176]{2,1,0:T(8,128)(2,1)S(1)}, u32[]{:S(2)}, u32[]{:S(2)}) async-start(bf16[64,8,2176]{2,1,0:T(8,128)(2,1)} %slots.1), calls=%async_computation | async-start | bytes 4456448 | tf_op jit(solution)/shard_map/all_to_all | solution.py:543
  147.2 7.4 %plain.1.own_ref = bf16[1024,2304]{1,0:T(8,128)(2,1)} custom-call(s32[2]{0:T(128)} %pad_add_fusion.me_ref.pos_ref, bf16[2048,512]{1,0:T(8,128)(2,1)} %get-tuple-element.34.x_t_ref.x_ref, bf16[512,2048]{1,0:T(8,128)(2,1)} %get-tuple-element.37.c_ref, bf16[2,512,768]{2,1,0:T(8,128)(2,1)} %get-tuple-element.35.g_ref, bf16[768,512]{1,0:T(8,128)(2,1)} %get-tuple-element.30.hid_t_ref), custom_call_target="tpu_custom_call" | custom-call | tf_op jit(solution)/shard_map/plain/pallas_call | solution.py:364
  154.6 23.1 %collective-permute-done.24.r2a = bf16[512,2304]{1,0:T(8,128)(2,1)} collective-permute-done((bf16[512,2304]{1,0:T(8,128)(2,1)}, bf16[512,2304]{1,0:T(8,128)(2,1)}, u32[]{:S(2)}, u32[]{:S(2)}) %collective-permute-start.24) | collective-permute-done | bytes 2359328 | tf_op jit(solution)/shard_map/ppermute | solution.py:60
  177.7 3.1 %collective-permute-done.25.r2b = bf16[512,2304]{1,0:T(8,128)(2,1)} collective-permute-done((bf16[512,2304]{1,0:T(8,128)(2,1)}, bf16[512,2304]{1,0:T(8,128)(2,1)}, u32[]{:S(2)}, u32[]{:S(2)}) %collective-permute-start.25) | collective-permute-done | bytes 2359328 | tf_op jit(solution)/shard_map/ppermute | solution.py:60
  180.8 3.1 %add_convert_fusion = (bf16[256,1536]{1,0:T(8,128)(2,1)S(1)}, bf16[256,1536]{1,0:T(8,128)(2,1)}) fusion(bf16[512,2304]{1,0:T(8,128)(2,1)} %collective-permute-done.24.r2a, bf16[1024,2304]{1,0:T(8,128)(2,1)} %plain.1.own_ref, bf16[512,2304]{1,0:T(8,128)(2,1)} %collective-permute-done.25.r2b), kind=kLoop, calls=%fused_computation.2 | loop fusion | flops 3145728 | bytes 4718592 | tf_op jit(solution)/shard_map/convert_element_type | solution.py:548
  192.0 11.3 %collective-permute-done.26.r3a = bf16[256,1536]{1,0:T(8,128)(2,1)} collective-permute-done((bf16[256,1536]{1,0:T(8,128)(2,1)}, bf16[256,1536]{1,0:T(8,128)(2,1)}, u32[]{:S(2)}, u32[]{:S(2)}) %collective-permute-start.26) | collective-permute-done | bytes 786464 | tf_op jit(solution)/shard_map/ppermute | solution.py:60
  203.4 4.9 %chunk.1 = (bf16[1,512,768]{2,1,0:T(8,128)(2,1)}, bf16[1,512,768]{2,1,0:T(8,128)(2,1)}, f32[512,768]{1,0:T(8,128)}) custom-call(bf16[1024,2304]{1,0:T(8,128)(2,1)} %plain.1.own_ref, bf16[512,2304]{1,0:T(8,128)(2,1)} %collective-permute-done.24.r2a, bf16[512,2304]{1,0:T(8,128)(2,1)} %collective-permute-done.25.r2b, ...), custom_call_target="tpu_custom_call" | custom-call | tf_op jit(solution)/shard_map/chunk/pallas_call | solution.py:404
  208.3 3.5 %collective-permute-done.28.ra_ref = bf16[256,768]{1,0:T(8,128)(2,1)} collective-permute-done((bf16[256,768]{1,0:T(8,128)(2,1)}, bf16[256,768]{1,0:T(8,128)(2,1)}, u32[]{:S(2)}, u32[]{:S(2)}) %collective-permute-start.28) | collective-permute-done | bytes 393248 | tf_op jit(solution)/shard_map/ppermute | solution.py:60
  (117 shorter events, 55.6 us)
Async XLA Ops:
  3.2 9.9 %collective-permute-start = (bf16[32,2176]{1,0:T(8,128)(2,1)S(1)}, bf16[32,2176]{1,0:T(8,128)(2,1)S(1)}, u32[]{:S(2)}, u32[]{:S(2)}) collective-permute-start(bf16[32,2176]{1,0:T(8,128)(2,1)S(1)} %concatenate.3.refs_0_), channel_id=1, source_target_pairs={{0,8},{4,12},{8,16},{12,20},{16,24},{20,28},{24,32},{28,36},{32,40... | collective-permute-start | bytes 417800 | tf_op jit(solution)/shard_map/ppermute | solution.py:52
  19.5 11.9 %collective-permute-start.5 = (bf16[32,2176]{1,0:T(8,128)(2,1)S(1)}, bf16[32,2176]{1,0:T(8,128)(2,1)S(1)}, u32[]{:S(2)}, u32[]{:S(2)}) collective-permute-start(bf16[32,2176]{1,0:T(8,128)(2,1)S(1)} %collective-permute-done.3.refs_4_), channel_id=1, source_target_pairs={{0,56},{4,60},{8,0},{12,4},{16,8},{20,12},{24,16},{28,20},{32,24},... | collective-permute-start | bytes 417800 | tf_op jit(solution)/shard_map/ppermute | solution.py:52
  23.3 8.1 %collective-permute-start.6 = (bf16[32,2176]{1,0:T(8,128)(2,1)S(1)}, bf16[32,2176]{1,0:T(8,128)(2,1)S(1)}, u32[]{:S(2)}, u32[]{:S(2)}) collective-permute-start(bf16[32,2176]{1,0:T(8,128)(2,1)S(1)} %collective-permute-done.4.refs_5_), channel_id=1, source_target_pairs={{0,8},{4,12},{8,16},{12,20},{16,24},{20,28},{24,32},{28,36},{32,40... | collective-permute-start | bytes 417800 | tf_op jit(solution)/shard_map/ppermute | solution.py:52
  35.2 22.8 %collective-permute-start.10 = (bf16[256,2176]{1,0:T(8,128)(2,1)}, bf16[256,2176]{1,0:T(8,128)(2,1)S(1)}, u32[]{:S(2)}, u32[]{:S(2)}) collective-permute-start(bf16[256,2176]{1,0:T(8,128)(2,1)} %join.2.refs_0_.refs_4_), channel_id=1, source_target_pairs={{0,64},{4,68},{8,72},{12,76},{16,80},{20,84},{24,88},{28,92},{32,9... | collective-permute-start | bytes 3342344 | tf_op jit(solution)/shard_map/ppermute | solution.py:52
  35.2 23.7 %collective-permute-start.11 = (bf16[256,2176]{1,0:T(8,128)(2,1)}, bf16[256,2176]{1,0:T(8,128)(2,1)S(1)}, u32[]{:S(2)}, u32[]{:S(2)}) collective-permute-start(bf16[256,2176]{1,0:T(8,128)(2,1)} %join.2.refs_0_.refs_4_), channel_id=1, source_target_pairs={{0,192},{4,196},{8,200},{12,204},{16,208},{20,212},{24,216},{28,22... | collective-permute-start | bytes 3342344 | tf_op jit(solution)/shard_map/ppermute | solution.py:52
  39.8 9.7 %collective-permute-start.14 = (bf16[128,2048]{1,0:T(8,128)(2,1)}, bf16[128,2048]{1,0:T(8,128)(2,1)S(1)}, u32[]{:S(2)}, u32[]{:S(2)}) collective-permute-start(bf16[128,2048]{1,0:T(8,128)(2,1)} %join.3.refs_0_), channel_id=1, source_target_pairs={{0,8},{4,12},{8,16},{12,20},{16,24},{20,28},{24,32},{28,36},{32,40... | collective-permute-start | bytes 1572872 | tf_op jit(solution)/shard_map/ppermute | solution.py:52
  39.8 9.8 %collective-permute-start.15 = (bf16[128,2048]{1,0:T(8,128)(2,1)}, bf16[128,2048]{1,0:T(8,128)(2,1)S(1)}, u32[]{:S(2)}, u32[]{:S(2)}) collective-permute-start(bf16[128,2048]{1,0:T(8,128)(2,1)} %join.3.refs_0_), channel_id=1, source_target_pairs={{0,56},{4,60},{8,0},{12,4},{16,8},{20,12},{24,16},{28,20},{32,24},... | collective-permute-start | bytes 1572872 | tf_op jit(solution)/shard_map/ppermute | solution.py:52
  49.5 13.0 %collective-permute-start.16 = (bf16[128,2048]{1,0:T(8,128)(2,1)S(1)}, bf16[128,2048]{1,0:T(8,128)(2,1)}, u32[]{:S(2)}, u32[]{:S(2)}) collective-permute-start(bf16[128,2048]{1,0:T(8,128)(2,1)S(1)} %collective-permute-done.14.refs_1_), channel_id=1, source_target_pairs={{0,8},{4,12},{8,16},{12,20},{16,24},{20,28},{24,32},{28,36},{32,40... | collective-permute-start | bytes 1572872 | tf_op jit(solution)/shard_map/ppermute | solution.py:52
  49.5 13.0 %collective-permute-start.17 = (bf16[128,2048]{1,0:T(8,128)(2,1)S(1)}, bf16[128,2048]{1,0:T(8,128)(2,1)}, u32[]{:S(2)}, u32[]{:S(2)}) collective-permute-start(bf16[128,2048]{1,0:T(8,128)(2,1)S(1)} %collective-permute-done.15.refs_2_), channel_id=1, source_target_pairs={{0,56},{4,60},{8,0},{12,4},{16,8},{20,12},{24,16},{28,20},{32,24},... | collective-permute-start | bytes 1572872 | tf_op jit(solution)/shard_map/ppermute | solution.py:52
  58.9 10.2 %collective-permute-start.12 = (bf16[128,2176]{1,0:T(8,128)(2,1)}, bf16[128,2176]{1,0:T(8,128)(2,1)}, u32[]{:S(2)}, u32[]{:S(2)}) collective-permute-start(bf16[128,2176]{1,0:T(8,128)(2,1)} %slice.56), channel_id=1, source_target_pairs={{0,64},{4,68},{8,72},{12,76},{16,80},{20,84},{24,88},{28,92},{32,9... | collective-permute-start | bytes 1671176 | tf_op jit(solution)/shard_map/ppermute | solution.py:52
  59.8 9.5 %collective-permute-start.13 = (bf16[128,2176]{1,0:T(8,128)(2,1)}, bf16[128,2176]{1,0:T(8,128)(2,1)}, u32[]{:S(2)}, u32[]{:S(2)}) collective-permute-start(bf16[128,2176]{1,0:T(8,128)(2,1)} %slice.57), channel_id=1, source_target_pairs={{0,192},{4,196},{8,200},{12,204},{16,208},{20,212},{24,216},{28,22... | collective-permute-start | bytes 1671176 | tf_op jit(solution)/shard_map/ppermute | solution.py:52
  62.5 19.8 %collective-permute-start.18 = (bf16[128,2048]{1,0:T(8,128)(2,1)}, bf16[128,2048]{1,0:T(8,128)(2,1)S(1)}, u32[]{:S(2)}, u32[]{:S(2)}) collective-permute-start(bf16[128,2048]{1,0:T(8,128)(2,1)} %collective-permute-done.16.refs_3_), channel_id=1, source_target_pairs={{0,8},{4,12},{8,16},{12,20},{16,24},{20,28},{24,32},{28,36},{32,40... | collective-permute-start | bytes 1572872 | tf_op jit(solution)/shard_map/ppermute | solution.py:52
  62.5 19.9 %collective-permute-start.19 = (bf16[128,2048]{1,0:T(8,128)(2,1)}, bf16[128,2048]{1,0:T(8,128)(2,1)S(1)}, u32[]{:S(2)}, u32[]{:S(2)}) collective-permute-start(bf16[128,2048]{1,0:T(8,128)(2,1)} %collective-permute-done.17.refs_4_), channel_id=1, source_target_pairs={{0,56},{4,60},{8,0},{12,4},{16,8},{20,12},{24,16},{28,20},{32,24},... | collective-permute-start | bytes 1572872 | tf_op jit(solution)/shard_map/ppermute | solution.py:52
  75.5 22.8 %collective-permute-start.23 = (bf16[256,2176]{1,0:T(8,128)(2,1)}, bf16[256,2176]{1,0:T(8,128)(2,1)S(1)}, u32[]{:S(2)}, u32[]{:S(2)}) collective-permute-start(bf16[256,2176]{1,0:T(8,128)(2,1)} %get-tuple-element.28), channel_id=1, source_target_pairs={{0,4},{4,0},{8,12},{12,8},{16,20},{20,16},{24,28},{28,24},{32,36},... | collective-permute-start | bytes 3342344 | tf_op jit(solution)/shard_map/ppermute | solution.py:56
  82.3 9.7 %collective-permute-start.20 = (bf16[64,2048]{1,0:T(8,128)(2,1)S(1)}, bf16[64,2048]{1,0:T(8,128)(2,1)S(1)}, u32[]{:S(2)}, u32[]{:S(2)}) collective-permute-start(bf16[64,2048]{1,0:T(8,128)(2,1)S(1)} %slice.58), channel_id=1, source_target_pairs={{0,8},{4,12},{8,16},{12,20},{16,24},{20,28},{24,32},{28,36},{32,40... | collective-permute-start | bytes 786440 | tf_op jit(solution)/shard_map/ppermute | solution.py:52
  82.5 9.6 %collective-permute-start.21 = (bf16[64,2048]{1,0:T(8,128)(2,1)S(1)}, bf16[64,2048]{1,0:T(8,128)(2,1)S(1)}, u32[]{:S(2)}, u32[]{:S(2)}) collective-permute-start(bf16[64,2048]{1,0:T(8,128)(2,1)S(1)} %slice.59), channel_id=1, source_target_pairs={{0,56},{4,60},{8,0},{12,4},{16,8},{20,12},{24,16},{28,20},{32,24},... | collective-permute-start | bytes 786440 | tf_op jit(solution)/shard_map/ppermute | solution.py:52
  97.7 10.9 %collective-permute-start.22 = (bf16[256,2048]{1,0:T(8,128)(2,1)}, bf16[256,2048]{1,0:T(8,128)(2,1)S(1)}, u32[]{:S(2)}, u32[]{:S(2)}) collective-permute-start(bf16[256,2048]{1,0:T(8,128)(2,1)} %get-tuple-element.26), channel_id=1, source_target_pairs={{0,4},{4,0},{8,12},{12,8},{16,20},{20,16},{24,28},{28,24},{32,36},... | collective-permute-start | bytes 3145736 | tf_op jit(solution)/shard_map/ppermute | solution.py:56
  124.2 53.5 %collective-permute-start.24 = (bf16[512,2304]{1,0:T(8,128)(2,1)}, bf16[512,2304]{1,0:T(8,128)(2,1)}, u32[]{:S(2)}, u32[]{:S(2)}) collective-permute-start(bf16[512,2304]{1,0:T(8,128)(2,1)} %get-tuple-element.38), channel_id=1, source_target_pairs={{0,3},{1,0},{2,1},{3,2},{4,7},{5,4},{6,5},{7,6},{8,11},{9,8},{10,9... | collective-permute-start | bytes 7077896 | tf_op jit(solution)/shard_map/ppermute | solution.py:60
  126.7 54.1 %collective-permute-start.25 = (bf16[512,2304]{1,0:T(8,128)(2,1)}, bf16[512,2304]{1,0:T(8,128)(2,1)}, u32[]{:S(2)}, u32[]{:S(2)}) collective-permute-start(bf16[512,2304]{1,0:T(8,128)(2,1)} %get-tuple-element.39), channel_id=1, source_target_pairs={{0,1},{1,2},{2,3},{3,0},{4,5},{5,6},{6,7},{7,4},{8,9},{9,10},{10,1... | collective-permute-start | bytes 7077896 | tf_op jit(solution)/shard_map/ppermute | solution.py:60
  137.3 77.1 %all-to-all-start = ((bf16[64,8,2176]{2,1,0:T(8,128)(2,1)}), bf16[64,8,2176]{2,1,0:T(8,128)(2,1)S(1)}, u32[]{:S(2)}, u32[]{:S(2)}) async-start(bf16[64,8,2176]{2,1,0:T(8,128)(2,1)} %slots.1), calls=%async_computation | async-start | bytes 4456448 | tf_op jit(solution)/shard_map/all_to_all | solution.py:543
  183.9 19.5 %collective-permute-start.26 = (bf16[256,1536]{1,0:T(8,128)(2,1)}, bf16[256,1536]{1,0:T(8,128)(2,1)}, u32[]{:S(2)}, u32[]{:S(2)}) collective-permute-start(bf16[256,1536]{1,0:T(8,128)(2,1)} %get-tuple-element.56), channel_id=1, source_target_pairs={{0,1},{1,2},{2,3},{3,0},{4,5},{5,6},{6,7},{7,4},{8,9},{9,10},{10,1... | collective-permute-start | bytes 2359304 | tf_op jit(solution)/shard_map/ppermute | solution.py:60
  183.9 19.5 %collective-permute-start.27 = (bf16[256,1536]{1,0:T(8,128)(2,1)S(1)}, bf16[256,1536]{1,0:T(8,128)(2,1)}, u32[]{:S(2)}, u32[]{:S(2)}) collective-permute-start(bf16[256,1536]{1,0:T(8,128)(2,1)S(1)} %get-tuple-element.55), channel_id=1, source_target_pairs={{0,3},{1,0},{2,1},{3,2},{4,7},{5,4},{6,5},{7,6},{8,11},{9,8},{10,9... | collective-permute-start | bytes 2359304 | tf_op jit(solution)/shard_map/ppermute | solution.py:60
  189.0 22.8 %collective-permute-start.28 = (bf16[256,768]{1,0:T(8,128)(2,1)}, bf16[256,768]{1,0:T(8,128)(2,1)}, u32[]{:S(2)}, u32[]{:S(2)}) collective-permute-start(bf16[256,768]{1,0:T(8,128)(2,1)} %get-tuple-element.54), channel_id=1, source_target_pairs={{0,1},{1,2},{2,3},{3,0},{4,5},{5,6},{6,7},{7,4},{8,9},{9,10},{10,1... | collective-permute-start | bytes 1179656 | tf_op jit(solution)/shard_map/ppermute | solution.py:60
  189.0 22.8 %collective-permute-start.29 = (bf16[256,768]{1,0:T(8,128)(2,1)S(1)}, bf16[256,768]{1,0:T(8,128)(2,1)}, u32[]{:S(2)}, u32[]{:S(2)}) collective-permute-start(bf16[256,768]{1,0:T(8,128)(2,1)S(1)} %get-tuple-element.53), channel_id=1, source_target_pairs={{0,3},{1,0},{2,1},{3,2},{4,7},{5,4},{6,5},{7,6},{8,11},{9,8},{10,9... | collective-permute-start | bytes 1179656 | tf_op jit(solution)/shard_map/ppermute | solution.py:60
  (29 other events, 244.8 us)

commit v3 on v2

--- a/solution.py
+++ b/solution.py
@@ -285,7 +285,7 @@
 
 def mid_kernel(
     pos_ref, own_ref, sib_ref, hid_ref, hid_t_ref, a_ref, b_ref, weight_ref, x_t_ref, wd_ref,
-    pa_ref, pb_ref, g_ref, route_ref, scot_ref, cot_scr, out_scr,
+    pa_ref, pb_ref, pc_ref, pd_ref, g_ref, route_ref, scot_ref, cot_scr, out_scr,
 ):
     j = pl.program_id(0)
 
@@ -307,7 +307,7 @@
     @pl.when(j == NFB - 1)
     def _():
         def step(n, _):
-            piece = jnp.where(n == 0, 4, jnp.where(n == 1, 3, jnp.where(n == 2, 5, 6)))
+            piece = jnp.where(n == 0, 4, jnp.where(n == 1, 5, jnp.where(n == 2, 3, 6)))
             some = pl.ds(pl.multiple_of(place(pos_ref, piece) * PIECE, PIECE), PIECE)
             piece_into(
                 out_scr.at[n], x_t_ref[some, :], g_ref, hid_t_ref, scot_ref[:, some]
@@ -315,19 +315,17 @@
             return 0
 
         lax.fori_loop(0, 4, step, 0)
-        for n in range(2):
-            pa_ref[n * PIECE : (n + 1) * PIECE] = out_scr[n]
-            pb_ref[n * PIECE : (n + 1) * PIECE] = out_scr[2 + n]
+        for n, ref in enumerate((pa_ref, pb_ref, pc_ref, pd_ref)):
+            ref[...] = out_scr[n]
 
 
 def mid(pos, own, sib, hid, hid_t, a, b, weight, x_t, wd):
     wide = pl.BlockSpec((ROWS, FB), lambda j, pos_ref: (0, j))
-    size = (2 * PIECE, 3 * FF)
+    size = (PIECE, 3 * FF)
     return pl.pallas_call(
         mid_kernel,
         out_shape=(
-            jax.ShapeDtypeStruct(size, bf16),
-            jax.ShapeDtypeStruct(size, bf16),
+            *[jax.ShapeDtypeStruct(size, bf16)] * 4,
             jax.ShapeDtypeStruct((2, ROWS, FF), bf16),
             jax.ShapeDtypeStruct((ROWS, META), f32),
             jax.ShapeDtypeStruct((ROWS, D), bf16),
@@ -341,8 +339,7 @@
                 pl.BlockSpec((FB, D), lambda j, pos_ref: (j, 0)),
             ],
             out_specs=(
-                whole(size), whole(size), whole((2, ROWS, FF)), whole((ROWS, META)),
-                whole((ROWS, D)),
+                *[whole(size)] * 4, whole((2, ROWS, FF)), whole((ROWS, META)), whole((ROWS, D)),
             ),
             scratch_shapes=[
                 pltpu.VMEM((ROWS, D), bf16), pltpu.VMEM((4, PIECE, 3 * FF), bf16),
@@ -353,11 +350,11 @@
     )(pos, own, sib, hid, hid_t, a, b, weight, x_t, wd)
 
 
-def plain_kernel(pos_ref, x_ref, c_ref, g_ref, hid_t_ref, out_ref):
+def plain_kernel(pos_ref, x_ref, c_ref, g_ref, hid_t_ref, _, out_ref):
     piece_into(out_ref, x_ref[...], g_ref, hid_t_ref, c_ref[...])
 
 
-def plain(pos, x_t, scot, g, hid_t):
+def plain(pos, x_t, scot, g, hid_t, after):
     def index(n, pos_ref):
         return place(pos_ref, jnp.where(n == 0, 2, jnp.where(n == 1, 7, n - 2)))
 
@@ -371,12 +368,13 @@
                 pl.BlockSpec((PIECE, ROWS), lambda n, pos_ref: (index(n, pos_ref), 0)),
                 pl.BlockSpec((ROWS, PIECE), lambda n, pos_ref: (0, index(n, pos_ref))),
                 whole((2, ROWS, FF)), whole((FF, ROWS)),
+                pl.BlockSpec(memory_space=pl.ANY),
             ],
             out_specs=pl.BlockSpec((PIECE, 3 * FF), lambda n, pos_ref: (n, 0)),
         ),
         compiler_params=pltpu.CompilerParams(vmem_limit_bytes=VLIM),
         name="plain",
-    )(pos, x_t, scot, g, hid_t)
+    )(pos, x_t, scot, g, hid_t, after)
 
 
 def chunk_kernel(own_ref, r2a, r2b, r3a, r3b, gate_ref, up_ref, down_ref):
@@ -410,14 +408,15 @@
             jax.ShapeDtypeStruct((per, FF), f32),
         ),
         in_specs=[pl.BlockSpec(size, lambda n: (n + 2, 0))]
-        + [pl.BlockSpec(size, lambda n: (1, 0))] * 2 + [whole((PIECE, 2 * FF))] * 2,
+        + [whole(size)] * 2 + [whole((PIECE, 2 * FF))] * 2,
         out_specs=(whole((1, per, FF)), whole((1, per, FF)), whole((per, FF))),
         compiler_params=pltpu.CompilerParams(vmem_limit_bytes=VLIM),
+        cost_estimate=cost(CHUNK_COST),
         name="chunk",
     )(more, *arrived)
 
 
-def tail_kernel(sum_ref, ra_ref, rb_ref, out_ref):
+def tail_kernel(sum_ref, ra_ref, rb_ref, _, out_ref):
     for n, ref in enumerate((ra_ref, rb_ref)):
         side = slice(n * PIECE, (n + 1) * PIECE)
         for q in range(NFB):
@@ -425,16 +424,15 @@
             out_ref[0, cols, side] = (sum_ref[side, cols] + ref[:, cols].astype(f32)).astype(bf16)
 
 
-def tail(partial, ra, rb):
+def tail(partial, ra, rb, after):
     return pl.pallas_call(
         tail_kernel,
         out_shape=jax.ShapeDtypeStruct((1, FF, D // NDP), bf16),
-        in_specs=[VM] * 3,
+        in_specs=[VM] * 3 + [pl.BlockSpec(memory_space=pl.ANY)],
         out_specs=VM,
         compiler_params=pltpu.CompilerParams(vmem_limit_bytes=VLIM),
-        cost_estimate=cost(TAIL_COST),
         name="tail",
-    )(partial, ra, rb)
+    )(partial, ra, rb, after)
 
 
 def slots_kernel(pos_ref, g_ref, route_ref, wg_ref, wu_ref, out_ref):
@@ -469,7 +467,7 @@
 
 
 WIDE = 512
-TAIL_COST = 30_000_000_000
+CHUNK_COST = 30_000_000_000
 PICK_COST = 0
 FRONT_COST = 5_000_000_000
 
@@ -537,21 +535,23 @@
     own_c, sib_c = pick_cot(code, parts, after=code)
     sib_c = swap_core(sib_c)
 
-    pa, pb, g, route, scot = mid(pos, own_c, sib_c, hid, hid_t, a, b, weight, x_t, wd)
-    ra, rb = shift_dp(pa, 1), shift_dp(pb, -1)
+    p2a, p2b, p1b, p3a, g, route, scot = mid(
+        pos, own_c, sib_c, hid, hid_t, a, b, weight, x_t, wd
+    )
+    r1a, r1b = shift_dp(p2a, 1), shift_dp(p2b, -1)
+    r2b, r2a = shift_dp(p1b, 1), shift_dp(p3a, -1)
     out = slots(pos, g, route, wg, wu)
     got = lax.all_to_all(out, "ep", split_axis=0, concat_axis=0, tiled=True)
-    more = plain(pos, x_t, scot, g, hid_t)
+    more = plain(pos, x_t, scot, g, hid_t, after=r1a)
 
     def added(n, arrived, cols):
         mine = more[n * PIECE : (n + 1) * PIECE, cols].astype(f32)
-        return (mine + arrived[:PIECE, cols].astype(f32)).astype(bf16)
+        return (mine + arrived[:, cols].astype(f32)).astype(bf16)
 
     first, last = slice(0, 2 * FF), slice(2 * FF, 3 * FF)
-    r3a, r3b = shift_dp(added(0, ra, first), 1), shift_dp(added(1, rb, first), -1)
-    r3a_down, r3b_down = shift_dp(added(0, ra, last), 1), shift_dp(added(1, rb, last), -1)
-    grad_gate, grad_up, partial = chunk(more, rb, ra, r3a, r3b)
-    grad_down = tail(partial, r3a_down, r3b_down)
+    r3a, r3b = shift_dp(added(0, r1a, first), 1), shift_dp(added(1, r1b, first), -1)
+    r3a_down, r3b_down = shift_dp(added(0, r1a, last), 1), shift_dp(added(1, r1b, last), -1)
+    grad_gate, grad_up, partial = chunk(more, r2a, r2b, r3a, r3b)
 
     experts = NY * NZ * NC
     one = (expert_ids[:, :, None] == jnp.arange(experts, dtype=i32)).astype(i32)
@@ -567,6 +567,7 @@
     mine = sel[:, None, :] & (expert_ids[:, :, None] == (row // CAP)[None, None, :])
     grad_route = jnp.sum(jnp.where(mine, got[:, D].astype(f32), 0.0), axis=2).astype(bf16)
 
+    grad_down = tail(partial, r3a_down, r3b_down, after=grad_tokens)
     return grad_tokens, grad_route, grad_gate, grad_up, grad_down
 
 

time: 219 us -> 208 us (0.950)
  waiting for transfers between devices: 76 us -> 62.5 us
    ppermute x6 -> x8, waiting for transfers between devices: 41 us -> 26.2 us  [shift_dp(): return lax.ppermute(arr, 'dp', [(i, (i + by) % NDP) for i in range(NDP)])]
    ppermute x6 -> x8, starting transfers between devices: 7.83 us -> 9.58 us  [shift_dp(): return lax.ppermute(arr, 'dp', [(i, (i + by) % NDP) for i in range(NDP)])]
    unnamed x48 -> x50, local copies, waits for them, and re-layouts: 5.67 us -> 6.77 us
  transfers between devices with their start and end apart: 31 -> 33, of which waited for: 14 -> 15; matrix products, arithmetic and copies ran while one was open for 4% -> 5% of each run, Pallas kernels for 22% -> 22%
where the time goes in v3:
time: 208 us; the launch traced here: 206 us
  Pallas kernels  64.9 us (31%)
  waiting for transfers between devices  62.5 us (30%)
  starting transfers between devices  59.6 us (29%)
  local copies, waits for them, and re-layouts  9.93 us (5%)
  other arithmetic  7.29 us (4%)
    ppermute x22, waiting for transfers between devices, shift(): return lax.ppermute(arr, 'ep', pairs)  35 us
    ppermute x22, starting transfers between devices, shift(): return lax.ppermute(arr, 'ep', pairs)  32.5 us
    ppermute x8, waiting for transfers between devices, shift_dp(): return lax.ppermute(arr, 'dp', [(i, (i + by) % NDP) for i in range(NDP)])  26.2 us
    pallas_call x1, Pallas kernels, mid(): pl.pallas_call(mid_kernel, out_shape=(*[jax.ShapeDtypeStruct(size, bf16)]...  14.7 us
    pallas_call x1, Pallas kernels, slots(): pl.pallas_call(slots_kernel, grid=(D // WIDE,), out_shape=jax.ShapeDtypeS...  10.5 us
    all_to_all x1, starting transfers between devices, body(): got = lax.all_to_all(out, 'ep', split_axis=0, concat_axis=0, tiled=True)  10.1 us
    ppermute x8, starting transfers between devices, shift_dp(): return lax.ppermute(arr, 'dp', [(i, (i + by) % NDP) for i in range(NDP)])  9.58 us
    pallas_call x1, Pallas kernels, front(): pl.pallas_call(front_kernel, grid=(NFB,), out_shape=(jax.ShapeDtypeStruct...  9.28 us
  transfers between devices with their start and end apart: 33, of which 15 were waited for; matrix products, arithmetic and copies ran while one was open for 5% of the time, Pallas kernels for 22%

profile of v3, /device:TPU:1, one launch (start us, length us, event | category | flops | bytes accessed | tf_op | source)
XLA Modules:
  0.0 206.5 jit_solution(15479710203262470858)
XLA Ops:
  5.7 4.0 %collective-permute-start.1 = (bf16[32,2176]{1,0:T(8,128)(2,1)S(1)}, bf16[32,2176]{1,0:T(8,128)(2,1)S(1)}, u32[]{:S(2)}, u32[]{:S(2)}) collective-permute-start(bf16[32,2176]{1,0:T(8,128)(2,1)S(1)} %concatenate.3.refs_0_), channel_id=1, source_target_pairs={{0,56},{4,60},{8,0},{12,4},{16,8},{20,12},{24,16},{28,20},{32,24},... | collective-permute-start | bytes 417800 | tf_op jit(solution)/shard_map/ppermute | solution.py:52
  9.8 3.3 %collective-permute-done.refs_1_ = bf16[32,2176]{1,0:T(8,128)(2,1)S(1)} collective-permute-done((bf16[32,2176]{1,0:T(8,128)(2,1)S(1)}, bf16[32,2176]{1,0:T(8,128)(2,1)S(1)}, u32[]{:S(2)}, u32[]{:S(2)}) %collective-permute-start) | collective-permute-done | bytes 139296 | tf_op jit(solution)/shard_map/ppermute | solution.py:52
  23.3 2.7 %collective-permute-start.7 = (bf16[32,2048]{1,0:T(8,128)(2,1)}, bf16[32,2048]{1,0:T(8,128)(2,1)S(1)}, u32[]{:S(2)}, u32[]{:S(2)}) collective-permute-start(bf16[32,2048]{1,0:T(8,128)(2,1)} %refs_0_.1), channel_id=1, source_target_pairs={{0,192},{4,196},{8,200},{12,204},{16,208},{20,212},{24,216},{28,22... | collective-permute-start | bytes 393224 | tf_op jit(solution)/shard_map/ppermute | solution.py:52
  28.3 3.1 %collective-permute-done.9.refs_9_.refs_3_ = bf16[32,2048]{1,0:T(8,128)(2,1)S(1)} collective-permute-done((bf16[32,2048]{1,0:T(8,128)(2,1)S(1)}, bf16[32,2048]{1,0:T(8,128)(2,1)S(1)}, u32[]{:S(2)}, u32[]{:S(2)}) %collective-permute-start.9) | collective-permute-done | bytes 131104 | tf_op jit(solution)/shard_map/ppermute | solution.py:52
  42.5 7.1 %collective-permute-done.14.refs_1_ = bf16[128,2048]{1,0:T(8,128)(2,1)S(1)} collective-permute-done((bf16[128,2048]{1,0:T(8,128)(2,1)}, bf16[128,2048]{1,0:T(8,128)(2,1)S(1)}, u32[]{:S(2)}, u32[]{:S(2)}) %collective-permute-start.14) | collective-permute-done | bytes 524320 | tf_op jit(solution)/shard_map/ppermute | solution.py:52
  52.2 5.8 %collective-permute-done.10.refs_1_ = bf16[256,2176]{1,0:T(8,128)(2,1)S(1)} collective-permute-done((bf16[256,2176]{1,0:T(8,128)(2,1)}, bf16[256,2176]{1,0:T(8,128)(2,1)S(1)}, u32[]{:S(2)}, u32[]{:S(2)}) %collective-permute-start.10) | collective-permute-done | bytes 1114144 | tf_op jit(solution)/shard_map/ppermute | solution.py:52
  62.5 2.7 %collective-permute-start.19 = (bf16[128,2048]{1,0:T(8,128)(2,1)}, bf16[128,2048]{1,0:T(8,128)(2,1)S(1)}, u32[]{:S(2)}, u32[]{:S(2)}) collective-permute-start(bf16[128,2048]{1,0:T(8,128)(2,1)} %collective-permute-done.17.refs_4_), channel_id=1, source_target_pairs={{0,56},{4,60},{8,0},{12,4},{16,8},{20,12},{24,16},{28,20},{32,24},... | collective-permute-start | bytes 1572872 | tf_op jit(solution)/shard_map/ppermute | solution.py:52
  65.9 3.2 %collective-permute-done.12.refs_3_ = bf16[128,2176]{1,0:T(8,128)(2,1)} collective-permute-done((bf16[128,2176]{1,0:T(8,128)(2,1)}, bf16[128,2176]{1,0:T(8,128)(2,1)}, u32[]{:S(2)}, u32[]{:S(2)}) %collective-permute-start.12) | collective-permute-done | bytes 557088 | tf_op jit(solution)/shard_map/ppermute | solution.py:52
  69.3 6.3 %pick_x.1 = (bf16[256,2176]{1,0:T(8,128)(2,1)}, bf16[256,2176]{1,0:T(8,128)(2,1)}, bf16[4,256,128]{2,1,0:T(8,128)(2,1)}) custom-call(s32[2]{0:T(128)} %pad_add_fusion.me_ref.pos_ref, bf16[256,2176]{1,0:T(8,128)(2,1)} %join.2.refs_0_.refs_4_, bf16[256,2176]{1,0:T(8,128)(2,1)} %copy-done.1, bf16[256,2176]{1,0:T(8,128)(2,1)} %copy-done.2, ...), custom_call_target="tpu_custom_call" | custom-call | tf_op jit(solution)/shard_map/pick_x/pallas_call | solution.py:148
  75.6 6.8 %collective-permute-start.23 = (bf16[256,2176]{1,0:T(8,128)(2,1)}, bf16[256,2176]{1,0:T(8,128)(2,1)S(1)}, u32[]{:S(2)}, u32[]{:S(2)}) collective-permute-start(bf16[256,2176]{1,0:T(8,128)(2,1)} %get-tuple-element.30), channel_id=1, source_target_pairs={{0,4},{4,0},{8,12},{12,8},{16,20},{20,16},{24,28},{28,24},{32,36},... | collective-permute-start | bytes 3342344 | tf_op jit(solution)/shard_map/ppermute | solution.py:56
  82.5 3.0 %collective-permute-start.21 = (bf16[64,2048]{1,0:T(8,128)(2,1)S(1)}, bf16[64,2048]{1,0:T(8,128)(2,1)S(1)}, u32[]{:S(2)}, u32[]{:S(2)}) collective-permute-start(bf16[64,2048]{1,0:T(8,128)(2,1)S(1)} %slice.59), channel_id=1, source_target_pairs={{0,56},{4,60},{8,0},{12,4},{16,8},{20,12},{24,16},{28,20},{32,24},... | collective-permute-start | bytes 786440 | tf_op jit(solution)/shard_map/ppermute | solution.py:52
  85.6 6.5 %collective-permute-done.20.refs_7_ = bf16[64,2048]{1,0:T(8,128)(2,1)S(1)} collective-permute-done((bf16[64,2048]{1,0:T(8,128)(2,1)S(1)}, bf16[64,2048]{1,0:T(8,128)(2,1)S(1)}, u32[]{:S(2)}, u32[]{:S(2)}) %collective-permute-start.20) | collective-permute-done | bytes 262176 | tf_op jit(solution)/shard_map/ppermute | solution.py:52
  92.9 4.8 %pick_cot.1 = (bf16[256,2048]{1,0:T(8,128)(2,1)}, bf16[256,2048]{1,0:T(8,128)(2,1)}) custom-call(bf16[4,256,128]{2,1,0:T(8,128)(2,1)} %get-tuple-element.26.code_ref.refs_9_, bf16[128,2048]{1,0:T(8,128)(2,1)} %join.3.refs_0_, bf16[128,2048]{1,0:T(8,128)(2,1)} %copy-done.7, bf16[128,2048]{1,0:T(8,128)(2,1)} %copy-done.8, ...), custom_call_target="tpu_custom_call" | custom-call | tf_op jit(solution)/shard_map/pick_cot/pallas_call | solution.py:195
  99.4 9.3 %front.1 = (bf16[512,768]{1,0:T(8,128)(2,1)}, bf16[768,512]{1,0:T(8,128)(2,1)}, f32[512,768]{1,0:T(8,128)}, f32[512,768]{1,0:T(8,128)}, f32[512,128]{1,0:T(8,128)}, /*index=5*/bf16[2048,512]{1,0:T(8,128)(2,1)}) custom-call(s32[2]{0:T(128)} %pad_add_fusion.me_ref.pos_ref, bf16[256,2176]{1,0:T(8,128)(2,1)} %get-tuple-element.29.own_ref, ...), custom_call_target="tpu_custom_call" | custom-call | flops 5000000000 | tf_op jit(solution)/shard_map/front/pallas_call | solution.py:243
  109.7 14.7 %mid.1 = (bf16[256,2304]{1,0:T(8,128)(2,1)}, bf16[256,2304]{1,0:T(8,128)(2,1)}, bf16[256,2304]{1,0:T(8,128)(2,1)}, bf16[256,2304]{1,0:T(8,128)(2,1)}, bf16[2,512...) custom-call(s32[2]{0:T(128)} %pad_add_fusion.me_ref.pos_ref, ...), custom_call_target="tpu_custom_call" | custom-call | tf_op jit(solution)/shard_map/mid/pallas_call | solution.py:325
  127.1 10.5 %slots.1 = bf16[64,8,2176]{2,1,0:T(8,128)(2,1)} custom-call(s32[2]{0:T(128)} %pad_add_fusion.me_ref.pos_ref, bf16[2,512,768]{2,1,0:T(8,128)(2,1)} %get-tuple-element.37.g_ref, f32[512,128]{1,0:T(8,128)} %get-tuple-element.38.route_ref, bf16[2048,768]{1,0:T(8,128)(2,1)} %bitcast.14, bf16[2048,768]{1,0:T(8,128)(2,1)} %bitcast.16), custom_call_target="tpu_custom_call" | custom-call | tf_op jit(solution)/shard_map/slots/pallas_call | solution.py:477
  137.6 10.1 %all-to-all-start = ((bf16[64,8,2176]{2,1,0:T(8,128)(2,1)}), bf16[64,8,2176]{2,1,0:T(8,128)(2,1)S(1)}, u32[]{:S(2)}, u32[]{:S(2)}) async-start(bf16[64,8,2176]{2,1,0:T(8,128)(2,1)} %slots.1), calls=%async_computation | async-start | bytes 4456448 | tf_op jit(solution)/shard_map/all_to_all | solution.py:544
  149.4 4.0 %collective-permute-done.24._ = bf16[256,2304]{1,0:T(8,128)(2,1)S(1)} collective-permute-done((bf16[256,2304]{1,0:T(8,128)(2,1)}, bf16[256,2304]{1,0:T(8,128)(2,1)S(1)}, u32[]{:S(2)}, u32[]{:S(2)}) %collective-permute-start.24) | collective-permute-done | bytes 1179680 | tf_op jit(solution)/shard_map/ppermute | solution.py:60
  154.4 7.4 %plain.1.own_ref = bf16[1024,2304]{1,0:T(8,128)(2,1)} custom-call(s32[2]{0:T(128)} %pad_add_fusion.me_ref.pos_ref, bf16[2048,512]{1,0:T(8,128)(2,1)} %get-tuple-element.36.x_t_ref.x_ref, bf16[512,2048]{1,0:T(8,128)(2,1)} %get-tuple-element.39.c_ref, bf16[2,512,768]{2,1,0:T(8,128)(2,1)} %get-tuple-element.37.g_ref, ...), custom_call_target="tpu_custom_call" | custom-call | tf_op jit(solution)/shard_map/plain/pallas_call | solution.py:361
  161.8 3.1 %add_convert_fusion = (bf16[256,1536]{1,0:T(8,128)(2,1)S(1)}, bf16[256,1536]{1,0:T(8,128)(2,1)}) fusion(bf16[256,2304]{1,0:T(8,128)(2,1)} %collective-permute-done.28, bf16[1024,2304]{1,0:T(8,128)(2,1)} %plain.1.own_ref, bf16[256,2304]{1,0:T(8,128)(2,1)} %copy-done), kind=kLoop, calls=%fused_computation.2 | loop fusion | flops 3145728 | bytes 4718592 | tf_op jit(solution)/shard_map/convert_element_type | solution.py:549
  170.4 8.1 %collective-permute-done.25.r2a = bf16[256,2304]{1,0:T(8,128)(2,1)} collective-permute-done((bf16[256,2304]{1,0:T(8,128)(2,1)}, bf16[256,2304]{1,0:T(8,128)(2,1)}, u32[]{:S(2)}, u32[]{:S(2)}) %collective-permute-start.25) | collective-permute-done | bytes 1179680 | tf_op jit(solution)/shard_map/ppermute | solution.py:60
  178.5 2.7 %collective-permute-start.31 = (bf16[256,768]{1,0:T(8,128)(2,1)S(1)}, bf16[256,768]{1,0:T(8,128)(2,1)}, u32[]{:S(2)}, u32[]{:S(2)}) collective-permute-start(bf16[256,768]{1,0:T(8,128)(2,1)S(1)} %get-tuple-element.57), channel_id=1, source_target_pairs={{0,3},{1,0},{2,1},{3,2},{4,7},{5,4},{6,5},{7,6},{8,11},{9,8},{10,9... | collective-permute-start | bytes 1179656 | tf_op jit(solution)/shard_map/ppermute | solution.py:60
  181.2 14.1 %collective-permute-done.27.r3a = bf16[256,1536]{1,0:T(8,128)(2,1)} collective-permute-done((bf16[256,1536]{1,0:T(8,128)(2,1)}, bf16[256,1536]{1,0:T(8,128)(2,1)}, u32[]{:S(2)}, u32[]{:S(2)}) %collective-permute-start.27) | collective-permute-done | bytes 786464 | tf_op jit(solution)/shard_map/ppermute | solution.py:60
  195.3 5.0 %chunk.1 = (bf16[1,512,768]{2,1,0:T(8,128)(2,1)}, bf16[1,512,768]{2,1,0:T(8,128)(2,1)}, f32[512,768]{1,0:T(8,128)}) custom-call(bf16[1024,2304]{1,0:T(8,128)(2,1)} %plain.1.own_ref, bf16[256,2304]{1,0:T(8,128)(2,1)} %collective-permute-done.25.r2a, bf16[256,2304]{1,0:T(8,128)(2,1)} %collective-permute-done.26.r2b, ...), custom_call_target="tpu_custom_call" | custom-call | flops 30000001024 | tf_op jit(solution)/shard_map/chunk/pallas_call | solution.py:402
  (123 shorter events, 57.3 us)
Async XLA Ops:
  3.2 9.9 %collective-permute-start = (bf16[32,2176]{1,0:T(8,128)(2,1)S(1)}, bf16[32,2176]{1,0:T(8,128)(2,1)S(1)}, u32[]{:S(2)}, u32[]{:S(2)}) collective-permute-start(bf16[32,2176]{1,0:T(8,128)(2,1)S(1)} %concatenate.3.refs_0_), channel_id=1, source_target_pairs={{0,8},{4,12},{8,16},{12,20},{16,24},{20,28},{24,32},{28,36},{32,40... | collective-permute-start | bytes 417800 | tf_op jit(solution)/shard_map/ppermute | solution.py:52
  19.5 11.9 %collective-permute-start.5 = (bf16[32,2176]{1,0:T(8,128)(2,1)S(1)}, bf16[32,2176]{1,0:T(8,128)(2,1)S(1)}, u32[]{:S(2)}, u32[]{:S(2)}) collective-permute-start(bf16[32,2176]{1,0:T(8,128)(2,1)S(1)} %collective-permute-done.3.refs_4_), channel_id=1, source_target_pairs={{0,56},{4,60},{8,0},{12,4},{16,8},{20,12},{24,16},{28,20},{32,24},... | collective-permute-start | bytes 417800 | tf_op jit(solution)/shard_map/ppermute | solution.py:52
  35.2 22.8 %collective-permute-start.10 = (bf16[256,2176]{1,0:T(8,128)(2,1)}, bf16[256,2176]{1,0:T(8,128)(2,1)S(1)}, u32[]{:S(2)}, u32[]{:S(2)}) collective-permute-start(bf16[256,2176]{1,0:T(8,128)(2,1)} %join.2.refs_0_.refs_4_), channel_id=1, source_target_pairs={{0,64},{4,68},{8,72},{12,76},{16,80},{20,84},{24,88},{28,92},{32,9... | collective-permute-start | bytes 3342344 | tf_op jit(solution)/shard_map/ppermute | solution.py:52
  35.2 23.7 %collective-permute-start.11 = (bf16[256,2176]{1,0:T(8,128)(2,1)}, bf16[256,2176]{1,0:T(8,128)(2,1)S(1)}, u32[]{:S(2)}, u32[]{:S(2)}) collective-permute-start(bf16[256,2176]{1,0:T(8,128)(2,1)} %join.2.refs_0_.refs_4_), channel_id=1, source_target_pairs={{0,192},{4,196},{8,200},{12,204},{16,208},{20,212},{24,216},{28,22... | collective-permute-start | bytes 3342344 | tf_op jit(solution)/shard_map/ppermute | solution.py:52
  39.8 9.7 %collective-permute-start.14 = (bf16[128,2048]{1,0:T(8,128)(2,1)}, bf16[128,2048]{1,0:T(8,128)(2,1)S(1)}, u32[]{:S(2)}, u32[]{:S(2)}) collective-permute-start(bf16[128,2048]{1,0:T(8,128)(2,1)} %join.3.refs_0_), channel_id=1, source_target_pairs={{0,8},{4,12},{8,16},{12,20},{16,24},{20,28},{24,32},{28,36},{32,40... | collective-permute-start | bytes 1572872 | tf_op jit(solution)/shard_map/ppermute | solution.py:52
  39.8 9.8 %collective-permute-start.15 = (bf16[128,2048]{1,0:T(8,128)(2,1)}, bf16[128,2048]{1,0:T(8,128)(2,1)S(1)}, u32[]{:S(2)}, u32[]{:S(2)}) collective-permute-start(bf16[128,2048]{1,0:T(8,128)(2,1)} %join.3.refs_0_), channel_id=1, source_target_pairs={{0,56},{4,60},{8,0},{12,4},{16,8},{20,12},{24,16},{28,20},{32,24},... | collective-permute-start | bytes 1572872 | tf_op jit(solution)/shard_map/ppermute | solution.py:52
  49.5 13.0 %collective-permute-start.16 = (bf16[128,2048]{1,0:T(8,128)(2,1)S(1)}, bf16[128,2048]{1,0:T(8,128)(2,1)}, u32[]{:S(2)}, u32[]{:S(2)}) collective-permute-start(bf16[128,2048]{1,0:T(8,128)(2,1)S(1)} %collective-permute-done.14.refs_1_), channel_id=1, source_target_pairs={{0,8},{4,12},{8,16},{12,20},{16,24},{20,28},{24,32},{28,36},{32,40... | collective-permute-start | bytes 1572872 | tf_op jit(solution)/shard_map/ppermute | solution.py:52
  49.6 13.0 %collective-permute-start.17 = (bf16[128,2048]{1,0:T(8,128)(2,1)S(1)}, bf16[128,2048]{1,0:T(8,128)(2,1)}, u32[]{:S(2)}, u32[]{:S(2)}) collective-permute-start(bf16[128,2048]{1,0:T(8,128)(2,1)S(1)} %collective-permute-done.15.refs_2_), channel_id=1, source_target_pairs={{0,56},{4,60},{8,0},{12,4},{16,8},{20,12},{24,16},{28,20},{32,24},... | collective-permute-start | bytes 1572872 | tf_op jit(solution)/shard_map/ppermute | solution.py:52
  58.9 10.2 %collective-permute-start.12 = (bf16[128,2176]{1,0:T(8,128)(2,1)}, bf16[128,2176]{1,0:T(8,128)(2,1)}, u32[]{:S(2)}, u32[]{:S(2)}) collective-permute-start(bf16[128,2176]{1,0:T(8,128)(2,1)} %slice.56), channel_id=1, source_target_pairs={{0,64},{4,68},{8,72},{12,76},{16,80},{20,84},{24,88},{28,92},{32,9... | collective-permute-start | bytes 1671176 | tf_op jit(solution)/shard_map/ppermute | solution.py:52
  62.5 19.9 %collective-permute-start.18 = (bf16[128,2048]{1,0:T(8,128)(2,1)}, bf16[128,2048]{1,0:T(8,128)(2,1)S(1)}, u32[]{:S(2)}, u32[]{:S(2)}) collective-permute-start(bf16[128,2048]{1,0:T(8,128)(2,1)} %collective-permute-done.16.refs_3_), channel_id=1, source_target_pairs={{0,8},{4,12},{8,16},{12,20},{16,24},{20,28},{24,32},{28,36},{32,40... | collective-permute-start | bytes 1572872 | tf_op jit(solution)/shard_map/ppermute | solution.py:52
  62.5 19.9 %collective-permute-start.19 = (bf16[128,2048]{1,0:T(8,128)(2,1)}, bf16[128,2048]{1,0:T(8,128)(2,1)S(1)}, u32[]{:S(2)}, u32[]{:S(2)}) collective-permute-start(bf16[128,2048]{1,0:T(8,128)(2,1)} %collective-permute-done.17.refs_4_), channel_id=1, source_target_pairs={{0,56},{4,60},{8,0},{12,4},{16,8},{20,12},{24,16},{28,20},{32,24},... | collective-permute-start | bytes 1572872 | tf_op jit(solution)/shard_map/ppermute | solution.py:52
  75.6 22.7 %collective-permute-start.23 = (bf16[256,2176]{1,0:T(8,128)(2,1)}, bf16[256,2176]{1,0:T(8,128)(2,1)S(1)}, u32[]{:S(2)}, u32[]{:S(2)}) collective-permute-start(bf16[256,2176]{1,0:T(8,128)(2,1)} %get-tuple-element.30), channel_id=1, source_target_pairs={{0,4},{4,0},{8,12},{12,8},{16,20},{20,16},{24,28},{28,24},{32,36},... | collective-permute-start | bytes 3342344 | tf_op jit(solution)/shard_map/ppermute | solution.py:56
  82.4 9.7 %collective-permute-start.20 = (bf16[64,2048]{1,0:T(8,128)(2,1)S(1)}, bf16[64,2048]{1,0:T(8,128)(2,1)S(1)}, u32[]{:S(2)}, u32[]{:S(2)}) collective-permute-start(bf16[64,2048]{1,0:T(8,128)(2,1)S(1)} %slice.58), channel_id=1, source_target_pairs={{0,8},{4,12},{8,16},{12,20},{16,24},{20,28},{24,32},{28,36},{32,40... | collective-permute-start | bytes 786440 | tf_op jit(solution)/shard_map/ppermute | solution.py:52
  82.5 9.6 %collective-permute-start.21 = (bf16[64,2048]{1,0:T(8,128)(2,1)S(1)}, bf16[64,2048]{1,0:T(8,128)(2,1)S(1)}, u32[]{:S(2)}, u32[]{:S(2)}) collective-permute-start(bf16[64,2048]{1,0:T(8,128)(2,1)S(1)} %slice.59), channel_id=1, source_target_pairs={{0,56},{4,60},{8,0},{12,4},{16,8},{20,12},{24,16},{28,20},{32,24},... | collective-permute-start | bytes 786440 | tf_op jit(solution)/shard_map/ppermute | solution.py:52
  97.7 10.9 %collective-permute-start.22 = (bf16[256,2048]{1,0:T(8,128)(2,1)}, bf16[256,2048]{1,0:T(8,128)(2,1)S(1)}, u32[]{:S(2)}, u32[]{:S(2)}) collective-permute-start(bf16[256,2048]{1,0:T(8,128)(2,1)} %get-tuple-element.28), channel_id=1, source_target_pairs={{0,4},{4,0},{8,12},{12,8},{16,20},{20,16},{24,28},{28,24},{32,36},... | collective-permute-start | bytes 3145736 | tf_op jit(solution)/shard_map/ppermute | solution.py:56
  124.4 29.0 %collective-permute-start.24 = (bf16[256,2304]{1,0:T(8,128)(2,1)}, bf16[256,2304]{1,0:T(8,128)(2,1)S(1)}, u32[]{:S(2)}, u32[]{:S(2)}) collective-permute-start(bf16[256,2304]{1,0:T(8,128)(2,1)} %get-tuple-element.40), channel_id=1, source_target_pairs={{0,1},{1,2},{2,3},{3,0},{4,5},{5,6},{6,7},{7,4},{8,9},{9,10},{10,1... | collective-permute-start | bytes 3538952 | tf_op jit(solution)/shard_map/ppermute | solution.py:60
  125.6 36.2 %collective-permute-start.28 = (bf16[256,2304]{1,0:T(8,128)(2,1)}, bf16[256,2304]{1,0:T(8,128)(2,1)}, u32[]{:S(2)}, u32[]{:S(2)}) collective-permute-start(bf16[256,2304]{1,0:T(8,128)(2,1)} %get-tuple-element.43), channel_id=1, source_target_pairs={{0,3},{1,0},{2,1},{3,2},{4,7},{5,4},{6,5},{7,6},{8,11},{9,8},{10,9... | collective-permute-start | bytes 3538952 | tf_op jit(solution)/shard_map/ppermute | solution.py:60
  137.6 64.0 %all-to-all-start = ((bf16[64,8,2176]{2,1,0:T(8,128)(2,1)}), bf16[64,8,2176]{2,1,0:T(8,128)(2,1)S(1)}, u32[]{:S(2)}, u32[]{:S(2)}) async-start(bf16[64,8,2176]{2,1,0:T(8,128)(2,1)} %slots.1), calls=%async_computation | async-start | bytes 4456448 | tf_op jit(solution)/shard_map/all_to_all | solution.py:544
  147.9 30.6 %collective-permute-start.25 = (bf16[256,2304]{1,0:T(8,128)(2,1)}, bf16[256,2304]{1,0:T(8,128)(2,1)}, u32[]{:S(2)}, u32[]{:S(2)}) collective-permute-start(bf16[256,2304]{1,0:T(8,128)(2,1)} %get-tuple-element.41), channel_id=1, source_target_pairs={{0,3},{1,0},{2,1},{3,2},{4,7},{5,4},{6,5},{7,6},{8,11},{9,8},{10,9... | collective-permute-start | bytes 3538952 | tf_op jit(solution)/shard_map/ppermute | solution.py:60
  149.2 31.9 %collective-permute-start.26 = (bf16[256,2304]{1,0:T(8,128)(2,1)}, bf16[256,2304]{1,0:T(8,128)(2,1)}, u32[]{:S(2)}, u32[]{:S(2)}) collective-permute-start(bf16[256,2304]{1,0:T(8,128)(2,1)} %get-tuple-element.42), channel_id=1, source_target_pairs={{0,1},{1,2},{2,3},{3,0},{4,5},{5,6},{6,7},{7,4},{8,9},{9,10},{10,1... | collective-permute-start | bytes 3538952 | tf_op jit(solution)/shard_map/ppermute | solution.py:60
  164.9 30.3 %collective-permute-start.27 = (bf16[256,1536]{1,0:T(8,128)(2,1)}, bf16[256,1536]{1,0:T(8,128)(2,1)}, u32[]{:S(2)}, u32[]{:S(2)}) collective-permute-start(bf16[256,1536]{1,0:T(8,128)(2,1)} %get-tuple-element.60), channel_id=1, source_target_pairs={{0,1},{1,2},{2,3},{3,0},{4,5},{5,6},{6,7},{7,4},{8,9},{9,10},{10,1... | collective-permute-start | bytes 2359304 | tf_op jit(solution)/shard_map/ppermute | solution.py:60
  165.0 30.3 %collective-permute-start.29 = (bf16[256,1536]{1,0:T(8,128)(2,1)S(1)}, bf16[256,1536]{1,0:T(8,128)(2,1)}, u32[]{:S(2)}, u32[]{:S(2)}) collective-permute-start(bf16[256,1536]{1,0:T(8,128)(2,1)S(1)} %get-tuple-element.59), channel_id=1, source_target_pairs={{0,3},{1,0},{2,1},{3,2},{4,7},{5,4},{6,5},{7,6},{8,11},{9,8},{10,9... | collective-permute-start | bytes 2359304 | tf_op jit(solution)/shard_map/ppermute | solution.py:60
  170.4 33.5 %collective-permute-start.30 = (bf16[256,768]{1,0:T(8,128)(2,1)}, bf16[256,768]{1,0:T(8,128)(2,1)}, u32[]{:S(2)}, u32[]{:S(2)}) collective-permute-start(bf16[256,768]{1,0:T(8,128)(2,1)} %get-tuple-element.58), channel_id=1, source_target_pairs={{0,1},{1,2},{2,3},{3,0},{4,5},{5,6},{6,7},{7,4},{8,9},{9,10},{10,1... | collective-permute-start | bytes 1179656 | tf_op jit(solution)/shard_map/ppermute | solution.py:60
  178.5 25.4 %collective-permute-start.31 = (bf16[256,768]{1,0:T(8,128)(2,1)S(1)}, bf16[256,768]{1,0:T(8,128)(2,1)}, u32[]{:S(2)}, u32[]{:S(2)}) collective-permute-start(bf16[256,768]{1,0:T(8,128)(2,1)S(1)} %get-tuple-element.57), channel_id=1, source_target_pairs={{0,3},{1,0},{2,1},{3,2},{4,7},{5,4},{6,5},{7,6},{8,11},{9,8},{10,9... | collective-permute-start | bytes 1179656 | tf_op jit(solution)/shard_map/ppermute | solution.py:60
  (32 other events, 263.8 us)

commit v4 on v3

--- a/solution.py
+++ b/solution.py
@@ -158,6 +158,7 @@
             pltpu.VMEM((NY * NZ * TOK, META), bf16), pltpu.VMEM((NY * NZ * TOK, META), bf16),
         ],
         compiler_params=pltpu.CompilerParams(vmem_limit_bytes=VLIM),
+        cost_estimate=cost(0),
         name="pick_x",
     )(me, *blocks)
 
@@ -468,7 +469,7 @@
 
 WIDE = 512
 CHUNK_COST = 30_000_000_000
-PICK_COST = 0
+PICK_COST = 5_000_000_000
 FRONT_COST = 5_000_000_000
 
 
@@ -507,11 +508,11 @@
         d.append(shift(d[-1], dz=-1))
     u.append(shift(u[-1], dz=1))
 
-    x0 = join([xa, u[1], d[1], u[2], d[2], u[3], d[3], u[4]], after=[c2, c3])
+    cot0 = join([cotangent, c1, c2, c3], after=[u[3], d[3]])
+    x0 = join([xa, u[1], d[1], u[2], d[2], u[3], d[3], u[4]], after=[cot0])
     p1 = shift(x0, dy=1)
     m1 = shift(x0, dy=-1)
 
-    cot0 = join([cotangent, c1, c2, c3], after=[x0])
     cu = [cot0]
     cd = [cot0]
     for _ in range(3):

time: 208 us -> 200 us (0.962)
  waiting for transfers between devices: 62.5 us -> 53.6 us
  local copies, waits for them, and re-layouts: 9.93 us -> 12.9 us
    ppermute x22, waiting for transfers between devices: 35 us -> 25.9 us  [shift(): return lax.ppermute(arr, 'ep', pairs)]
    unnamed x50 -> x54, local copies, waits for them, and re-layouts: 6.77 us -> 8.25 us
  transfers between devices with their start and end apart: 33 -> 33, of which waited for: 15 -> 13; matrix products, arithmetic and copies ran while one was open for 5% -> 6% of each run, Pallas kernels for 22% -> 24%
where the time goes in v4:
time: 200 us; the launch traced here: 199 us
  Pallas kernels  65 us (32%)
  starting transfers between devices  58.3 us (29%)
  waiting for transfers between devices  53.6 us (27%)
  local copies, waits for them, and re-layouts  12.9 us (6%)
  other arithmetic  7.27 us (4%)
    ppermute x22, starting transfers between devices, shift(): return lax.ppermute(arr, 'ep', pairs)  32.1 us
    ppermute x8, waiting for transfers between devices, shift_dp(): return lax.ppermute(arr, 'dp', [(i, (i + by) % NDP) for i in range(NDP)])  26.7 us
    ppermute x22, waiting for transfers between devices, shift(): return lax.ppermute(arr, 'ep', pairs)  25.9 us
    pallas_call x1, Pallas kernels, mid(): pl.pallas_call(mid_kernel, out_shape=(*[jax.ShapeDtypeStruct(size, bf16)]...  14.7 us
    pallas_call x1, Pallas kernels, slots(): pl.pallas_call(slots_kernel, grid=(D // WIDE,), out_shape=jax.ShapeDtypeS...  10.5 us
    all_to_all x1, starting transfers between devices, body(): got = lax.all_to_all(out, 'ep', split_axis=0, concat_axis=0, tiled=True)  9.92 us
    ppermute x8, starting transfers between devices, shift_dp(): return lax.ppermute(arr, 'dp', [(i, (i + by) % NDP) for i in range(NDP)])  9.58 us
    pallas_call x1, Pallas kernels, front(): pl.pallas_call(front_kernel, grid=(NFB,), out_shape=(jax.ShapeDtypeStruct...  9.36 us
  transfers between devices with their start and end apart: 33, of which 13 were waited for; matrix products, arithmetic and copies ran while one was open for 6% of the time, Pallas kernels for 24%

profile of v4, /device:TPU:1, one launch (start us, length us, event | category | flops | bytes accessed | tf_op | source)
XLA Modules:
  0.0 199.3 jit_solution(2396215990591866609)
XLA Ops:
  5.7 4.0 %collective-permute-start.1 = (bf16[32,2176]{1,0:T(8,128)(2,1)S(1)}, bf16[32,2176]{1,0:T(8,128)(2,1)S(1)}, u32[]{:S(2)}, u32[]{:S(2)}) collective-permute-start(bf16[32,2176]{1,0:T(8,128)(2,1)S(1)} %concatenate.3.refs_0_), channel_id=1, source_target_pairs={{0,56},{4,60},{8,0},{12,4},{16,8},{20,12},{24,16},{28,20},{32,24},... | collective-permute-start | bytes 417800 | tf_op jit(solution)/shard_map/ppermute | solution.py:52
  9.8 3.3 %collective-permute-done.refs_1_ = bf16[32,2176]{1,0:T(8,128)(2,1)S(1)} collective-permute-done((bf16[32,2176]{1,0:T(8,128)(2,1)S(1)}, bf16[32,2176]{1,0:T(8,128)(2,1)S(1)}, u32[]{:S(2)}, u32[]{:S(2)}) %collective-permute-start) | collective-permute-done | bytes 139296 | tf_op jit(solution)/shard_map/ppermute | solution.py:52
  20.9 2.7 %collective-permute-start.8 = (bf16[32,2048]{1,0:T(8,128)(2,1)}, bf16[32,2048]{1,0:T(8,128)(2,1)S(1)}, u32[]{:S(2)}, u32[]{:S(2)}) collective-permute-start(bf16[32,2048]{1,0:T(8,128)(2,1)} %refs_0_.1), channel_id=1, source_target_pairs={{0,192},{4,196},{8,200},{12,204},{16,208},{20,212},{24,216},{28,22... | collective-permute-start | bytes 393224 | tf_op jit(solution)/shard_map/ppermute | solution.py:52
  25.9 2.8 %collective-permute-done.9.refs_3_ = bf16[32,2048]{1,0:T(8,128)(2,1)S(1)} collective-permute-done((bf16[32,2048]{1,0:T(8,128)(2,1)S(1)}, bf16[32,2048]{1,0:T(8,128)(2,1)S(1)}, u32[]{:S(2)}, u32[]{:S(2)}) %collective-permute-start.9) | collective-permute-done | bytes 131104 | tf_op jit(solution)/shard_map/ppermute | solution.py:52
  31.9 2.7 %collective-permute-start.15 = (bf16[128,2048]{1,0:T(8,128)(2,1)}, bf16[128,2048]{1,0:T(8,128)(2,1)S(1)}, u32[]{:S(2)}, u32[]{:S(2)}) collective-permute-start(bf16[128,2048]{1,0:T(8,128)(2,1)} %join.2.refs_8_.refs_0_), channel_id=1, source_target_pairs={{0,56},{4,60},{8,0},{12,4},{16,8},{20,12},{24,16},{28,20},{32,24},... | collective-permute-start | bytes 1572872 | tf_op jit(solution)/shard_map/ppermute | solution.py:52
  37.7 2.7 %collective-permute-start.11 = (bf16[256,2176]{1,0:T(8,128)(2,1)}, bf16[256,2176]{1,0:T(8,128)(2,1)S(1)}, u32[]{:S(2)}, u32[]{:S(2)}) collective-permute-start(bf16[256,2176]{1,0:T(8,128)(2,1)} %join.3.refs_0_), channel_id=1, source_target_pairs={{0,192},{4,196},{8,200},{12,204},{16,208},{20,212},{24,216},{28,22... | collective-permute-start | bytes 3342344 | tf_op jit(solution)/shard_map/ppermute | solution.py:52
  45.0 7.8 %collective-permute-done.16.refs_3_ = bf16[128,2048]{1,0:T(8,128)(2,1)S(1)} collective-permute-done((bf16[128,2048]{1,0:T(8,128)(2,1)S(1)}, bf16[128,2048]{1,0:T(8,128)(2,1)S(1)}, u32[]{:S(2)}, u32[]{:S(2)}) %collective-permute-start.16) | collective-permute-done | bytes 524320 | tf_op jit(solution)/shard_map/ppermute | solution.py:52
  55.5 4.7 %collective-permute-done.10.refs_1_ = bf16[256,2176]{1,0:T(8,128)(2,1)S(1)} collective-permute-done((bf16[256,2176]{1,0:T(8,128)(2,1)}, bf16[256,2176]{1,0:T(8,128)(2,1)S(1)}, u32[]{:S(2)}, u32[]{:S(2)}) %collective-permute-start.10) | collective-permute-done | bytes 1114144 | tf_op jit(solution)/shard_map/ppermute | solution.py:52
  62.1 2.7 %collective-permute-start.13 = (bf16[128,2176]{1,0:T(8,128)(2,1)}, bf16[128,2176]{1,0:T(8,128)(2,1)S(1)}, u32[]{:S(2)}, u32[]{:S(2)}) collective-permute-start(bf16[128,2176]{1,0:T(8,128)(2,1)} %slice.57), channel_id=1, source_target_pairs={{0,192},{4,196},{8,200},{12,204},{16,208},{20,212},{24,216},{28,22... | collective-permute-start | bytes 1671176 | tf_op jit(solution)/shard_map/ppermute | solution.py:52
  66.3 2.7 %collective-permute-start.21 = (bf16[64,2048]{1,0:T(8,128)(2,1)}, bf16[64,2048]{1,0:T(8,128)(2,1)}, u32[]{:S(2)}, u32[]{:S(2)}) collective-permute-start(bf16[64,2048]{1,0:T(8,128)(2,1)} %slice.59), channel_id=1, source_target_pairs={{0,56},{4,60},{8,0},{12,4},{16,8},{20,12},{24,16},{28,20},{32,24},... | collective-permute-start | bytes 786440 | tf_op jit(solution)/shard_map/ppermute | solution.py:52
  73.2 6.3 %pick_x.1 = (bf16[256,2176]{1,0:T(8,128)(2,1)}, bf16[256,2176]{1,0:T(8,128)(2,1)}, bf16[4,256,128]{2,1,0:T(8,128)(2,1)}) custom-call(s32[2]{0:T(128)} %pad_add_fusion.me_ref.pos_ref, bf16[256,2176]{1,0:T(8,128)(2,1)} %join.3.refs_0_, bf16[256,2176]{1,0:T(8,128)(2,1)} %copy-done.1, bf16[256,2176]{1,0:T(8,128)(2,1)} %copy-done.2, bf16[128,2176]{1,0:T(8,128)(2,1)} %copy-done.4, ...), custom_call_target="tpu_custom_call" | custom-call | tf_op jit(solution)/shard_map/pick_x/pallas_call | solution.py:148
  79.5 6.7 %collective-permute-start.23 = (bf16[256,2176]{1,0:T(8,128)(2,1)}, bf16[256,2176]{1,0:T(8,128)(2,1)S(1)}, u32[]{:S(2)}, u32[]{:S(2)}) collective-permute-start(bf16[256,2176]{1,0:T(8,128)(2,1)} %get-tuple-element.30), channel_id=1, source_target_pairs={{0,4},{4,0},{8,12},{12,8},{16,20},{20,16},{24,28},{28,24},{32,36},... | collective-permute-start | bytes 3342344 | tf_op jit(solution)/shard_map/ppermute | solution.py:56
  86.2 4.8 %pick_cot.1 = (bf16[256,2048]{1,0:T(8,128)(2,1)}, bf16[256,2048]{1,0:T(8,128)(2,1)}) custom-call(bf16[4,256,128]{2,1,0:T(8,128)(2,1)} %get-tuple-element.26.code_ref.refs_9_, bf16[128,2048]{1,0:T(8,128)(2,1)} %join.2.refs_8_.refs_0_, bf16[128,2048]{1,0:T(8,128)(2,1)} %copy-done.21, bf16[128,2048]{1,0:T(8,128)(2,1)} %copy-done.22, ...), custom_call_target="tpu_custom_call" | custom-call | flops 5000000000 | tf_op jit(solution)/shard_map/pick_cot/pallas_call | solution.py:196
  92.0 9.4 %front.1 = (bf16[512,768]{1,0:T(8,128)(2,1)}, bf16[768,512]{1,0:T(8,128)(2,1)}, f32[512,768]{1,0:T(8,128)}, f32[512,768]{1,0:T(8,128)}, f32[512,128]{1,0:T(8,128)}, /*index=5*/bf16[2048,512]{1,0:T(8,128)(2,1)}) custom-call(s32[2]{0:T(128)} %pad_add_fusion.me_ref.pos_ref, bf16[256,2176]{1,0:T(8,128)(2,1)} %get-tuple-element.29.own_ref, ...), custom_call_target="tpu_custom_call" | custom-call | flops 5000000000 | tf_op jit(solution)/shard_map/front/pallas_call | solution.py:244
  102.4 14.7 %mid.1 = (bf16[256,2304]{1,0:T(8,128)(2,1)}, bf16[256,2304]{1,0:T(8,128)(2,1)}, bf16[256,2304]{1,0:T(8,128)(2,1)}, bf16[256,2304]{1,0:T(8,128)(2,1)}, bf16[2,512...) custom-call(s32[2]{0:T(128)} %pad_add_fusion.me_ref.pos_ref, ...), custom_call_target="tpu_custom_call" | custom-call | tf_op jit(solution)/shard_map/mid/pallas_call | solution.py:326
  119.9 10.5 %slots.1 = bf16[64,8,2176]{2,1,0:T(8,128)(2,1)} custom-call(s32[2]{0:T(128)} %pad_add_fusion.me_ref.pos_ref, bf16[2,512,768]{2,1,0:T(8,128)(2,1)} %get-tuple-element.37.g_ref, f32[512,128]{1,0:T(8,128)} %get-tuple-element.38.route_ref, bf16[2048,768]{1,0:T(8,128)(2,1)} %bitcast.14, bf16[2048,768]{1,0:T(8,128)(2,1)} %bitcast.16), custom_call_target="tpu_custom_call" | custom-call | tf_op jit(solution)/shard_map/slots/pallas_call | solution.py:478
  130.4 9.9 %all-to-all-start = ((bf16[64,8,2176]{2,1,0:T(8,128)(2,1)}), bf16[64,8,2176]{2,1,0:T(8,128)(2,1)S(1)}, u32[]{:S(2)}, u32[]{:S(2)}) async-start(bf16[64,8,2176]{2,1,0:T(8,128)(2,1)} %slots.1), calls=%async_computation | async-start | bytes 4456448 | tf_op jit(solution)/shard_map/all_to_all | solution.py:545
  142.0 3.6 %collective-permute-done.24._ = bf16[256,2304]{1,0:T(8,128)(2,1)S(1)} collective-permute-done((bf16[256,2304]{1,0:T(8,128)(2,1)}, bf16[256,2304]{1,0:T(8,128)(2,1)S(1)}, u32[]{:S(2)}, u32[]{:S(2)}) %collective-permute-start.24) | collective-permute-done | bytes 1179680 | tf_op jit(solution)/shard_map/ppermute | solution.py:60
  146.7 7.4 %plain.1.own_ref = bf16[1024,2304]{1,0:T(8,128)(2,1)} custom-call(s32[2]{0:T(128)} %pad_add_fusion.me_ref.pos_ref, bf16[2048,512]{1,0:T(8,128)(2,1)} %get-tuple-element.36.x_t_ref.x_ref, bf16[512,2048]{1,0:T(8,128)(2,1)} %get-tuple-element.39.c_ref, bf16[2,512,768]{2,1,0:T(8,128)(2,1)} %get-tuple-element.37.g_ref, ...), custom_call_target="tpu_custom_call" | custom-call | tf_op jit(solution)/shard_map/plain/pallas_call | solution.py:362
  154.1 3.1 %add_convert_fusion = (bf16[256,1536]{1,0:T(8,128)(2,1)S(1)}, bf16[256,1536]{1,0:T(8,128)(2,1)}) fusion(bf16[256,2304]{1,0:T(8,128)(2,1)} %collective-permute-done.28, bf16[1024,2304]{1,0:T(8,128)(2,1)} %plain.1.own_ref, bf16[256,2304]{1,0:T(8,128)(2,1)} %copy-done), kind=kLoop, calls=%fused_computation.2 | loop fusion | flops 3145728 | bytes 4718592 | tf_op jit(solution)/shard_map/convert_element_type | solution.py:550
  162.7 8.0 %collective-permute-done.25.r2a = bf16[256,2304]{1,0:T(8,128)(2,1)} collective-permute-done((bf16[256,2304]{1,0:T(8,128)(2,1)}, bf16[256,2304]{1,0:T(8,128)(2,1)}, u32[]{:S(2)}, u32[]{:S(2)}) %collective-permute-start.25) | collective-permute-done | bytes 1179680 | tf_op jit(solution)/shard_map/ppermute | solution.py:60
  170.7 2.7 %collective-permute-start.31 = (bf16[256,768]{1,0:T(8,128)(2,1)S(1)}, bf16[256,768]{1,0:T(8,128)(2,1)}, u32[]{:S(2)}, u32[]{:S(2)}) collective-permute-start(bf16[256,768]{1,0:T(8,128)(2,1)S(1)} %get-tuple-element.57), channel_id=1, source_target_pairs={{0,3},{1,0},{2,1},{3,2},{4,7},{5,4},{6,5},{7,6},{8,11},{9,8},{10,9... | collective-permute-start | bytes 1179656 | tf_op jit(solution)/shard_map/ppermute | solution.py:60
  173.4 14.8 %collective-permute-done.27.r3a = bf16[256,1536]{1,0:T(8,128)(2,1)} collective-permute-done((bf16[256,1536]{1,0:T(8,128)(2,1)}, bf16[256,1536]{1,0:T(8,128)(2,1)}, u32[]{:S(2)}, u32[]{:S(2)}) %collective-permute-start.27) | collective-permute-done | bytes 786464 | tf_op jit(solution)/shard_map/ppermute | solution.py:60
  188.2 5.0 %chunk.1 = (bf16[1,512,768]{2,1,0:T(8,128)(2,1)}, bf16[1,512,768]{2,1,0:T(8,128)(2,1)}, f32[512,768]{1,0:T(8,128)}) custom-call(bf16[1024,2304]{1,0:T(8,128)(2,1)} %plain.1.own_ref, bf16[256,2304]{1,0:T(8,128)(2,1)} %collective-permute-done.25.r2a, bf16[256,2304]{1,0:T(8,128)(2,1)} %collective-permute-done.26.r2b, ...), custom_call_target="tpu_custom_call" | custom-call | flops 30000001024 | tf_op jit(solution)/shard_map/chunk/pallas_call | solution.py:403
  (127 shorter events, 55.4 us)
Async XLA Ops:
  18.2 10.4 %collective-permute-start.5 = (bf16[32,2176]{1,0:T(8,128)(2,1)S(1)}, bf16[32,2176]{1,0:T(8,128)(2,1)S(1)}, u32[]{:S(2)}, u32[]{:S(2)}) collective-permute-start(bf16[32,2176]{1,0:T(8,128)(2,1)S(1)} %collective-permute-done.3.refs_4_), channel_id=1, source_target_pairs={{0,56},{4,60},{8,0},{12,4},{16,8},{20,12},{24,16},{28,20},{32,24},... | collective-permute-start | bytes 417800 | tf_op jit(solution)/shard_map/ppermute | solution.py:52
  23.6 10.9 %collective-permute-start.6 = (bf16[32,2176]{1,0:T(8,128)(2,1)S(1)}, bf16[32,2176]{1,0:T(8,128)(2,1)S(1)}, u32[]{:S(2)}, u32[]{:S(2)}) collective-permute-start(bf16[32,2176]{1,0:T(8,128)(2,1)S(1)} %collective-permute-done.4.refs_4_.refs_5_), channel_id=1, source_target_pairs={{0,8},{4,12},{8,16},{12,20},{16,24},{20,28},{24,32},{28,36},{32,40... | collective-permute-start | bytes 417800 | tf_op jit(solution)/shard_map/ppermute | solution.py:52
  31.9 10.5 %collective-permute-start.14 = (bf16[128,2048]{1,0:T(8,128)(2,1)}, bf16[128,2048]{1,0:T(8,128)(2,1)S(1)}, u32[]{:S(2)}, u32[]{:S(2)}) collective-permute-start(bf16[128,2048]{1,0:T(8,128)(2,1)} %join.2.refs_8_.refs_0_), channel_id=1, source_target_pairs={{0,8},{4,12},{8,16},{12,20},{16,24},{20,28},{24,32},{28,36},{32,40... | collective-permute-start | bytes 1572872 | tf_op jit(solution)/shard_map/ppermute | solution.py:52
  31.9 10.5 %collective-permute-start.15 = (bf16[128,2048]{1,0:T(8,128)(2,1)}, bf16[128,2048]{1,0:T(8,128)(2,1)S(1)}, u32[]{:S(2)}, u32[]{:S(2)}) collective-permute-start(bf16[128,2048]{1,0:T(8,128)(2,1)} %join.2.refs_8_.refs_0_), channel_id=1, source_target_pairs={{0,56},{4,60},{8,0},{12,4},{16,8},{20,12},{24,16},{28,20},{32,24},... | collective-permute-start | bytes 1572872 | tf_op jit(solution)/shard_map/ppermute | solution.py:52
  37.7 22.5 %collective-permute-start.10 = (bf16[256,2176]{1,0:T(8,128)(2,1)}, bf16[256,2176]{1,0:T(8,128)(2,1)S(1)}, u32[]{:S(2)}, u32[]{:S(2)}) collective-permute-start(bf16[256,2176]{1,0:T(8,128)(2,1)} %join.3.refs_0_), channel_id=1, source_target_pairs={{0,64},{4,68},{8,72},{12,76},{16,80},{20,84},{24,88},{28,92},{32,9... | collective-permute-start | bytes 3342344 | tf_op jit(solution)/shard_map/ppermute | solution.py:52
  37.7 23.5 %collective-permute-start.11 = (bf16[256,2176]{1,0:T(8,128)(2,1)}, bf16[256,2176]{1,0:T(8,128)(2,1)S(1)}, u32[]{:S(2)}, u32[]{:S(2)}) collective-permute-start(bf16[256,2176]{1,0:T(8,128)(2,1)} %join.3.refs_0_), channel_id=1, source_target_pairs={{0,192},{4,196},{8,200},{12,204},{16,208},{20,212},{24,216},{28,22... | collective-permute-start | bytes 3342344 | tf_op jit(solution)/shard_map/ppermute | solution.py:52
  42.3 10.5 %collective-permute-start.16 = (bf16[128,2048]{1,0:T(8,128)(2,1)S(1)}, bf16[128,2048]{1,0:T(8,128)(2,1)S(1)}, u32[]{:S(2)}, u32[]{:S(2)}) collective-permute-start(bf16[128,2048]{1,0:T(8,128)(2,1)S(1)} %collective-permute-done.14.refs_1_), channel_id=1, source_target_pairs={{0,8},{4,12},{8,16},{12,20},{16,24},{20,28},{24,32},{28,36},{32,40... | collective-permute-start | bytes 1572872 | tf_op jit(solution)/shard_map/ppermute | solution.py:52
  42.4 10.5 %collective-permute-start.17 = (bf16[128,2048]{1,0:T(8,128)(2,1)S(1)}, bf16[128,2048]{1,0:T(8,128)(2,1)S(1)}, u32[]{:S(2)}, u32[]{:S(2)}) collective-permute-start(bf16[128,2048]{1,0:T(8,128)(2,1)S(1)} %collective-permute-done.15.refs_2_), channel_id=1, source_target_pairs={{0,56},{4,60},{8,0},{12,4},{16,8},{20,12},{24,16},{28,20},{32,24},... | collective-permute-start | bytes 1572872 | tf_op jit(solution)/shard_map/ppermute | solution.py:52
  52.9 11.9 %collective-permute-start.18 = (bf16[128,2048]{1,0:T(8,128)(2,1)S(1)}, bf16[128,2048]{1,0:T(8,128)(2,1)S(1)}, u32[]{:S(2)}, u32[]{:S(2)}) collective-permute-start(bf16[128,2048]{1,0:T(8,128)(2,1)S(1)} %collective-permute-done.16.refs_3_), channel_id=1, source_target_pairs={{0,8},{4,12},{8,16},{12,20},{16,24},{20,28},{24,32},{28,36},{32,40... | collective-permute-start | bytes 1572872 | tf_op jit(solution)/shard_map/ppermute | solution.py:52
  52.9 12.6 %collective-permute-start.19 = (bf16[128,2048]{1,0:T(8,128)(2,1)S(1)}, bf16[128,2048]{1,0:T(8,128)(2,1)S(1)}, u32[]{:S(2)}, u32[]{:S(2)}) collective-permute-start(bf16[128,2048]{1,0:T(8,128)(2,1)S(1)} %collective-permute-done.17.refs_4_), channel_id=1, source_target_pairs={{0,56},{4,60},{8,0},{12,4},{16,8},{20,12},{24,16},{28,20},{32,24},... | collective-permute-start | bytes 1572872 | tf_op jit(solution)/shard_map/ppermute | solution.py:52
  61.2 10.4 %collective-permute-start.12 = (bf16[128,2176]{1,0:T(8,128)(2,1)}, bf16[128,2176]{1,0:T(8,128)(2,1)S(1)}, u32[]{:S(2)}, u32[]{:S(2)}) collective-permute-start(bf16[128,2176]{1,0:T(8,128)(2,1)} %slice.56), channel_id=1, source_target_pairs={{0,64},{4,68},{8,72},{12,76},{16,80},{20,84},{24,88},{28,92},{32,9... | collective-permute-start | bytes 1671176 | tf_op jit(solution)/shard_map/ppermute | solution.py:52
  65.5 20.7 %collective-permute-start.20 = (bf16[64,2048]{1,0:T(8,128)(2,1)}, bf16[64,2048]{1,0:T(8,128)(2,1)}, u32[]{:S(2)}, u32[]{:S(2)}) collective-permute-start(bf16[64,2048]{1,0:T(8,128)(2,1)} %slice.58), channel_id=1, source_target_pairs={{0,8},{4,12},{8,16},{12,20},{16,24},{20,28},{24,32},{28,36},{32,40... | collective-permute-start | bytes 786440 | tf_op jit(solution)/shard_map/ppermute | solution.py:52
  66.3 19.9 %collective-permute-start.21 = (bf16[64,2048]{1,0:T(8,128)(2,1)}, bf16[64,2048]{1,0:T(8,128)(2,1)}, u32[]{:S(2)}, u32[]{:S(2)}) collective-permute-start(bf16[64,2048]{1,0:T(8,128)(2,1)} %slice.59), channel_id=1, source_target_pairs={{0,56},{4,60},{8,0},{12,4},{16,8},{20,12},{24,16},{28,20},{32,24},... | collective-permute-start | bytes 786440 | tf_op jit(solution)/shard_map/ppermute | solution.py:52
  79.5 11.6 %collective-permute-start.23 = (bf16[256,2176]{1,0:T(8,128)(2,1)}, bf16[256,2176]{1,0:T(8,128)(2,1)S(1)}, u32[]{:S(2)}, u32[]{:S(2)}) collective-permute-start(bf16[256,2176]{1,0:T(8,128)(2,1)} %get-tuple-element.30), channel_id=1, source_target_pairs={{0,4},{4,0},{8,12},{12,8},{16,20},{20,16},{24,28},{28,24},{32,36},... | collective-permute-start | bytes 3342344 | tf_op jit(solution)/shard_map/ppermute | solution.py:56
  91.0 10.4 %collective-permute-start.22 = (bf16[256,2048]{1,0:T(8,128)(2,1)}, bf16[256,2048]{1,0:T(8,128)(2,1)S(1)}, u32[]{:S(2)}, u32[]{:S(2)}) collective-permute-start(bf16[256,2048]{1,0:T(8,128)(2,1)} %get-tuple-element.28), channel_id=1, source_target_pairs={{0,4},{4,0},{8,12},{12,8},{16,20},{20,16},{24,28},{28,24},{32,36},... | collective-permute-start | bytes 3145736 | tf_op jit(solution)/shard_map/ppermute | solution.py:56
  117.2 28.5 %collective-permute-start.24 = (bf16[256,2304]{1,0:T(8,128)(2,1)}, bf16[256,2304]{1,0:T(8,128)(2,1)S(1)}, u32[]{:S(2)}, u32[]{:S(2)}) collective-permute-start(bf16[256,2304]{1,0:T(8,128)(2,1)} %get-tuple-element.40), channel_id=1, source_target_pairs={{0,1},{1,2},{2,3},{3,0},{4,5},{5,6},{6,7},{7,4},{8,9},{9,10},{10,1... | collective-permute-start | bytes 3538952 | tf_op jit(solution)/shard_map/ppermute | solution.py:60
  118.4 35.7 %collective-permute-start.28 = (bf16[256,2304]{1,0:T(8,128)(2,1)}, bf16[256,2304]{1,0:T(8,128)(2,1)}, u32[]{:S(2)}, u32[]{:S(2)}) collective-permute-start(bf16[256,2304]{1,0:T(8,128)(2,1)} %get-tuple-element.43), channel_id=1, source_target_pairs={{0,3},{1,0},{2,1},{3,2},{4,7},{5,4},{6,5},{7,6},{8,11},{9,8},{10,9... | collective-permute-start | bytes 3538952 | tf_op jit(solution)/shard_map/ppermute | solution.py:60
  130.4 63.8 %all-to-all-start = ((bf16[64,8,2176]{2,1,0:T(8,128)(2,1)}), bf16[64,8,2176]{2,1,0:T(8,128)(2,1)S(1)}, u32[]{:S(2)}, u32[]{:S(2)}) async-start(bf16[64,8,2176]{2,1,0:T(8,128)(2,1)} %slots.1), calls=%async_computation | async-start | bytes 4456448 | tf_op jit(solution)/shard_map/all_to_all | solution.py:545
  140.5 30.3 %collective-permute-start.25 = (bf16[256,2304]{1,0:T(8,128)(2,1)}, bf16[256,2304]{1,0:T(8,128)(2,1)}, u32[]{:S(2)}, u32[]{:S(2)}) collective-permute-start(bf16[256,2304]{1,0:T(8,128)(2,1)} %get-tuple-element.41), channel_id=1, source_target_pairs={{0,3},{1,0},{2,1},{3,2},{4,7},{5,4},{6,5},{7,6},{8,11},{9,8},{10,9... | collective-permute-start | bytes 3538952 | tf_op jit(solution)/shard_map/ppermute | solution.py:60
  141.8 31.6 %collective-permute-start.26 = (bf16[256,2304]{1,0:T(8,128)(2,1)}, bf16[256,2304]{1,0:T(8,128)(2,1)}, u32[]{:S(2)}, u32[]{:S(2)}) collective-permute-start(bf16[256,2304]{1,0:T(8,128)(2,1)} %get-tuple-element.42), channel_id=1, source_target_pairs={{0,1},{1,2},{2,3},{3,0},{4,5},{5,6},{6,7},{7,4},{8,9},{9,10},{10,1... | collective-permute-start | bytes 3538952 | tf_op jit(solution)/shard_map/ppermute | solution.py:60
  157.2 31.0 %collective-permute-start.27 = (bf16[256,1536]{1,0:T(8,128)(2,1)}, bf16[256,1536]{1,0:T(8,128)(2,1)}, u32[]{:S(2)}, u32[]{:S(2)}) collective-permute-start(bf16[256,1536]{1,0:T(8,128)(2,1)} %get-tuple-element.60), channel_id=1, source_target_pairs={{0,1},{1,2},{2,3},{3,0},{4,5},{5,6},{6,7},{7,4},{8,9},{9,10},{10,1... | collective-permute-start | bytes 2359304 | tf_op jit(solution)/shard_map/ppermute | solution.py:60
  157.3 30.9 %collective-permute-start.29 = (bf16[256,1536]{1,0:T(8,128)(2,1)S(1)}, bf16[256,1536]{1,0:T(8,128)(2,1)}, u32[]{:S(2)}, u32[]{:S(2)}) collective-permute-start(bf16[256,1536]{1,0:T(8,128)(2,1)S(1)} %get-tuple-element.59), channel_id=1, source_target_pairs={{0,3},{1,0},{2,1},{3,2},{4,7},{5,4},{6,5},{7,6},{8,11},{9,8},{10,9... | collective-permute-start | bytes 2359304 | tf_op jit(solution)/shard_map/ppermute | solution.py:60
  162.7 34.0 %collective-permute-start.30 = (bf16[256,768]{1,0:T(8,128)(2,1)}, bf16[256,768]{1,0:T(8,128)(2,1)}, u32[]{:S(2)}, u32[]{:S(2)}) collective-permute-start(bf16[256,768]{1,0:T(8,128)(2,1)} %get-tuple-element.58), channel_id=1, source_target_pairs={{0,1},{1,2},{2,3},{3,0},{4,5},{5,6},{6,7},{7,4},{8,9},{9,10},{10,1... | collective-permute-start | bytes 1179656 | tf_op jit(solution)/shard_map/ppermute | solution.py:60
  170.7 25.9 %collective-permute-start.31 = (bf16[256,768]{1,0:T(8,128)(2,1)S(1)}, bf16[256,768]{1,0:T(8,128)(2,1)}, u32[]{:S(2)}, u32[]{:S(2)}) collective-permute-start(bf16[256,768]{1,0:T(8,128)(2,1)S(1)} %get-tuple-element.57), channel_id=1, source_target_pairs={{0,3},{1,0},{2,1},{3,2},{4,7},{5,4},{6,5},{7,6},{8,11},{9,8},{10,9... | collective-permute-start | bytes 1179656 | tf_op jit(solution)/shard_map/ppermute | solution.py:60
  (34 other events, 296.4 us)

commit v5 on v4

--- a/solution.py
+++ b/solution.py
@@ -89,6 +89,25 @@
 
 def iota(shape, dim):
     return lax.broadcasted_iota(i32, shape, dim)
+
+
+def widen_kernel(tokens_ref, ids_ref, weights_ref, out_ref, scr):
+    scr[...] = jnp.zeros_like(scr)
+    scr[:TOPK, :TOK] = ids_ref[...].astype(f32)
+    scr[TOPK : 2 * TOPK, :TOK] = weights_ref[...].astype(f32)
+    out_ref[:, :D] = tokens_ref[...]
+    out_ref[:, D:] = scr[...].T[:TOK].astype(bf16)
+
+
+def widen(tokens, ids, weights):
+    return pl.pallas_call(
+        widen_kernel,
+        out_shape=jax.ShapeDtypeStruct((TOK, DA), bf16),
+        in_specs=[VM] * 3,
+        out_specs=VM,
+        scratch_shapes=[pltpu.VMEM((META, META), f32)],
+        name="widen",
+    )(tokens, ids, weights)
 
 
 def pick_x_kernel(me_ref, *refs):
@@ -492,10 +511,7 @@
 
 def body(tokens, cotangent, expert_ids, route_weights, w_gate, w_up, w_down):
     pos = jnp.stack([lax.axis_index("ep"), lax.axis_index("dp")]).astype(i32)
-    meta = jnp.concatenate(
-        [expert_ids.astype(bf16), route_weights, jnp.zeros((TOK, META - 2 * TOPK), bf16)], axis=1
-    )
-    xa = jnp.concatenate([tokens, meta], axis=1)
+    xa = widen(tokens, expert_ids.T, route_weights.T)
 
     c1 = shift(cotangent, dy=1)
     c2 = shift(cotangent, dy=-1)

time: 200 us -> 199 us (level)
    unnamed x54 -> x51, local copies, waits for them, and re-layouts: 8.25 us -> 7.46 us
where the time goes in v5:
time: 199 us; the launch traced here: 198 us
  Pallas kernels  66.6 us (33%)
  starting transfers between devices  58.2 us (29%)
  waiting for transfers between devices  53.9 us (27%)
  local copies, waits for them, and re-layouts  11 us (6%)
  other arithmetic  6.6 us (3%)
    ppermute x22, starting transfers between devices, shift(): return lax.ppermute(arr, 'ep', pairs)  31.9 us
    ppermute x8, waiting for transfers between devices, shift_dp(): return lax.ppermute(arr, 'dp', [(i, (i + by) % NDP) for i in range(NDP)])  26.7 us
    ppermute x22, waiting for transfers between devices, shift(): return lax.ppermute(arr, 'ep', pairs)  26.1 us
    pallas_call x1, Pallas kernels, mid(): pl.pallas_call(mid_kernel, out_shape=(*[jax.ShapeDtypeStruct(size, bf16)]...  14.7 us
    pallas_call x1, Pallas kernels, slots(): pl.pallas_call(slots_kernel, grid=(D // WIDE,), out_shape=jax.ShapeDtypeS...  10.5 us
    all_to_all x1, starting transfers between devices, body(): got = lax.all_to_all(out, 'ep', split_axis=0, concat_axis=0, tiled=True)  9.94 us
    ppermute x8, starting transfers between devices, shift_dp(): return lax.ppermute(arr, 'dp', [(i, (i + by) % NDP) for i in range(NDP)])  9.58 us
    pallas_call x1, Pallas kernels, front(): pl.pallas_call(front_kernel, grid=(NFB,), out_shape=(jax.ShapeDtypeStruct...  9.33 us
  transfers between devices with their start and end apart: 33, of which 13 were waited for; matrix products, arithmetic and copies ran while one was open for 6% of the time, Pallas kernels for 24%

profile of v5, /device:TPU:1, one launch (start us, length us, event | category | flops | bytes accessed | tf_op | source)
XLA Modules:
  0.0 198.5 jit_solution(16616767669452625799)
XLA Ops:
  4.8 3.9 %collective-permute-start.1 = (bf16[32,2176]{1,0:T(8,128)(2,1)}, bf16[32,2176]{1,0:T(8,128)(2,1)S(1)}, u32[]{:S(2)}, u32[]{:S(2)}) collective-permute-start(bf16[32,2176]{1,0:T(8,128)(2,1)} %widen.1.refs_0_), channel_id=1, source_target_pairs={{0,56},{4,60},{8,0},{12,4},{16,8},{20,12},{24,16},{28,20},{32,24},... | collective-permute-start | bytes 417800 | tf_op jit(solution)/shard_map/ppermute | solution.py:52
  8.7 3.6 %collective-permute-done.refs_1_ = bf16[32,2176]{1,0:T(8,128)(2,1)S(1)} collective-permute-done((bf16[32,2176]{1,0:T(8,128)(2,1)}, bf16[32,2176]{1,0:T(8,128)(2,1)S(1)}, u32[]{:S(2)}, u32[]{:S(2)}) %collective-permute-start) | collective-permute-done | bytes 139296 | tf_op jit(solution)/shard_map/ppermute | solution.py:52
  20.1 2.7 %collective-permute-start.8 = (bf16[32,2048]{1,0:T(8,128)(2,1)}, bf16[32,2048]{1,0:T(8,128)(2,1)S(1)}, u32[]{:S(2)}, u32[]{:S(2)}) collective-permute-start(bf16[32,2048]{1,0:T(8,128)(2,1)} %refs_0_.1), channel_id=1, source_target_pairs={{0,192},{4,196},{8,200},{12,204},{16,208},{20,212},{24,216},{28,22... | collective-permute-start | bytes 393224 | tf_op jit(solution)/shard_map/ppermute | solution.py:52
  25.1 2.8 %collective-permute-done.9.refs_3_ = bf16[32,2048]{1,0:T(8,128)(2,1)S(1)} collective-permute-done((bf16[32,2048]{1,0:T(8,128)(2,1)S(1)}, bf16[32,2048]{1,0:T(8,128)(2,1)S(1)}, u32[]{:S(2)}, u32[]{:S(2)}) %collective-permute-start.9) | collective-permute-done | bytes 131104 | tf_op jit(solution)/shard_map/ppermute | solution.py:52
  31.1 2.7 %collective-permute-start.15 = (bf16[128,2048]{1,0:T(8,128)(2,1)}, bf16[128,2048]{1,0:T(8,128)(2,1)S(1)}, u32[]{:S(2)}, u32[]{:S(2)}) collective-permute-start(bf16[128,2048]{1,0:T(8,128)(2,1)} %join.2.refs_8_.refs_0_), channel_id=1, source_target_pairs={{0,56},{4,60},{8,0},{12,4},{16,8},{20,12},{24,16},{28,20},{32,24},... | collective-permute-start | bytes 1572872 | tf_op jit(solution)/shard_map/ppermute | solution.py:52
  36.9 2.7 %collective-permute-start.11 = (bf16[256,2176]{1,0:T(8,128)(2,1)}, bf16[256,2176]{1,0:T(8,128)(2,1)S(1)}, u32[]{:S(2)}, u32[]{:S(2)}) collective-permute-start(bf16[256,2176]{1,0:T(8,128)(2,1)} %join.3.refs_0_), channel_id=1, source_target_pairs={{0,192},{4,196},{8,200},{12,204},{16,208},{20,212},{24,216},{28,22... | collective-permute-start | bytes 3342344 | tf_op jit(solution)/shard_map/ppermute | solution.py:52
  44.3 7.8 %collective-permute-done.16.refs_3_ = bf16[128,2048]{1,0:T(8,128)(2,1)S(1)} collective-permute-done((bf16[128,2048]{1,0:T(8,128)(2,1)S(1)}, bf16[128,2048]{1,0:T(8,128)(2,1)S(1)}, u32[]{:S(2)}, u32[]{:S(2)}) %collective-permute-start.16) | collective-permute-done | bytes 524320 | tf_op jit(solution)/shard_map/ppermute | solution.py:52
  54.8 4.7 %collective-permute-done.10.refs_1_ = bf16[256,2176]{1,0:T(8,128)(2,1)S(1)} collective-permute-done((bf16[256,2176]{1,0:T(8,128)(2,1)}, bf16[256,2176]{1,0:T(8,128)(2,1)S(1)}, u32[]{:S(2)}, u32[]{:S(2)}) %collective-permute-start.10) | collective-permute-done | bytes 1114144 | tf_op jit(solution)/shard_map/ppermute | solution.py:52
  61.3 2.7 %collective-permute-start.13 = (bf16[128,2176]{1,0:T(8,128)(2,1)}, bf16[128,2176]{1,0:T(8,128)(2,1)S(1)}, u32[]{:S(2)}, u32[]{:S(2)}) collective-permute-start(bf16[128,2176]{1,0:T(8,128)(2,1)} %slice.57), channel_id=1, source_target_pairs={{0,192},{4,196},{8,200},{12,204},{16,208},{20,212},{24,216},{28,22... | collective-permute-start | bytes 1671176 | tf_op jit(solution)/shard_map/ppermute | solution.py:52
  65.5 2.7 %collective-permute-start.21 = (bf16[64,2048]{1,0:T(8,128)(2,1)}, bf16[64,2048]{1,0:T(8,128)(2,1)}, u32[]{:S(2)}, u32[]{:S(2)}) collective-permute-start(bf16[64,2048]{1,0:T(8,128)(2,1)} %slice.59), channel_id=1, source_target_pairs={{0,56},{4,60},{8,0},{12,4},{16,8},{20,12},{24,16},{28,20},{32,24},... | collective-permute-start | bytes 786440 | tf_op jit(solution)/shard_map/ppermute | solution.py:52
  72.4 6.3 %pick_x.1 = (bf16[256,2176]{1,0:T(8,128)(2,1)}, bf16[256,2176]{1,0:T(8,128)(2,1)}, bf16[4,256,128]{2,1,0:T(8,128)(2,1)}) custom-call(s32[2]{0:T(128)} %pad_add_fusion.me_ref.pos_ref, bf16[256,2176]{1,0:T(8,128)(2,1)} %join.3.refs_0_, bf16[256,2176]{1,0:T(8,128)(2,1)} %copy-done.1, bf16[256,2176]{1,0:T(8,128)(2,1)} %copy-done.2, bf16[128,2176]{1,0:T(8,128)(2,1)} %copy-done.4, ...), custom_call_target="tpu_custom_call" | custom-call | tf_op jit(solution)/shard_map/pick_x/pallas_call | solution.py:167
  78.7 6.7 %collective-permute-start.23 = (bf16[256,2176]{1,0:T(8,128)(2,1)}, bf16[256,2176]{1,0:T(8,128)(2,1)S(1)}, u32[]{:S(2)}, u32[]{:S(2)}) collective-permute-start(bf16[256,2176]{1,0:T(8,128)(2,1)} %get-tuple-element.30), channel_id=1, source_target_pairs={{0,4},{4,0},{8,12},{12,8},{16,20},{20,16},{24,28},{28,24},{32,36},... | collective-permute-start | bytes 3342344 | tf_op jit(solution)/shard_map/ppermute | solution.py:56
  85.4 4.8 %pick_cot.1 = (bf16[256,2048]{1,0:T(8,128)(2,1)}, bf16[256,2048]{1,0:T(8,128)(2,1)}) custom-call(bf16[4,256,128]{2,1,0:T(8,128)(2,1)} %get-tuple-element.26.code_ref.refs_9_, bf16[128,2048]{1,0:T(8,128)(2,1)} %join.2.refs_8_.refs_0_, bf16[128,2048]{1,0:T(8,128)(2,1)} %copy-done.20, bf16[128,2048]{1,0:T(8,128)(2,1)} %copy-done.21, ...), custom_call_target="tpu_custom_call" | custom-call | flops 5000000000 | tf_op jit(solution)/shard_map/pick_cot/pallas_call | solution.py:215
  91.3 9.3 %front.1 = (bf16[512,768]{1,0:T(8,128)(2,1)}, bf16[768,512]{1,0:T(8,128)(2,1)}, f32[512,768]{1,0:T(8,128)}, f32[512,768]{1,0:T(8,128)}, f32[512,128]{1,0:T(8,128)}, /*index=5*/bf16[2048,512]{1,0:T(8,128)(2,1)}) custom-call(s32[2]{0:T(128)} %pad_add_fusion.me_ref.pos_ref, bf16[256,2176]{1,0:T(8,128)(2,1)} %get-tuple-element.29.own_ref, ...), custom_call_target="tpu_custom_call" | custom-call | flops 5000000000 | tf_op jit(solution)/shard_map/front/pallas_call | solution.py:263
  101.6 14.7 %mid.1 = (bf16[256,2304]{1,0:T(8,128)(2,1)}, bf16[256,2304]{1,0:T(8,128)(2,1)}, bf16[256,2304]{1,0:T(8,128)(2,1)}, bf16[256,2304]{1,0:T(8,128)(2,1)}, bf16[2,512...) custom-call(s32[2]{0:T(128)} %pad_add_fusion.me_ref.pos_ref, ...), custom_call_target="tpu_custom_call" | custom-call | tf_op jit(solution)/shard_map/mid/pallas_call | solution.py:345
  119.1 10.5 %slots.1 = bf16[64,8,2176]{2,1,0:T(8,128)(2,1)} custom-call(s32[2]{0:T(128)} %pad_add_fusion.me_ref.pos_ref, bf16[2,512,768]{2,1,0:T(8,128)(2,1)} %get-tuple-element.37.g_ref, f32[512,128]{1,0:T(8,128)} %get-tuple-element.38.route_ref, bf16[2048,768]{1,0:T(8,128)(2,1)} %bitcast.16, bf16[2048,768]{1,0:T(8,128)(2,1)} %bitcast.18), custom_call_target="tpu_custom_call" | custom-call | tf_op jit(solution)/shard_map/slots/pallas_call | solution.py:497
  129.6 9.9 %all-to-all-start = ((bf16[64,8,2176]{2,1,0:T(8,128)(2,1)}), bf16[64,8,2176]{2,1,0:T(8,128)(2,1)S(1)}, u32[]{:S(2)}, u32[]{:S(2)}) async-start(bf16[64,8,2176]{2,1,0:T(8,128)(2,1)} %slots.1), calls=%async_computation | async-start | bytes 4456448 | tf_op jit(solution)/shard_map/all_to_all | solution.py:561
  141.2 3.6 %collective-permute-done.24._ = bf16[256,2304]{1,0:T(8,128)(2,1)S(1)} collective-permute-done((bf16[256,2304]{1,0:T(8,128)(2,1)}, bf16[256,2304]{1,0:T(8,128)(2,1)S(1)}, u32[]{:S(2)}, u32[]{:S(2)}) %collective-permute-start.24) | collective-permute-done | bytes 1179680 | tf_op jit(solution)/shard_map/ppermute | solution.py:60
  145.8 7.4 %plain.1.own_ref = bf16[1024,2304]{1,0:T(8,128)(2,1)} custom-call(s32[2]{0:T(128)} %pad_add_fusion.me_ref.pos_ref, bf16[2048,512]{1,0:T(8,128)(2,1)} %get-tuple-element.36.x_t_ref.x_ref, bf16[512,2048]{1,0:T(8,128)(2,1)} %get-tuple-element.39.c_ref, bf16[2,512,768]{2,1,0:T(8,128)(2,1)} %get-tuple-element.37.g_ref, ...), custom_call_target="tpu_custom_call" | custom-call | tf_op jit(solution)/shard_map/plain/pallas_call | solution.py:381
  153.2 3.1 %add_convert_fusion = (bf16[256,1536]{1,0:T(8,128)(2,1)S(1)}, bf16[256,1536]{1,0:T(8,128)(2,1)}) fusion(bf16[256,2304]{1,0:T(8,128)(2,1)} %collective-permute-done.28, bf16[1024,2304]{1,0:T(8,128)(2,1)} %plain.1.own_ref, bf16[256,2304]{1,0:T(8,128)(2,1)} %copy-done), kind=kLoop, calls=%fused_computation.2 | loop fusion | flops 3145728 | bytes 4718592 | tf_op jit(solution)/shard_map/convert_element_type | solution.py:566
  161.8 8.1 %collective-permute-done.25.r2a = bf16[256,2304]{1,0:T(8,128)(2,1)} collective-permute-done((bf16[256,2304]{1,0:T(8,128)(2,1)}, bf16[256,2304]{1,0:T(8,128)(2,1)}, u32[]{:S(2)}, u32[]{:S(2)}) %collective-permute-start.25) | collective-permute-done | bytes 1179680 | tf_op jit(solution)/shard_map/ppermute | solution.py:60
  169.9 2.7 %collective-permute-start.31 = (bf16[256,768]{1,0:T(8,128)(2,1)S(1)}, bf16[256,768]{1,0:T(8,128)(2,1)}, u32[]{:S(2)}, u32[]{:S(2)}) collective-permute-start(bf16[256,768]{1,0:T(8,128)(2,1)S(1)} %get-tuple-element.52), channel_id=1, source_target_pairs={{0,3},{1,0},{2,1},{3,2},{4,7},{5,4},{6,5},{7,6},{8,11},{9,8},{10,9... | collective-permute-start | bytes 1179656 | tf_op jit(solution)/shard_map/ppermute | solution.py:60
  172.6 14.9 %collective-permute-done.27.r3a = bf16[256,1536]{1,0:T(8,128)(2,1)} collective-permute-done((bf16[256,1536]{1,0:T(8,128)(2,1)}, bf16[256,1536]{1,0:T(8,128)(2,1)}, u32[]{:S(2)}, u32[]{:S(2)}) %collective-permute-start.27) | collective-permute-done | bytes 786464 | tf_op jit(solution)/shard_map/ppermute | solution.py:60
  187.4 5.0 %chunk.1 = (bf16[1,512,768]{2,1,0:T(8,128)(2,1)}, bf16[1,512,768]{2,1,0:T(8,128)(2,1)}, f32[512,768]{1,0:T(8,128)}) custom-call(bf16[1024,2304]{1,0:T(8,128)(2,1)} %plain.1.own_ref, bf16[256,2304]{1,0:T(8,128)(2,1)} %collective-permute-done.25.r2a, bf16[256,2304]{1,0:T(8,128)(2,1)} %collective-permute-done.26.r2b, ...), custom_call_target="tpu_custom_call" | custom-call | flops 30000001024 | tf_op jit(solution)/shard_map/chunk/pallas_call | solution.py:422
  (121 shorter events, 54.3 us)
Async XLA Ops:
  17.4 10.4 %collective-permute-start.5 = (bf16[32,2176]{1,0:T(8,128)(2,1)S(1)}, bf16[32,2176]{1,0:T(8,128)(2,1)S(1)}, u32[]{:S(2)}, u32[]{:S(2)}) collective-permute-start(bf16[32,2176]{1,0:T(8,128)(2,1)S(1)} %collective-permute-done.3.refs_4_), channel_id=1, source_target_pairs={{0,56},{4,60},{8,0},{12,4},{16,8},{20,12},{24,16},{28,20},{32,24},... | collective-permute-start | bytes 417800 | tf_op jit(solution)/shard_map/ppermute | solution.py:52
  22.9 10.9 %collective-permute-start.6 = (bf16[32,2176]{1,0:T(8,128)(2,1)S(1)}, bf16[32,2176]{1,0:T(8,128)(2,1)S(1)}, u32[]{:S(2)}, u32[]{:S(2)}) collective-permute-start(bf16[32,2176]{1,0:T(8,128)(2,1)S(1)} %collective-permute-done.4.refs_4_.refs_5_), channel_id=1, source_target_pairs={{0,8},{4,12},{8,16},{12,20},{16,24},{20,28},{24,32},{28,36},{32,40... | collective-permute-start | bytes 417800 | tf_op jit(solution)/shard_map/ppermute | solution.py:52
  31.1 10.5 %collective-permute-start.14 = (bf16[128,2048]{1,0:T(8,128)(2,1)}, bf16[128,2048]{1,0:T(8,128)(2,1)S(1)}, u32[]{:S(2)}, u32[]{:S(2)}) collective-permute-start(bf16[128,2048]{1,0:T(8,128)(2,1)} %join.2.refs_8_.refs_0_), channel_id=1, source_target_pairs={{0,8},{4,12},{8,16},{12,20},{16,24},{20,28},{24,32},{28,36},{32,40... | collective-permute-start | bytes 1572872 | tf_op jit(solution)/shard_map/ppermute | solution.py:52
  31.1 10.5 %collective-permute-start.15 = (bf16[128,2048]{1,0:T(8,128)(2,1)}, bf16[128,2048]{1,0:T(8,128)(2,1)S(1)}, u32[]{:S(2)}, u32[]{:S(2)}) collective-permute-start(bf16[128,2048]{1,0:T(8,128)(2,1)} %join.2.refs_8_.refs_0_), channel_id=1, source_target_pairs={{0,56},{4,60},{8,0},{12,4},{16,8},{20,12},{24,16},{28,20},{32,24},... | collective-permute-start | bytes 1572872 | tf_op jit(solution)/shard_map/ppermute | solution.py:52
  36.9 22.5 %collective-permute-start.10 = (bf16[256,2176]{1,0:T(8,128)(2,1)}, bf16[256,2176]{1,0:T(8,128)(2,1)S(1)}, u32[]{:S(2)}, u32[]{:S(2)}) collective-permute-start(bf16[256,2176]{1,0:T(8,128)(2,1)} %join.3.refs_0_), channel_id=1, source_target_pairs={{0,64},{4,68},{8,72},{12,76},{16,80},{20,84},{24,88},{28,92},{32,9... | collective-permute-start | bytes 3342344 | tf_op jit(solution)/shard_map/ppermute | solution.py:52
  36.9 23.5 %collective-permute-start.11 = (bf16[256,2176]{1,0:T(8,128)(2,1)}, bf16[256,2176]{1,0:T(8,128)(2,1)S(1)}, u32[]{:S(2)}, u32[]{:S(2)}) collective-permute-start(bf16[256,2176]{1,0:T(8,128)(2,1)} %join.3.refs_0_), channel_id=1, source_target_pairs={{0,192},{4,196},{8,200},{12,204},{16,208},{20,212},{24,216},{28,22... | collective-permute-start | bytes 3342344 | tf_op jit(solution)/shard_map/ppermute | solution.py:52
  41.6 10.5 %collective-permute-start.16 = (bf16[128,2048]{1,0:T(8,128)(2,1)S(1)}, bf16[128,2048]{1,0:T(8,128)(2,1)S(1)}, u32[]{:S(2)}, u32[]{:S(2)}) collective-permute-start(bf16[128,2048]{1,0:T(8,128)(2,1)S(1)} %collective-permute-done.14.refs_1_), channel_id=1, source_target_pairs={{0,8},{4,12},{8,16},{12,20},{16,24},{20,28},{24,32},{28,36},{32,40... | collective-permute-start | bytes 1572872 | tf_op jit(solution)/shard_map/ppermute | solution.py:52
  41.6 10.5 %collective-permute-start.17 = (bf16[128,2048]{1,0:T(8,128)(2,1)S(1)}, bf16[128,2048]{1,0:T(8,128)(2,1)S(1)}, u32[]{:S(2)}, u32[]{:S(2)}) collective-permute-start(bf16[128,2048]{1,0:T(8,128)(2,1)S(1)} %collective-permute-done.15.refs_2_), channel_id=1, source_target_pairs={{0,56},{4,60},{8,0},{12,4},{16,8},{20,12},{24,16},{28,20},{32,24},... | collective-permute-start | bytes 1572872 | tf_op jit(solution)/shard_map/ppermute | solution.py:52
  52.1 11.9 %collective-permute-start.18 = (bf16[128,2048]{1,0:T(8,128)(2,1)S(1)}, bf16[128,2048]{1,0:T(8,128)(2,1)S(1)}, u32[]{:S(2)}, u32[]{:S(2)}) collective-permute-start(bf16[128,2048]{1,0:T(8,128)(2,1)S(1)} %collective-permute-done.16.refs_3_), channel_id=1, source_target_pairs={{0,8},{4,12},{8,16},{12,20},{16,24},{20,28},{24,32},{28,36},{32,40... | collective-permute-start | bytes 1572872 | tf_op jit(solution)/shard_map/ppermute | solution.py:52
  52.1 12.6 %collective-permute-start.19 = (bf16[128,2048]{1,0:T(8,128)(2,1)S(1)}, bf16[128,2048]{1,0:T(8,128)(2,1)S(1)}, u32[]{:S(2)}, u32[]{:S(2)}) collective-permute-start(bf16[128,2048]{1,0:T(8,128)(2,1)S(1)} %collective-permute-done.17.refs_4_), channel_id=1, source_target_pairs={{0,56},{4,60},{8,0},{12,4},{16,8},{20,12},{24,16},{28,20},{32,24},... | collective-permute-start | bytes 1572872 | tf_op jit(solution)/shard_map/ppermute | solution.py:52
  60.4 10.4 %collective-permute-start.12 = (bf16[128,2176]{1,0:T(8,128)(2,1)}, bf16[128,2176]{1,0:T(8,128)(2,1)S(1)}, u32[]{:S(2)}, u32[]{:S(2)}) collective-permute-start(bf16[128,2176]{1,0:T(8,128)(2,1)} %slice.56), channel_id=1, source_target_pairs={{0,64},{4,68},{8,72},{12,76},{16,80},{20,84},{24,88},{28,92},{32,9... | collective-permute-start | bytes 1671176 | tf_op jit(solution)/shard_map/ppermute | solution.py:52
  64.7 20.7 %collective-permute-start.20 = (bf16[64,2048]{1,0:T(8,128)(2,1)}, bf16[64,2048]{1,0:T(8,128)(2,1)}, u32[]{:S(2)}, u32[]{:S(2)}) collective-permute-start(bf16[64,2048]{1,0:T(8,128)(2,1)} %slice.58), channel_id=1, source_target_pairs={{0,8},{4,12},{8,16},{12,20},{16,24},{20,28},{24,32},{28,36},{32,40... | collective-permute-start | bytes 786440 | tf_op jit(solution)/shard_map/ppermute | solution.py:52
  65.5 19.9 %collective-permute-start.21 = (bf16[64,2048]{1,0:T(8,128)(2,1)}, bf16[64,2048]{1,0:T(8,128)(2,1)}, u32[]{:S(2)}, u32[]{:S(2)}) collective-permute-start(bf16[64,2048]{1,0:T(8,128)(2,1)} %slice.59), channel_id=1, source_target_pairs={{0,56},{4,60},{8,0},{12,4},{16,8},{20,12},{24,16},{28,20},{32,24},... | collective-permute-start | bytes 786440 | tf_op jit(solution)/shard_map/ppermute | solution.py:52
  78.7 11.6 %collective-permute-start.23 = (bf16[256,2176]{1,0:T(8,128)(2,1)}, bf16[256,2176]{1,0:T(8,128)(2,1)S(1)}, u32[]{:S(2)}, u32[]{:S(2)}) collective-permute-start(bf16[256,2176]{1,0:T(8,128)(2,1)} %get-tuple-element.30), channel_id=1, source_target_pairs={{0,4},{4,0},{8,12},{12,8},{16,20},{20,16},{24,28},{28,24},{32,36},... | collective-permute-start | bytes 3342344 | tf_op jit(solution)/shard_map/ppermute | solution.py:56
  90.3 10.4 %collective-permute-start.22 = (bf16[256,2048]{1,0:T(8,128)(2,1)}, bf16[256,2048]{1,0:T(8,128)(2,1)S(1)}, u32[]{:S(2)}, u32[]{:S(2)}) collective-permute-start(bf16[256,2048]{1,0:T(8,128)(2,1)} %get-tuple-element.28), channel_id=1, source_target_pairs={{0,4},{4,0},{8,12},{12,8},{16,20},{20,16},{24,28},{28,24},{32,36},... | collective-permute-start | bytes 3145736 | tf_op jit(solution)/shard_map/ppermute | solution.py:56
  116.4 28.5 %collective-permute-start.24 = (bf16[256,2304]{1,0:T(8,128)(2,1)}, bf16[256,2304]{1,0:T(8,128)(2,1)S(1)}, u32[]{:S(2)}, u32[]{:S(2)}) collective-permute-start(bf16[256,2304]{1,0:T(8,128)(2,1)} %get-tuple-element.40), channel_id=1, source_target_pairs={{0,1},{1,2},{2,3},{3,0},{4,5},{5,6},{6,7},{7,4},{8,9},{9,10},{10,1... | collective-permute-start | bytes 3538952 | tf_op jit(solution)/shard_map/ppermute | solution.py:60
  117.6 35.7 %collective-permute-start.28 = (bf16[256,2304]{1,0:T(8,128)(2,1)}, bf16[256,2304]{1,0:T(8,128)(2,1)}, u32[]{:S(2)}, u32[]{:S(2)}) collective-permute-start(bf16[256,2304]{1,0:T(8,128)(2,1)} %get-tuple-element.43), channel_id=1, source_target_pairs={{0,3},{1,0},{2,1},{3,2},{4,7},{5,4},{6,5},{7,6},{8,11},{9,8},{10,9... | collective-permute-start | bytes 3538952 | tf_op jit(solution)/shard_map/ppermute | solution.py:60
  129.6 63.8 %all-to-all-start = ((bf16[64,8,2176]{2,1,0:T(8,128)(2,1)}), bf16[64,8,2176]{2,1,0:T(8,128)(2,1)S(1)}, u32[]{:S(2)}, u32[]{:S(2)}) async-start(bf16[64,8,2176]{2,1,0:T(8,128)(2,1)} %slots.1), calls=%async_computation | async-start | bytes 4456448 | tf_op jit(solution)/shard_map/all_to_all | solution.py:561
  139.7 30.2 %collective-permute-start.25 = (bf16[256,2304]{1,0:T(8,128)(2,1)}, bf16[256,2304]{1,0:T(8,128)(2,1)}, u32[]{:S(2)}, u32[]{:S(2)}) collective-permute-start(bf16[256,2304]{1,0:T(8,128)(2,1)} %get-tuple-element.41), channel_id=1, source_target_pairs={{0,3},{1,0},{2,1},{3,2},{4,7},{5,4},{6,5},{7,6},{8,11},{9,8},{10,9... | collective-permute-start | bytes 3538952 | tf_op jit(solution)/shard_map/ppermute | solution.py:60
  141.0 31.6 %collective-permute-start.26 = (bf16[256,2304]{1,0:T(8,128)(2,1)}, bf16[256,2304]{1,0:T(8,128)(2,1)}, u32[]{:S(2)}, u32[]{:S(2)}) collective-permute-start(bf16[256,2304]{1,0:T(8,128)(2,1)} %get-tuple-element.42), channel_id=1, source_target_pairs={{0,1},{1,2},{2,3},{3,0},{4,5},{5,6},{6,7},{7,4},{8,9},{9,10},{10,1... | collective-permute-start | bytes 3538952 | tf_op jit(solution)/shard_map/ppermute | solution.py:60
  156.4 31.1 %collective-permute-start.27 = (bf16[256,1536]{1,0:T(8,128)(2,1)}, bf16[256,1536]{1,0:T(8,128)(2,1)}, u32[]{:S(2)}, u32[]{:S(2)}) collective-permute-start(bf16[256,1536]{1,0:T(8,128)(2,1)} %get-tuple-element.55), channel_id=1, source_target_pairs={{0,1},{1,2},{2,3},{3,0},{4,5},{5,6},{6,7},{7,4},{8,9},{9,10},{10,1... | collective-permute-start | bytes 2359304 | tf_op jit(solution)/shard_map/ppermute | solution.py:60
  156.5 31.0 %collective-permute-start.29 = (bf16[256,1536]{1,0:T(8,128)(2,1)S(1)}, bf16[256,1536]{1,0:T(8,128)(2,1)}, u32[]{:S(2)}, u32[]{:S(2)}) collective-permute-start(bf16[256,1536]{1,0:T(8,128)(2,1)S(1)} %get-tuple-element.54), channel_id=1, source_target_pairs={{0,3},{1,0},{2,1},{3,2},{4,7},{5,4},{6,5},{7,6},{8,11},{9,8},{10,9... | collective-permute-start | bytes 2359304 | tf_op jit(solution)/shard_map/ppermute | solution.py:60
  161.8 34.0 %collective-permute-start.30 = (bf16[256,768]{1,0:T(8,128)(2,1)}, bf16[256,768]{1,0:T(8,128)(2,1)}, u32[]{:S(2)}, u32[]{:S(2)}) collective-permute-start(bf16[256,768]{1,0:T(8,128)(2,1)} %get-tuple-element.53), channel_id=1, source_target_pairs={{0,1},{1,2},{2,3},{3,0},{4,5},{5,6},{6,7},{7,4},{8,9},{9,10},{10,1... | collective-permute-start | bytes 1179656 | tf_op jit(solution)/shard_map/ppermute | solution.py:60
  169.9 26.0 %collective-permute-start.31 = (bf16[256,768]{1,0:T(8,128)(2,1)S(1)}, bf16[256,768]{1,0:T(8,128)(2,1)}, u32[]{:S(2)}, u32[]{:S(2)}) collective-permute-start(bf16[256,768]{1,0:T(8,128)(2,1)S(1)} %get-tuple-element.52), channel_id=1, source_target_pairs={{0,3},{1,0},{2,1},{3,2},{4,7},{5,4},{6,5},{7,6},{8,11},{9,8},{10,9... | collective-permute-start | bytes 1179656 | tf_op jit(solution)/shard_map/ppermute | solution.py:60
  (33 other events, 265.2 us)
